TPU v7x, 32 devices: a whole 2x2x4 slice. The times are simulated.
32 devices in a mesh: row: 4 (over y, x), col: 8 (over z, core).
Axes of the slice: x: 2, y: 2, z: 4, core: 2. Of those that a mesh axis runs over, the one named last changes fastest.
Arguments:
- eigvecs: float32 [4096, 4096], P('row', 'col'), may hold values from -6 to 6
- house_one: float32 [4096, 128], P('row', 'col'), may hold values from -0.09375 to 0.09375
- house_two: float32 [4096, 128], P('row', 'col'), may hold values from -0.09375 to 0.09375
- tile_map: int32 [32], replicated, may hold values from 0 to 31, each once
- select: int32 [256], replicated, may hold values from 0 to 4095, as said below
- ritz_basis: bfloat16 [32768, 4096], P(('row', 'col')), may hold values from -0.09375 to 0.09375
Outputs:
- back_vectors: float32 [4096, 4096], P('row', 'col')
- mode_shapes: bfloat16 [32768, 256], P(('row', 'col'))
Inputs may be any that keep to these rules, and one draw needn't show every extreme that they name: `select`: the 256 indices are distinct and include 0 and 4095. `tile_map`: each global tile row appears once.
All inputs are finite; a program needn't handle non-finite values.
Results may differ from a plain program's by a relative error of at most 0.0049.
Values may be sent and summed in bfloat16 or wider, within the bound.
No kernel may reach another device: no remote copies, remote signals or barrier semaphores. Data moves between devices by JAX's collectives and lax.ppermute only.
A program may use at most 64 MiB of HBM per device.

v0:
```python
import jax
import jax.numpy as jnp
from jax import lax
from jax.sharding import PartitionSpec as P

TILE = 128


def precise(left, right):
    return jnp.dot(left, right, precision=lax.Precision.HIGHEST, preferred_element_type=jnp.float32)


def compact(gram):
    width = gram.shape[0]
    scales = 0.5 * jnp.diag(gram)
    strict = jnp.triu(gram, 1) / scales[:, None]
    identity = jnp.eye(width, dtype=gram.dtype)
    power = -strict
    total = identity + power
    for level in range((width - 1).bit_length() - 1):
        power = precise(power, power)
        total = precise(total, identity + power)
    return total / scales[None, :]


def expand_panel(panel, tile_map, ritz_basis):
    tile_count = tile_map.shape[0]
    tiles = panel.reshape(tile_count, TILE, panel.shape[1])
    places = jnp.arange(tile_count, dtype=jnp.int32)
    mover = (places[:, None] == tile_map[None, :]).astype(jnp.bfloat16)
    ordered = jnp.einsum("gs,sip->gip", mover, tiles, preferred_element_type=jnp.float32)
    ordered = ordered.astype(jnp.bfloat16).reshape(panel.shape[0], panel.shape[1])
    return jnp.dot(ritz_basis, ordered, preferred_element_type=jnp.float32)


def per_device(eigvecs, house_one, house_two, tile_map, select, ritz_basis):
    vec_one, vec_two = (
        lax.all_gather(house_one, "col", axis=1, tiled=True),
        lax.all_gather(house_two, "col", axis=1, tiled=True),
    )

    def apply_block(field, vectors):
        projected, gram = lax.psum((precise(vectors.T, field), precise(vectors.T, vectors)), "row")
        return field - precise(vectors, precise(compact(gram), projected))

    section = apply_block(eigvecs, vec_two)
    back_vectors = apply_block(section, vec_one)
    local_cols = eigvecs.shape[1]
    col_ids = lax.axis_index("col") * local_cols + jnp.arange(local_cols, dtype=jnp.int32)
    chooser = (col_ids[:, None] == select[None, :]).astype(jnp.float32)
    picked = precise(back_vectors, chooser)
    rows_part = lax.psum(picked.astype(jnp.bfloat16), "col")
    panel = lax.all_gather(rows_part, "row", axis=0, tiled=True)
    modes = expand_panel(panel, tile_map, ritz_basis)
    return (back_vectors, modes.astype(jnp.bfloat16))


def solution(mesh):
    return jax.shard_map(
        per_device,
        mesh=mesh,
        in_specs=(
            P("row", "col"),
            P("row", "col"),
            P("row", "col"),
            P(),
            P(),
            P(("row", "col"), None),
        ),
        out_specs=(P("row", "col"), P(("row", "col"), None)),
        check_vma=False,
    )
```

profile of v0, /device:TPU:0, one launch (start us, length us, event | category | flops | bytes accessed | tf_op | source)
XLA Modules:
  0.0 253.1 jit_solution(4916615402586915821)
XLA Ops:
  7.2 16.8 %all_gather.9 = f32[1024,128]{0,1:T(8,128)S(1)} all-gather(f32[1024,16]{0,1:T(8,128)} %param.8), channel_id=1, replica_groups=mesh['row'=4,'col'=8] {'col'}, dimensions={1}, use_global_device_ids=true | all-gather | bytes 589824 | tf_op jit(solution)/shard_map/all_gather | solution.py:39
  24.0 1.2 fusion.24
  25.2 3.6 %fusion.29 = f32[128,512]{1,0:T(8,128)} fusion(f32[1024,128]{0,1:T(8,128)S(1)} %all_gather.9, f32[1024,512]{1,0:T(8,128)} %param.6), kind=kOutput, calls=%fused_computation.58 | convolution fusion | flops 805306368 | bytes 2883584 | tf_op jit(solution)/shard_map/dot_general | solution.py:10
  28.9 1.8 copy.12
  30.7 14.7 %all_gather.10 = f32[1024,128]{0,1:T(8,128)S(1)} all-gather(f32[1024,16]{0,1:T(8,128)S(1)} %copy-done.4), channel_id=1, replica_groups=mesh['row'=4,'col'=8] {'col'}, dimensions={1}, use_global_device_ids=true | all-gather | bytes 589824 | tf_op jit(solution)/shard_map/all_gather | solution.py:38
  45.4 1.2 fusion.31
  46.7 27.0 %all-reduce.10.cloned.1.call-done = (f32[128,128]{1,0:T(8,128)}, f32[128,512]{1,0:T(8,128)}) async-done(((f32[128,128]{1,0:T(8,128)}, f32[128,512]{1,0:T(8,128)}), (f32[128,128]{1,0:T(8,128)}, f32[128,512]{1,0:T(8,128)})) %all-reduce.10.cloned.1.call-update) | async-done | bytes 327696 | tf_op jit(solution)/shard_map/psum | solution.py:43
  73.7 2.0 gather_fusion
  75.7 1.2 fusion.22
  80.5 3.5 %bitcast_subtract_fusion.1 = f32[1024,512]{0,1:T(8,128)S(1)} fusion(f32[1024,512]{0,1:T(8,128)} %copy.12, f32[128,512]{1,0:T(8,128)S(1)} %fusion.30, f32[1024,128]{0,1:T(8,128)S(1)} %all_gather.9), kind=kOutput, calls=%fused_computation.3 | convolution fusion | flops 805830656 | bytes 4980736 | tf_op jit(solution)/shard_map/dot_general | solution.py:10
  84.0 2.5 convolution_bitcast_fusion
  86.8 43.6 %all-reduce.8.cloned.1.call-done = (f32[128,128]{1,0:T(8,128)}, f32[128,512]{0,1:T(8,128)}) async-done(((f32[128,128]{1,0:T(8,128)}, f32[128,512]{0,1:T(8,128)}), (f32[128,128]{1,0:T(8,128)}, f32[128,512]{0,1:T(8,128)})) %all-reduce.8.cloned.1.call-update) | async-done | bytes 327696 | tf_op jit(solution)/shard_map/psum | solution.py:43
  130.3 2.0 gather_fusion.1
  132.3 1.2 fusion.23
  133.5 1.1 fusion.14
  137.2 1.9 bitcast_subtract_fusion
  139.1 1.3 copy-done
  140.4 2.7 %convolution_convert_fusion.1 = bf16[1024,256]{1,0:T(8,128)(2,1)} fusion(f32[1024,512]{0,1:T(8,128)S(1)} %bitcast_subtract_fusion, s32[256]{0:T(256)S(1)} %copy-done.5, s32[512]{0:T(512)S(1)} %iota_add_fusion), kind=kOutput, calls=%fused_computation.8 | convolution fusion | flops 1611005952 | bytes 2624512 | tf_op jit(solution)/shard_map/dot_general | solution.py:10
  143.2 56.2 %all-reduce.6.cloned.1.call-done = bf16[1024,256]{1,0:T(8,128)(2,1)} async-done(((bf16[1024,256]{1,0:T(8,128)(2,1)}), bf16[1024,256]{1,0:T(8,128)(2,1)}) %all-reduce.6.cloned.1.call-update) | async-done | bytes 524304 | tf_op jit(solution)/shard_map/psum | solution.py:52
  199.5 2.9 %copy.15 = f32[1024,512]{1,0:T(8,128)} copy(f32[1024,512]{0,1:T(8,128)} %copy-done) | data formatting | bytes 4194304
  202.4 33.2 %all-gather.2.cloned.1.call-done = bf16[4096,256]{1,0:T(8,128)(2,1)} async-done(((bf16[1024,256]{1,0:T(8,128)(2,1)}), bf16[4096,256]{1,0:T(8,128)(2,1)}) %all-gather.2.cloned.1.call-update) | async-done | bytes 2097168 | tf_op jit(solution)/shard_map/all_gather | solution.py:53
  235.6 3.0 %fusion.2 = bf16[32,128,256]{2,0,1:T(8,128)(2,1)S(1)} fusion(bf16[32,128,256]{2,1,0:T(8,128)(2,1)} %bitcast.66, s32[32]{0:T(128)S(1)} %copy-done.6), kind=kOutput, calls=%fused_computation.6 | convolution fusion | flops 68158464 | bytes 4194432 | tf_op jit(solution)/shard_map/gs,sip->gip/dot_general | solution.py:31
  238.6 1.2 copy.14
  239.7 5.8 %fusion.5 = bf16[1024,256]{0,1:T(8,128)(2,1)S(1)} fusion(bf16[4096,256]{1,0:T(8,128)(2,1)S(1)} %bitcast.67, bf16[1024,4096]{1,0:T(8,128)(2,1)} %param.11), kind=kOutput, calls=%fused_computation.9 | convolution fusion | flops 2147745792 | bytes 11010048 | tf_op jit(solution)/shard_map/dot_general | solution.py:33
  (49 shorter events, 7.4 us)
Async XLA Ops:
  7.2 66.5 %all-reduce.10.cloned.1.call-start = ((), (), s32[]{:S(2)}) async-start(), calls=%async_computation.3 | async-start | bytes 655360 | tf_op jit(solution)/shard_map/psum | solution.py:43
  24.0 4.9 %copy-start.1 = (f32[1024,512]{1,0:T(8,128)S(1)}, f32[1024,512]{1,0:T(8,128)}, u32[]{:S(2)}) copy-start(f32[1024,512]{1,0:T(8,128)} %param.6) | copy-start | bytes 6291460
  28.8 1.9 copy-start.4
  28.8 101.5 %all-reduce.8.cloned.1.call-start = ((), (), s32[]{:S(2)}) async-start(), calls=%async_computation.2 | async-start | bytes 655360 | tf_op jit(solution)/shard_map/psum | solution.py:43
  73.7 6.4 %copy-start.3 = (f32[128,512]{1,0:T(8,128)S(1)}, f32[128,512]{1,0:T(8,128)}, u32[]{:S(2)}) copy-start(f32[128,512]{1,0:T(8,128)} %get-tuple-element.9) | copy-start | bytes 786436
  86.5 112.9 %all-reduce.6.cloned.1.call-start = ((), (), s32[]{:S(2)}) async-start(), calls=%async_computation | async-start | bytes 1048576 | tf_op jit(solution)/shard_map/psum | solution.py:52
  130.3 6.4 %copy-start.2 = (f32[128,512]{0,1:T(8,128)S(1)}, f32[128,512]{0,1:T(8,128)}, u32[]{:S(2)}) copy-start(f32[128,512]{0,1:T(8,128)} %get-tuple-element.7) | copy-start | bytes 786436
  137.2 3.2 %copy-start.5 = (s32[256]{0:T(256)S(1)}, s32[256]{0:T(256)}, u32[]{:S(2)}) copy-start(s32[256]{0:T(256)} %param.10) | copy-start | bytes 3076
  139.1 1.3 copy-start
  143.1 92.5 %all-gather.2.cloned.1.call-start = ((), (), s32[]{:S(2)}) async-start(), calls=%async_computation.1 | async-start | bytes 2621440 | tf_op jit(solution)/shard_map/all_gather | solution.py:53
  199.5 36.1 %copy-start.6 = (s32[32]{0:T(128)S(1)}, s32[32]{0:T(128)}, u32[]{:S(2)}) copy-start(s32[32]{0:T(128)} %param.9) | copy-start | bytes 388
Sparse Core Ops, SparseCore 0:
  29.0 44.6 all-reduce.9
  86.7 43.6 all-reduce.7
  143.3 56.1 all-reduce.5
  201.3 34.2 all-gather.1
where the time goes:
time: 254 us; the launch traced here: 253 us
  waiting for transfers between devices  160 us (63%)
  matrix products  34.8 us (14%)
  blocking collectives  31.5 us (12%)
  between operations  14.1 us (6%)
  local copies, waits for them, and re-layouts  12.2 us (5%)
    psum x2, waiting for transfers between devices, apply_block(): lax.psum((precise(vectors.T, field), precise(vectors.T, vectors)), 'row')  70.6 us
    psum x1, waiting for transfers between devices, per_device(): rows_part = lax.psum(picked.astype(jnp.bfloat16), 'col')  56.2 us
    all_gather x1, waiting for transfers between devices, per_device(): panel = lax.all_gather(rows_part, 'row', axis=0, tiled=True)  33.2 us
    dot_general x33, matrix products, precise(): jnp.dot(left, right, precision=lax.Precision.HIGHEST, preferred_element_t...  26.1 us
    all_gather x1, blocking collectives, per_device(): lax.all_gather(house_two, 'col', axis=1, tiled=True)  16.8 us
    all_gather x1, blocking collectives, per_device(): lax.all_gather(house_one, 'col', axis=1, tiled=True)  14.7 us
    unnamed x17, local copies, waits for them, and re-layouts  7.04 us
    dot_general x1, matrix products, expand_panel(): return jnp.dot(ritz_basis, ordered, preferred_element_type=jnp.float32)  5.77 us
  transfers between devices with their start and end apart: 4, of which 4 were waited for; matrix products, arithmetic and copies ran while one was open for 2% of the time, Pallas kernels for 0%

commit v1 on v0

v1 whole, which is shorter than its diff:
```python
import functools

import jax
import jax.numpy as jnp
from jax import lax
from jax.experimental import pallas as pl
from jax.experimental.pallas import tpu as pltpu
from jax.sharding import PartitionSpec as P

TILE = 128
F32 = jnp.float32
BF16 = jnp.bfloat16


def precise(left, right):
    return jnp.dot(left, right, precision=lax.Precision.HIGHEST, preferred_element_type=F32)


def inverses(grams):
    width = grams[0].shape[0]
    rows = lax.broadcasted_iota(jnp.int32, (width, width), 0)
    cols = lax.broadcasted_iota(jnp.int32, (width, width), 1)
    identity = (rows == cols).astype(F32)
    powers, totals, downs = [], [], []
    for gram in grams:
        diagonal = 0.5 * gram * identity
        across = 1.0 / jnp.sum(diagonal, axis=1, keepdims=True)
        downs.append(1.0 / jnp.sum(diagonal, axis=0, keepdims=True))
        power = jnp.where(rows < cols, -gram * across, 0.0)
        powers.append(power)
        totals.append(identity + power)
    for _ in range((width - 1).bit_length() - 1):
        powers = [precise(power, power) for power in powers]
        totals = [precise(total, identity + power) for total, power in zip(totals, powers)]
    return [total * down for total, down in zip(totals, downs)]


def factor_kernel(place_ref, gram_ref, out_ref):
    size = gram_ref.shape[0]
    half = size // 2
    reflectors = lax.broadcasted_iota(jnp.int32, (size, size), 0)
    order = (reflectors == place_ref[...]).astype(F32)
    turned = (((1,), (1,)), ((), ()))
    gram = lax.dot_general(
        precise(order, gram_ref[...]), order, turned, precision=lax.Precision.HIGHEST, preferred_element_type=F32
    )
    two, one = inverses([gram[:half, :half], gram[half:, half:]])
    mixed = -precise(one, precise(gram[half:, :half], two))
    factor = jnp.concatenate(
        [
            jnp.concatenate([two, jnp.zeros_like(two)], axis=1),
            jnp.concatenate([mixed, one], axis=1),
        ],
        axis=0,
    )
    front = lax.dot_general(
        order, factor, (((0,), (0,)), ((), ())), precision=lax.Precision.HIGHEST, preferred_element_type=F32
    )
    out_ref[...] = precise(front, order)


def factor_of(place, gram):
    size = gram.shape[0]
    return pl.pallas_call(
        factor_kernel,
        out_shape=jax.ShapeDtypeStruct((size, size), F32),
        compiler_params=pltpu.CompilerParams(vmem_limit_bytes=32 << 20),
        cost_estimate=pl.CostEstimate(flops=2 * 6 * 16 * size**3, bytes_accessed=8 * size * size, transcendentals=0),
    )(place, gram)


def modes_kernel(
    here_ref, map_ref, ritz_ref, mine_e, sib_e, mine_v, sib_v, factor_ref, out_ref, sel, vec, buffer, sems
):
    row_at, deep_at, core_at = here_ref[0], here_ref[1], here_ref[2]
    peers, deep, piece, _ = mine_e.shape
    local = mine_v.shape[2]
    chunk = buffer.shape[1]
    steps = ritz_ref.shape[0] // chunk

    def fetch(step):
        return pltpu.make_async_copy(
            ritz_ref.at[pl.ds(step * chunk, chunk)], buffer.at[step], sems.at[step]
        )

    for step in range(steps):
        fetch(step).start()
    tile = min(TILE, local)
    half = vec.shape[0] // 2
    for peer in range(peers):
        start = (row_at ^ peer) * local
        for core, source in ((core_at, mine_e), (1 - core_at, sib_e)):
            for level in range(deep):
                row = start + ((deep_at ^ level) * 2 + core) * piece
                goal = map_ref[row // TILE] * TILE + row % TILE
                sel[pl.ds(pl.multiple_of(goal, piece), piece), :] = source[peer, level]
        for at in range(0, local, tile):
            goal = pl.multiple_of(map_ref[(start + at) // TILE] * TILE, TILE)
            vec[:half, pl.ds(goal, tile)] = mine_v[peer, :, at : at + tile]
            vec[half:, pl.ds(goal, tile)] = sib_v[peer, :, at : at + tile]
    projected = jnp.dot(vec[...], sel[...], preferred_element_type=F32)
    weights = precise(factor_ref[...], projected).astype(BF16)
    change = lax.dot_general(vec[...], weights, (((0,), (0,)), ((), ())), preferred_element_type=F32)
    sel[...] = (sel[...].astype(F32) - change).astype(BF16)
    for step in range(steps):
        fetch(step).wait()
        out_ref[pl.ds(step * chunk, chunk), :] = jnp.dot(
            buffer[step], sel[...], preferred_element_type=F32
        ).astype(BF16)


def modes_of(here, tile_map, ritz_basis, mine_e, sib_e, mine_v, sib_v, factor):
    dofs, order = ritz_basis.shape
    width = mine_e.shape[-1]
    size = factor.shape[0]
    chunk = 256
    in_vmem = pl.BlockSpec(memory_space=pltpu.VMEM)
    in_smem = pl.BlockSpec(memory_space=pltpu.SMEM)
    return pl.pallas_call(
        modes_kernel,
        out_shape=jax.ShapeDtypeStruct((dofs, width), BF16),
        in_specs=[in_smem, in_smem, pl.BlockSpec(memory_space=pl.ANY)] + [in_vmem] * 5,
        out_specs=in_vmem,
        scratch_shapes=[
            pltpu.VMEM((order, width), BF16),
            pltpu.VMEM((size, order), BF16),
            pltpu.VMEM((dofs // chunk, chunk, order), BF16),
            pltpu.SemaphoreType.DMA((dofs // chunk,)),
        ],
        compiler_params=pltpu.CompilerParams(vmem_limit_bytes=48 << 20),
        cost_estimate=pl.CostEstimate(
            flops=2 * order * width * (dofs + 2 * size), bytes_accessed=2 * dofs * order, transcendentals=0
        ),
    )(here, tile_map, ritz_basis, mine_e, sib_e, mine_v, sib_v, factor)


def per_device(rows, cols, eigvecs, house_one, house_two, tile_map, select, ritz_basis):
    deep = cols // 2
    row_at, col_at = lax.axis_index("row"), lax.axis_index("col")
    deep_at, core_at = col_at // 2, col_at % 2
    local, wide = eigvecs.shape
    width = select.shape[0]
    share = house_one.shape[1]
    size = 2 * share * cols

    def to_core(x):
        return lax.ppermute(x, "col", [(i, i ^ 1) for i in range(cols)])

    def to_deep(x, level):
        return lax.ppermute(x, "col", [(i, i ^ (2 * level)) for i in range(cols)])

    def to_row(x, peer):
        return lax.ppermute(x, "row", [(i, i ^ peer) for i in range(rows)])

    own = jnp.concatenate([house_two.T, house_one.T], axis=0).astype(BF16)
    mine_here = jnp.concatenate([own] + [to_deep(own, level) for level in range(1, deep)], axis=0)
    sib_here = to_core(mine_here)
    here_v = jnp.concatenate([mine_here, sib_here], axis=0)
    mine_far = [to_row(mine_here, peer) for peer in range(1, rows)]
    mine_v = jnp.stack([mine_here] + mine_far)
    sib_v = jnp.concatenate([sib_here[None], to_core(jnp.stack(mine_far))])

    field = eigvecs.astype(BF16)
    ids = col_at * wide + jnp.arange(wide, dtype=jnp.int32)
    chooser = (ids[:, None] == select[None, :]).astype(BF16)
    piece = local // cols
    picked = jnp.dot(field, chooser, preferred_element_type=F32).astype(BF16)
    picked = picked.reshape(deep, 2, piece, width)
    first = core_at == 0
    keep = jnp.where(first, picked[:, 0], picked[:, 1])
    give = jnp.where(first, picked[:, 1], picked[:, 0])
    keep = keep + to_core(give)
    block = lax.dynamic_index_in_dim(keep, deep_at, 0, keepdims=False)
    for level in range(1, deep):
        block = block + to_deep(lax.dynamic_index_in_dim(keep, deep_at ^ level, 0, keepdims=False), level)
    mine_sel = jnp.stack([block] + [to_deep(block, level) for level in range(1, deep)])
    mine_e = jnp.stack([mine_sel] + [to_row(mine_sel, peer) for peer in range(1, rows)])
    sib_e = to_core(mine_e)

    part = wide // rows
    partial = jnp.dot(here_v, field, preferred_element_type=F32)

    def chunk_of(x, peer):
        return lax.dynamic_slice_in_dim(x, (row_at ^ peer) * part, part, axis=1)

    projected = chunk_of(partial, 0)
    for peer in range(1, rows):
        projected = projected + to_row(chunk_of(partial, peer).astype(BF16), peer).astype(F32)

    turned = (((1,), (1,)), ((), ()))
    gram = jnp.zeros((size, size), F32)
    for peer in range(rows):
        both = jnp.concatenate([mine_v[peer], sib_v[peer]], axis=0)
        gram = gram + lax.dot_general(both, both, turned, preferred_element_type=F32)
    arrival = jnp.arange(size, dtype=jnp.int32)
    at_share = arrival % share
    at_block = arrival // share % 2
    at_level = arrival // (2 * share) % deep
    at_core = arrival // (2 * share * deep)
    place = at_block * (size // 2) + ((at_level ^ deep_at) * 2 + (at_core ^ core_at)) * share + at_share
    factor = factor_of(place[None, :], gram)

    weights = precise(factor, projected).astype(BF16)
    all_weights = jnp.zeros((size, wide), BF16)
    for peer in range(rows):
        arrived = to_row(weights, peer) if peer else weights
        all_weights = lax.dynamic_update_slice_in_dim(all_weights, arrived, (row_at ^ peer) * part, axis=1)
    change = lax.dot_general(here_v, all_weights, (((0,), (0,)), ((), ())), preferred_element_type=F32)
    back_vectors = eigvecs - change

    here = jnp.stack([row_at, deep_at, core_at]).astype(jnp.int32)
    modes = modes_of(here, tile_map, ritz_basis, mine_e, sib_e, mine_v, sib_v, factor)
    return back_vectors, modes


def solution(mesh):
    return jax.shard_map(
        functools.partial(per_device, mesh.shape["row"], mesh.shape["col"]),
        mesh=mesh,
        in_specs=(P("row", "col"), P("row", "col"), P("row", "col"), P(), P(), P(("row", "col"), None)),
        out_specs=(P("row", "col"), P(("row", "col"), None)),
        check_vma=False,
    )
```

time: 254 us -> 84.5 us (0.33)
  waiting for transfers between devices: 160 us -> 19.9 us
  blocking collectives: 31.5 us -> 0 us
  starting transfers between devices: 0.34 us -> 29.8 us
  matrix products: 34.8 us -> 7.24 us
  Pallas kernels: 0 us -> 14.6 us
  between operations: 14.1 us -> 1.15 us
  local copies, waits for them, and re-layouts: 12.2 us -> 5.06 us
  other arithmetic: 0.02 us -> 6.42 us
    psum x3 -> x0, waiting for transfers between devices: 127 us -> none  [the longest x2 70.6 us: apply_block(): lax.psum((precise(vectors.T, field), precise(vectors.T, vectors)), 'row')]
    all_gather x1 -> x0, waiting for transfers between devices: 33.2 us -> none  [per_device(): panel = lax.all_gather(rows_part, 'row', axis=0, tiled=True)]
    all_gather x2 -> x0, blocking collectives: 31.5 us -> none  [the longest x1 16.8 us: per_device(): lax.all_gather(house_two, 'col', axis=1, tiled=True)]
    ppermute x0 -> x25, starting transfers between devices: none -> 29.8 us  [the longest x12 15.1 us: to_row(): return lax.ppermute(x, 'row', [(i, i ^ peer) for i in range(rows)])]
    dot_general x33 -> x1, matrix products: 26.1 us -> 0.42 us  [precise(): jnp.dot(left, right, precision=lax.Precision.HIGHEST, preferred_element_t...]
    ppermute x0 -> x25, waiting for transfers between devices: none -> 19.9 us  [the longest x12 10.9 us: to_row(): return lax.ppermute(x, 'row', [(i, i ^ peer) for i in range(rows)])]
    pallas_call x0 -> x2, Pallas kernels: none -> 14.6 us  [the longest x1 10 us: modes_of(): pl.pallas_call(modes_kernel, out_shape=jax.ShapeDtypeStruct((dofs, width)...]
    unnamed x17 -> x10, local copies, waits for them, and re-layouts: 7.04 us -> 2.43 us
  transfers between devices with their start and end apart: 4 -> 25, of which waited for: 4 -> 9; matrix products, arithmetic and copies ran while one was open for 2% -> 19% of each run, Pallas kernels for 0% -> 5%
where the time goes in v1:
time: 84.5 us; the launch traced here: 84.1 us
  starting transfers between devices  29.8 us (35%)
  waiting for transfers between devices  19.9 us (24%)
  Pallas kernels  14.6 us (17%)
  matrix products  7.24 us (9%)
  other arithmetic  6.42 us (8%)
  local copies, waits for them, and re-layouts  5.06 us (6%)
  between operations  1.15 us (1%)
    ppermute x12, starting transfers between devices, to_row(): return lax.ppermute(x, 'row', [(i, i ^ peer) for i in range(rows)])  15.1 us
    ppermute x9, starting transfers between devices, to_deep(): return lax.ppermute(x, 'col', [(i, i ^ 2 * level) for i in range(cols)])  14.5 us
    ppermute x12, waiting for transfers between devices, to_row(): return lax.ppermute(x, 'row', [(i, i ^ peer) for i in range(rows)])  10.9 us
    pallas_call x1, Pallas kernels, modes_of(): pl.pallas_call(modes_kernel, out_shape=jax.ShapeDtypeStruct((dofs, width)...  10 us
    ppermute x9, waiting for transfers between devices, to_deep(): return lax.ppermute(x, 'col', [(i, i ^ 2 * level) for i in range(cols)])  8.88 us
    pallas_call x1, Pallas kernels, factor_of(): pl.pallas_call(factor_kernel, out_shape=jax.ShapeDtypeStruct((size, size)...  4.57 us
    unnamed x2, other arithmetic  2.92 us
    unnamed x10, local copies, waits for them, and re-layouts  2.43 us
  transfers between devices with their start and end apart: 25, of which 9 were waited for; matrix products, arithmetic and copies ran while one was open for 19% of the time, Pallas kernels for 5%

profile of v1, /device:TPU:0, one launch (start us, length us, event | category | flops | bytes accessed | tf_op | source)
XLA Modules:
  0.0 84.1 jit_solution(11983482970992899751)
XLA Ops:
  0.6 1.5 %constant_dynamic-update-slice_fusion.4 = (bf16[128,1024]{1,0:T(8,128)(2,1)}, bf16[16,1024]{1,0:T(8,128)(2,1)S(1)}) fusion(f32[1024,16]{0,1:T(8,128)} %param.8), kind=kLoop, calls=%fused_computation.58 | loop fusion | flops 16383 | bytes 131072
  2.1 1.5 %constant_dynamic-update-slice_fusion.3 = (bf16[128,1024]{1,0:T(8,128)(2,1)}, bf16[16,1024]{1,0:T(8,128)(2,1)S(1)}) fusion(bf16[128,1024]{1,0:T(8,128)(2,1)} %get-tuple-element.4, f32[1024,16]{0,1:T(8,128)} %param.7), kind=kLoop, calls=%fused_computation.57 | loop fusion | flops 16384 | bytes 131072
  3.6 5.0 %collective-permute-start.2 = (bf16[32,1024]{1,0:T(8,128)(2,1)S(1)}, bf16[32,1024]{1,0:T(8,128)(2,1)S(1)}, u32[]{:S(2)}, u32[]{:S(2)}) collective-permute-start(bf16[32,1024]{1,0:T(8,128)(2,1)S(1)} %pad_maximum_fusion.5), channel_id=1, source_target_pairs={{0,6},{1,7},{2,4},{3,5},{4,2},{5,3},{6,0},{7,1},{8,14},{9,15},{10,... | collective-permute-start | bytes 196616 | tf_op jit(solution)/shard_map/ppermute | solution.py:150
  9.2 2.2 %fusion = bf16[1024,256]{0,1:T(8,128)(2,1)S(1)} fusion(f32[1024,512]{1,0:T(8,128)} %param.6, s32[256]{0:T(256)} %param.10, s32[512]{0:T(512)S(1)} %iota_add_fusion), kind=kOutput, calls=%fused_computation.2 | convolution fusion | flops 269484032 | bytes 2624512 | tf_op jit(solution)/shard_map/dot_general | solution.py:167
  16.1 1.4 %collective-permute-start.15 = (bf16[128,256]{1,0:T(8,128)(2,1)S(1)}, bf16[128,256]{1,0:T(8,128)(2,1)S(1)}, u32[]{:S(2)}, u32[]{:S(2)}) collective-permute-start(bf16[128,256]{1,0:T(8,128)(2,1)S(1)} %get-tuple-element.16), channel_id=1, source_target_pairs={{0,2},{1,3},{2,0},{3,1},{4,6},{5,7},{6,4},{7,5},{8,10},{9,11},{10,... | collective-permute-start | bytes 196616 | tf_op jit(solution)/shard_map/ppermute | solution.py:150
  18.1 2.4 %collective-permute-start.6 = (bf16[128,1024]{1,0:T(8,128)(2,1)}, bf16[128,1024]{1,0:T(8,128)(2,1)S(1)}, u32[]{:S(2)}, u32[]{:S(2)}) collective-permute-start(bf16[128,1024]{1,0:T(8,128)(2,1)} %get-tuple-element.19), channel_id=1, source_target_pairs={{0,24},{8,16},{16,8},{24,0},{1,25},{9,17},{17,9},{25,1},{2,26},{10... | collective-permute-start | bytes 786440 | tf_op jit(solution)/shard_map/ppermute | solution.py:153
  21.6 2.4 %collective-permute-start.17 = (bf16[128,256]{1,0:T(8,128)(2,1)}, bf16[128,256]{1,0:T(8,128)(2,1)S(1)}, u32[]{:S(2)}, u32[]{:S(2)}) collective-permute-start(bf16[128,256]{1,0:T(8,128)(2,1)} %get-tuple-element.17), channel_id=1, source_target_pairs={{0,6},{1,7},{2,4},{3,5},{4,2},{5,3},{6,0},{7,1},{8,14},{9,15},{10,... | collective-permute-start | bytes 196616 | tf_op jit(solution)/shard_map/ppermute | solution.py:150
  24.6 4.1 %collective-permute-done.17 = bf16[128,256]{1,0:T(8,128)(2,1)S(1)} collective-permute-done((bf16[128,256]{1,0:T(8,128)(2,1)}, bf16[128,256]{1,0:T(8,128)(2,1)S(1)}, u32[]{:S(2)}, u32[]{:S(2)}) %collective-permute-start.17) | collective-permute-done | bytes 65568 | tf_op jit(solution)/shard_map/ppermute | solution.py:150
  28.7 1.9 %collective-permute-done.16 = bf16[128,256]{1,0:T(8,128)(2,1)} collective-permute-done((bf16[128,256]{1,0:T(8,128)(2,1)}, bf16[128,256]{1,0:T(8,128)(2,1)}, u32[]{:S(2)}, u32[]{:S(2)}) %collective-permute-start.16) | collective-permute-done | bytes 65568 | tf_op jit(solution)/shard_map/ppermute | solution.py:150
  31.5 2.6 %collective-permute-start.20 = (bf16[128,256]{1,0:T(8,128)(2,1)S(1)}, bf16[128,256]{1,0:T(8,128)(2,1)S(1)}, u32[]{:S(2)}, u32[]{:S(2)}) collective-permute-start(bf16[128,256]{1,0:T(8,128)(2,1)S(1)} %fusion.28), channel_id=1, source_target_pairs={{0,6},{1,7},{2,4},{3,5},{4,2},{5,3},{6,0},{7,1},{8,14},{9,15},{10,... | collective-permute-start | bytes 196616 | tf_op jit(solution)/shard_map/ppermute | solution.py:150
  34.1 1.8 %collective-permute-start.18 = (bf16[128,256]{1,0:T(8,128)(2,1)S(1)}, bf16[128,256]{1,0:T(8,128)(2,1)S(1)}, u32[]{:S(2)}, u32[]{:S(2)}) collective-permute-start(bf16[128,256]{1,0:T(8,128)(2,1)S(1)} %fusion.28), channel_id=1, source_target_pairs={{0,2},{1,3},{2,0},{3,1},{4,6},{5,7},{6,4},{7,5},{8,10},{9,11},{10,... | collective-permute-start | bytes 196616 | tf_op jit(solution)/shard_map/ppermute | solution.py:150
  38.0 2.0 %collective-permute-done.19 = bf16[128,256]{1,0:T(8,128)(2,1)S(1)} collective-permute-done((bf16[128,256]{1,0:T(8,128)(2,1)S(1)}, bf16[128,256]{1,0:T(8,128)(2,1)S(1)}, u32[]{:S(2)}, u32[]{:S(2)}) %collective-permute-start.19) | collective-permute-done | bytes 65568 | tf_op jit(solution)/shard_map/ppermute | solution.py:150
  40.0 1.6 %collective-permute-start.22 = (bf16[4,128,256]{2,1,0:T(8,128)(2,1)S(1)}, bf16[4,128,256]{2,1,0:T(8,128)(2,1)S(1)}, u32[]{:S(2)}, u32[]{:S(2)}) collective-permute-start(bf16[4,128,256]{2,1,0:T(8,128)(2,1)S(1)} %get-tuple-element.15), channel_id=1, source_target_pairs={{0,16},{8,24},{16,0},{24,8},{1,17},{9,25},{17,1},{25,9},{2,18},{10... | collective-permute-start | bytes 786440 | tf_op jit(solution)/shard_map/ppermute | solution.py:153
  41.6 1.5 %collective-permute-start.21 = (bf16[4,128,256]{2,1,0:T(8,128)(2,1)S(1)}, bf16[4,128,256]{2,1,0:T(8,128)(2,1)S(1)}, u32[]{:S(2)}, u32[]{:S(2)}) collective-permute-start(bf16[4,128,256]{2,1,0:T(8,128)(2,1)S(1)} %get-tuple-element.15), channel_id=1, source_target_pairs={{0,8},{8,0},{16,24},{24,16},{1,9},{9,1},{17,25},{25,17},{2,10},{10... | collective-permute-start | bytes 786440 | tf_op jit(solution)/shard_map/ppermute | solution.py:153
  44.1 1.6 %collective-permute-start.8 = (bf16[256,128]{1,0:T(8,128)(2,1)S(1)}, bf16[256,128]{1,0:T(8,128)(2,1)S(1)}, u32[]{:S(2)}, u32[]{:S(2)}) collective-permute-start(bf16[256,128]{1,0:T(8,128)(2,1)S(1)} %get-tuple-element.11), channel_id=1, source_target_pairs={{0,8},{8,0},{16,24},{24,16},{1,9},{9,1},{17,25},{25,17},{2,10},{10... | collective-permute-start | bytes 196616 | tf_op jit(solution)/shard_map/ppermute | solution.py:153
  46.8 1.6 %collective-permute-done.22 = bf16[4,128,256]{2,1,0:T(8,128)(2,1)S(1)} collective-permute-done((bf16[4,128,256]{2,1,0:T(8,128)(2,1)S(1)}, bf16[4,128,256]{2,1,0:T(8,128)(2,1)S(1)}, u32[]{:S(2)}, u32[]{:S(2)}) %collective-permute-start.22) | collective-permute-done | bytes 262176 | tf_op jit(solution)/shard_map/ppermute | solution.py:153
  48.4 2.5 %collective-permute-start.10 = (bf16[256,128]{1,0:T(8,128)(2,1)S(1)}, bf16[256,128]{1,0:T(8,128)(2,1)S(1)}, u32[]{:S(2)}, u32[]{:S(2)}) collective-permute-start(bf16[256,128]{1,0:T(8,128)(2,1)S(1)} %get-tuple-element.12), channel_id=1, source_target_pairs={{0,24},{8,16},{16,8},{24,0},{1,25},{9,17},{17,9},{25,1},{2,26},{10... | collective-permute-start | bytes 196616 | tf_op jit(solution)/shard_map/ppermute | solution.py:153
  51.4 5.1 %collective-permute-done.23 = bf16[4,128,256]{2,1,0:T(8,128)(2,1)S(1)} collective-permute-done((bf16[4,128,256]{2,1,0:T(8,128)(2,1)S(1)}, bf16[4,128,256]{2,1,0:T(8,128)(2,1)S(1)}, u32[]{:S(2)}, u32[]{:S(2)}) %collective-permute-start.23) | collective-permute-done | bytes 262176 | tf_op jit(solution)/shard_map/ppermute | solution.py:153
  59.2 4.6 %shard_map.77.factor_ref = f32[256,256]{1,0:T(8,128)S(1)} custom-call(s32[1,256]{1,0:T(1,128)S(1)} %fusion.30.place_ref, f32[256,256]{1,0:T(8,128)S(1)} %fusion.2.gram_ref), custom_call_target="tpu_custom_call" | custom-call | flops 3221225472 | bytes 524288 | tf_op jit(solution)/shard_map/pallas_call | solution.py:64
  64.3 1.6 %collective-permute-start.12 = (bf16[256,128]{1,0:T(8,128)(2,1)S(1)}, bf16[256,128]{1,0:T(8,128)(2,1)S(1)}, u32[]{:S(2)}, u32[]{:S(2)}) collective-permute-start(bf16[256,128]{1,0:T(8,128)(2,1)S(1)} %get-tuple-element.26), channel_id=1, source_target_pairs={{0,16},{8,24},{16,0},{24,8},{1,17},{9,25},{17,1},{25,9},{2,18},{10... | collective-permute-start | bytes 196616 | tf_op jit(solution)/shard_map/ppermute | solution.py:153
  67.9 2.5 %collective-permute-done.11 = bf16[256,128]{1,0:T(8,128)(2,1)S(1)} collective-permute-done((bf16[256,128]{1,0:T(8,128)(2,1)S(1)}, bf16[256,128]{1,0:T(8,128)(2,1)S(1)}, u32[]{:S(2)}, u32[]{:S(2)}) %collective-permute-start.11) | collective-permute-done | bytes 65568 | tf_op jit(solution)/shard_map/ppermute | solution.py:153
  70.5 1.6 %collective-permute-done.13 = bf16[256,128]{1,0:T(8,128)(2,1)S(1)} collective-permute-done((bf16[256,128]{1,0:T(8,128)(2,1)S(1)}, bf16[256,128]{1,0:T(8,128)(2,1)S(1)}, u32[]{:S(2)}, u32[]{:S(2)}) %collective-permute-start.13) | collective-permute-done | bytes 65568 | tf_op jit(solution)/shard_map/ppermute | solution.py:153
  72.2 1.8 %convolution_subtract_fusion = f32[1024,512]{1,0:T(8,128)} fusion(f32[1024,512]{1,0:T(8,128)S(1)} %copy-done.1, bf16[256,1024]{1,0:T(8,128)(2,1)S(1)} %constant_dynamic-update-slice_fusion.5, bf16[256,512]{1,0:T(8,128)(2,1)S(1)} %constant_dynamic-update-slice_fusion.11), kind=kOutput, calls=%fused_computation | convolution fusion | flops 268959744 | bytes 4980736 | tf_op jit(solution)/shard_map/dot_general | solution.py:208
  73.9 10.0 %shard_map.78 = bf16[1024,256]{1,0:T(8,128)(2,1)} custom-call(s32[3]{0:T(128)S(1)} %pad_add_fusion.here_ref, s32[32]{0:T(128)S(1)} %copy-done, bf16[1024,4096]{1,0:T(8,128)(2,1)} %ritz_ref.1, bf16[4,4,128,256]{3,2,1,0:T(8,128)(2,1)S(1)} %pad_maximum_fusion.mine_e, bf16[4,4,128,256]{3,2,1,0:T(8,128)(2,1)S(1)} %collective-permute-done.24.sib_e, ...), custom_call_target="tpu_custom_call" | custom-call | flops 3221225472 | bytes 8388608 | tf_op jit(solution)/shard_map/pallas_call | solution.py:119
  (71 shorter events, 18.3 us)
Async XLA Ops:
  3.6 13.9 %collective-permute-start.2 = (bf16[32,1024]{1,0:T(8,128)(2,1)S(1)}, bf16[32,1024]{1,0:T(8,128)(2,1)S(1)}, u32[]{:S(2)}, u32[]{:S(2)}) collective-permute-start(bf16[32,1024]{1,0:T(8,128)(2,1)S(1)} %pad_maximum_fusion.5), channel_id=1, source_target_pairs={{0,6},{1,7},{2,4},{3,5},{4,2},{5,3},{6,0},{7,1},{8,14},{9,15},{10,... | collective-permute-start | bytes 196616 | tf_op jit(solution)/shard_map/ppermute | solution.py:150
  8.6 6.0 %collective-permute-start.1 = (bf16[32,1024]{1,0:T(8,128)(2,1)S(1)}, bf16[32,1024]{1,0:T(8,128)(2,1)S(1)}, u32[]{:S(2)}, u32[]{:S(2)}) collective-permute-start(bf16[32,1024]{1,0:T(8,128)(2,1)S(1)} %pad_maximum_fusion.5), channel_id=1, source_target_pairs={{0,4},{1,5},{2,6},{3,7},{4,0},{5,1},{6,2},{7,3},{8,12},{9,13},{10,... | collective-permute-start | bytes 196616 | tf_op jit(solution)/shard_map/ppermute | solution.py:150
  8.6 5.3 %collective-permute-start = (bf16[32,1024]{1,0:T(8,128)(2,1)S(1)}, bf16[32,1024]{1,0:T(8,128)(2,1)S(1)}, u32[]{:S(2)}, u32[]{:S(2)}) collective-permute-start(bf16[32,1024]{1,0:T(8,128)(2,1)S(1)} %pad_maximum_fusion.5), channel_id=1, source_target_pairs={{0,2},{1,3},{2,0},{3,1},{4,6},{5,7},{6,4},{7,5},{8,10},{9,11},{10,... | collective-permute-start | bytes 196616 | tf_op jit(solution)/shard_map/ppermute | solution.py:150
  16.1 7.9 %collective-permute-start.15 = (bf16[128,256]{1,0:T(8,128)(2,1)S(1)}, bf16[128,256]{1,0:T(8,128)(2,1)S(1)}, u32[]{:S(2)}, u32[]{:S(2)}) collective-permute-start(bf16[128,256]{1,0:T(8,128)(2,1)S(1)} %get-tuple-element.16), channel_id=1, source_target_pairs={{0,2},{1,3},{2,0},{3,1},{4,6},{5,7},{6,4},{7,5},{8,10},{9,11},{10,... | collective-permute-start | bytes 196616 | tf_op jit(solution)/shard_map/ppermute | solution.py:150
  18.1 16.0 %collective-permute-start.6 = (bf16[128,1024]{1,0:T(8,128)(2,1)}, bf16[128,1024]{1,0:T(8,128)(2,1)S(1)}, u32[]{:S(2)}, u32[]{:S(2)}) collective-permute-start(bf16[128,1024]{1,0:T(8,128)(2,1)} %get-tuple-element.19), channel_id=1, source_target_pairs={{0,24},{8,16},{16,8},{24,0},{1,25},{9,17},{17,9},{25,1},{2,26},{10... | collective-permute-start | bytes 786440 | tf_op jit(solution)/shard_map/ppermute | solution.py:153
  20.6 13.5 %collective-permute-start.5 = (bf16[128,1024]{1,0:T(8,128)(2,1)}, bf16[128,1024]{1,0:T(8,128)(2,1)S(1)}, u32[]{:S(2)}, u32[]{:S(2)}) collective-permute-start(bf16[128,1024]{1,0:T(8,128)(2,1)} %get-tuple-element.19), channel_id=1, source_target_pairs={{0,16},{8,24},{16,0},{24,8},{1,17},{9,25},{17,1},{25,9},{2,18},{10... | collective-permute-start | bytes 786440 | tf_op jit(solution)/shard_map/ppermute | solution.py:153
  21.1 14.9 %collective-permute-start.4 = (bf16[128,1024]{1,0:T(8,128)(2,1)}, bf16[128,1024]{1,0:T(8,128)(2,1)}, u32[]{:S(2)}, u32[]{:S(2)}) collective-permute-start(bf16[128,1024]{1,0:T(8,128)(2,1)} %get-tuple-element.19), channel_id=1, source_target_pairs={{0,8},{8,0},{16,24},{24,16},{1,9},{9,1},{17,25},{25,17},{2,10},{10... | collective-permute-start | bytes 786440 | tf_op jit(solution)/shard_map/ppermute | solution.py:153
  21.6 7.1 %collective-permute-start.17 = (bf16[128,256]{1,0:T(8,128)(2,1)}, bf16[128,256]{1,0:T(8,128)(2,1)S(1)}, u32[]{:S(2)}, u32[]{:S(2)}) collective-permute-start(bf16[128,256]{1,0:T(8,128)(2,1)} %get-tuple-element.17), channel_id=1, source_target_pairs={{0,6},{1,7},{2,4},{3,5},{4,2},{5,3},{6,0},{7,1},{8,14},{9,15},{10,... | collective-permute-start | bytes 196616 | tf_op jit(solution)/shard_map/ppermute | solution.py:150
  24.0 6.6 %collective-permute-start.16 = (bf16[128,256]{1,0:T(8,128)(2,1)}, bf16[128,256]{1,0:T(8,128)(2,1)}, u32[]{:S(2)}, u32[]{:S(2)}) collective-permute-start(bf16[128,256]{1,0:T(8,128)(2,1)} %get-tuple-element.18), channel_id=1, source_target_pairs={{0,4},{1,5},{2,6},{3,7},{4,0},{5,1},{6,2},{7,3},{8,12},{9,13},{10,... | collective-permute-start | bytes 196616 | tf_op jit(solution)/shard_map/ppermute | solution.py:150
  28.7 8.4 %collective-permute-start.3 = (bf16[128,1024]{1,0:T(8,128)(2,1)}, bf16[128,1024]{1,0:T(8,128)(2,1)S(1)}, u32[]{:S(2)}, u32[]{:S(2)}) collective-permute-start(bf16[128,1024]{1,0:T(8,128)(2,1)} %get-tuple-element.19), channel_id=1, source_target_pairs={{0,1},{1,0},{2,3},{3,2},{4,5},{5,4},{6,7},{7,6},{8,9},{9,8},{10,11... | collective-permute-start | bytes 786440 | tf_op jit(solution)/shard_map/ppermute | solution.py:147
  31.5 6.5 %collective-permute-start.20 = (bf16[128,256]{1,0:T(8,128)(2,1)S(1)}, bf16[128,256]{1,0:T(8,128)(2,1)S(1)}, u32[]{:S(2)}, u32[]{:S(2)}) collective-permute-start(bf16[128,256]{1,0:T(8,128)(2,1)S(1)} %fusion.28), channel_id=1, source_target_pairs={{0,6},{1,7},{2,4},{3,5},{4,2},{5,3},{6,0},{7,1},{8,14},{9,15},{10,... | collective-permute-start | bytes 196616 | tf_op jit(solution)/shard_map/ppermute | solution.py:150
  34.1 5.9 %collective-permute-start.19 = (bf16[128,256]{1,0:T(8,128)(2,1)S(1)}, bf16[128,256]{1,0:T(8,128)(2,1)S(1)}, u32[]{:S(2)}, u32[]{:S(2)}) collective-permute-start(bf16[128,256]{1,0:T(8,128)(2,1)S(1)} %fusion.28), channel_id=1, source_target_pairs={{0,4},{1,5},{2,6},{3,7},{4,0},{5,1},{6,2},{7,3},{8,12},{9,13},{10,... | collective-permute-start | bytes 196616 | tf_op jit(solution)/shard_map/ppermute | solution.py:150
  34.1 5.9 %collective-permute-start.18 = (bf16[128,256]{1,0:T(8,128)(2,1)S(1)}, bf16[128,256]{1,0:T(8,128)(2,1)S(1)}, u32[]{:S(2)}, u32[]{:S(2)}) collective-permute-start(bf16[128,256]{1,0:T(8,128)(2,1)S(1)} %fusion.28), channel_id=1, source_target_pairs={{0,2},{1,3},{2,0},{3,1},{4,6},{5,7},{6,4},{7,5},{8,10},{9,11},{10,... | collective-permute-start | bytes 196616 | tf_op jit(solution)/shard_map/ppermute | solution.py:150
  37.0 19.7 %collective-permute-start.7 = (bf16[3,128,1024]{2,1,0:T(8,128)(2,1)S(1)}, bf16[3,128,1024]{2,1,0:T(8,128)(2,1)S(1)}, u32[]{:S(2)}, u32[]{:S(2)}) collective-permute-start(bf16[3,128,1024]{2,1,0:T(8,128)(2,1)S(1)} %pad_maximum_fusion.3), channel_id=1, source_target_pairs={{0,1},{1,0},{2,3},{3,2},{4,5},{5,4},{6,7},{7,6},{8,9},{9,8},{10,11... | collective-permute-start | bytes 2359304 | tf_op jit(solution)/shard_map/ppermute | solution.py:147
  40.0 8.4 %collective-permute-start.22 = (bf16[4,128,256]{2,1,0:T(8,128)(2,1)S(1)}, bf16[4,128,256]{2,1,0:T(8,128)(2,1)S(1)}, u32[]{:S(2)}, u32[]{:S(2)}) collective-permute-start(bf16[4,128,256]{2,1,0:T(8,128)(2,1)S(1)} %get-tuple-element.15), channel_id=1, source_target_pairs={{0,16},{8,24},{16,0},{24,8},{1,17},{9,25},{17,1},{25,9},{2,18},{10... | collective-permute-start | bytes 786440 | tf_op jit(solution)/shard_map/ppermute | solution.py:153
  41.6 9.3 %collective-permute-start.21 = (bf16[4,128,256]{2,1,0:T(8,128)(2,1)S(1)}, bf16[4,128,256]{2,1,0:T(8,128)(2,1)S(1)}, u32[]{:S(2)}, u32[]{:S(2)}) collective-permute-start(bf16[4,128,256]{2,1,0:T(8,128)(2,1)S(1)} %get-tuple-element.15), channel_id=1, source_target_pairs={{0,8},{8,0},{16,24},{24,16},{1,9},{9,1},{17,25},{25,17},{2,10},{10... | collective-permute-start | bytes 786440 | tf_op jit(solution)/shard_map/ppermute | solution.py:153
  43.1 13.4 %collective-permute-start.23 = (bf16[4,128,256]{2,1,0:T(8,128)(2,1)S(1)}, bf16[4,128,256]{2,1,0:T(8,128)(2,1)S(1)}, u32[]{:S(2)}, u32[]{:S(2)}) collective-permute-start(bf16[4,128,256]{2,1,0:T(8,128)(2,1)S(1)} %get-tuple-element.15), channel_id=1, source_target_pairs={{0,24},{8,16},{16,8},{24,0},{1,25},{9,17},{17,9},{25,1},{2,26},{10... | collective-permute-start | bytes 786440 | tf_op jit(solution)/shard_map/ppermute | solution.py:153
  44.1 19.7 %collective-permute-start.8 = (bf16[256,128]{1,0:T(8,128)(2,1)S(1)}, bf16[256,128]{1,0:T(8,128)(2,1)S(1)}, u32[]{:S(2)}, u32[]{:S(2)}) collective-permute-start(bf16[256,128]{1,0:T(8,128)(2,1)S(1)} %get-tuple-element.11), channel_id=1, source_target_pairs={{0,8},{8,0},{16,24},{24,16},{1,9},{9,1},{17,25},{25,17},{2,10},{10... | collective-permute-start | bytes 196616 | tf_op jit(solution)/shard_map/ppermute | solution.py:153
  48.4 15.4 %collective-permute-start.10 = (bf16[256,128]{1,0:T(8,128)(2,1)S(1)}, bf16[256,128]{1,0:T(8,128)(2,1)S(1)}, u32[]{:S(2)}, u32[]{:S(2)}) collective-permute-start(bf16[256,128]{1,0:T(8,128)(2,1)S(1)} %get-tuple-element.12), channel_id=1, source_target_pairs={{0,24},{8,16},{16,8},{24,0},{1,25},{9,17},{17,9},{25,1},{2,26},{10... | collective-permute-start | bytes 196616 | tf_op jit(solution)/shard_map/ppermute | solution.py:153
  50.9 12.9 %collective-permute-start.9 = (bf16[256,128]{1,0:T(8,128)(2,1)S(1)}, bf16[256,128]{1,0:T(8,128)(2,1)S(1)}, u32[]{:S(2)}, u32[]{:S(2)}) collective-permute-start(bf16[256,128]{1,0:T(8,128)(2,1)S(1)} %get-tuple-element.13), channel_id=1, source_target_pairs={{0,16},{8,24},{16,0},{24,8},{1,17},{9,25},{17,1},{25,9},{2,18},{10... | collective-permute-start | bytes 196616 | tf_op jit(solution)/shard_map/ppermute | solution.py:153
  56.6 17.3 %collective-permute-start.24 = (bf16[4,4,128,256]{3,2,1,0:T(8,128)(2,1)S(1)}, bf16[4,4,128,256]{3,2,1,0:T(8,128)(2,1)S(1)}, u32[]{:S(2)}, u32[]{:S(2)}) collective-permute-start(bf16[4,4,128,256]{3,2,1,0:T(8,128)(2,1)S(1)} %pad_maximum_fusion.mine_e), channel_id=1, source_target_pairs={{0,1},{1,0},{2,3},{3,2},{4,5},{5,4},{6,7},{7,6},{8,9},{9,8},{10,11... | collective-permute-start | bytes 3145736 | tf_op jit(solution)/shard_map/ppermute | solution.py:147
  64.3 6.2 %collective-permute-start.12 = (bf16[256,128]{1,0:T(8,128)(2,1)S(1)}, bf16[256,128]{1,0:T(8,128)(2,1)S(1)}, u32[]{:S(2)}, u32[]{:S(2)}) collective-permute-start(bf16[256,128]{1,0:T(8,128)(2,1)S(1)} %get-tuple-element.26), channel_id=1, source_target_pairs={{0,16},{8,24},{16,0},{24,8},{1,17},{9,25},{17,1},{25,9},{2,18},{10... | collective-permute-start | bytes 196616 | tf_op jit(solution)/shard_map/ppermute | solution.py:153
  65.8 4.6 %collective-permute-start.11 = (bf16[256,128]{1,0:T(8,128)(2,1)S(1)}, bf16[256,128]{1,0:T(8,128)(2,1)S(1)}, u32[]{:S(2)}, u32[]{:S(2)}) collective-permute-start(bf16[256,128]{1,0:T(8,128)(2,1)S(1)} %get-tuple-element.26), channel_id=1, source_target_pairs={{0,8},{8,0},{16,24},{24,16},{1,9},{9,1},{17,25},{25,17},{2,10},{10... | collective-permute-start | bytes 196616 | tf_op jit(solution)/shard_map/ppermute | solution.py:153
  67.0 5.2 %collective-permute-start.13 = (bf16[256,128]{1,0:T(8,128)(2,1)S(1)}, bf16[256,128]{1,0:T(8,128)(2,1)S(1)}, u32[]{:S(2)}, u32[]{:S(2)}) collective-permute-start(bf16[256,128]{1,0:T(8,128)(2,1)S(1)} %get-tuple-element.26), channel_id=1, source_target_pairs={{0,24},{8,16},{16,8},{24,0},{1,25},{9,17},{17,9},{25,1},{2,26},{10... | collective-permute-start | bytes 196616 | tf_op jit(solution)/shard_map/ppermute | solution.py:153
  (3 other events, 31.6 us)

commit v2 on v1

v2 whole, which is shorter than its diff:
```python
import functools

import jax
import jax.numpy as jnp
from jax import lax
from jax.experimental import pallas as pl
from jax.experimental.pallas import tpu as pltpu
from jax.sharding import PartitionSpec as P

TILE = 128
F32 = jnp.float32
BF16 = jnp.bfloat16


def precise(left, right):
    return jnp.dot(left, right, precision=lax.Precision.HIGHEST, preferred_element_type=F32)


def inverses(grams):
    width = grams[0].shape[0]
    rows = lax.broadcasted_iota(jnp.int32, (width, width), 0)
    cols = lax.broadcasted_iota(jnp.int32, (width, width), 1)
    identity = (rows == cols).astype(F32)
    powers, totals, downs = [], [], []
    for gram in grams:
        diagonal = 0.5 * gram * identity
        across = 1.0 / jnp.sum(diagonal, axis=1, keepdims=True)
        downs.append(1.0 / jnp.sum(diagonal, axis=0, keepdims=True))
        power = jnp.where(rows < cols, -gram * across, 0.0)
        powers.append(power)
        totals.append(identity + power)
    for _ in range((width - 1).bit_length() - 1):
        powers = [precise(power, power) for power in powers]
        totals = [precise(total, identity + power) for total, power in zip(totals, powers)]
    return [total * down for total, down in zip(totals, downs)]


def mirrored(number, rows):
    bits = rows.bit_length() - 1
    return sum(1 << (bits - 1 - bit) for bit in range(bits) if number >> bit & 1)


def pairs_of(mine, sib):
    mine = [part.at[at] for part in mine for at in range(part.shape[0])]
    sib = [part.at[at] for part in sib for at in range(part.shape[0])]
    rows = len(mine)
    for number in range(rows):
        other = mirrored(number, rows)
        yield mine[number], sib[other], (number, other)


def prepare_kernel(
    here_ref, select_ref, eig_ref, two_ref, one_ref, vec_ref, keep_ref, give_ref, buffer, picked, chosen, house, sems
):
    deep_at, core_at = here_ref[1], here_ref[2]
    steps, chunk, wide = buffer.shape
    deep, piece, width = keep_ref.shape
    share = two_ref.shape[0]
    small = [
        pltpu.make_async_copy(select_ref, chosen, sems.at[steps]),
        pltpu.make_async_copy(two_ref, house.at[0], sems.at[steps + 1]),
        pltpu.make_async_copy(one_ref, house.at[1], sems.at[steps + 2]),
    ]
    for copy in small:
        copy.start()

    def fetch(step):
        return pltpu.make_async_copy(eig_ref.at[pl.ds(step * chunk, chunk)], buffer.at[step], sems.at[step])

    for step in range(steps):
        fetch(step).start()
    for copy in small:
        copy.wait()
    vec_ref[:share, :] = house[0].astype(BF16)
    vec_ref[share:, :] = house[1].astype(BF16)
    ids = lax.broadcasted_iota(jnp.int32, (wide, width), 0) + (deep_at * 2 + core_at) * wide
    chooser = jnp.where(ids == chosen[...], 1.0, 0.0).astype(BF16)
    for step in range(steps):
        fetch(step).wait()
        picked[step * chunk : (step + 1) * chunk, :] = jnp.dot(
            buffer[step].astype(BF16), chooser, preferred_element_type=F32
        ).astype(BF16)
    for level in range(deep):
        for out, core in ((keep_ref, core_at), (give_ref, 1 - core_at)):
            row = ((deep_at ^ level) * 2 + core) * piece
            out[level] = picked[pl.ds(pl.multiple_of(row, piece), piece), :]


def prepare(here, select, eigvecs, two, one, cols):
    local, wide = eigvecs.shape
    width = select.shape[0]
    share = two.shape[0]
    deep, piece, steps = cols // 2, local // cols, 4
    in_vmem = pl.BlockSpec(memory_space=pltpu.VMEM)
    some = jax.ShapeDtypeStruct((deep, piece, width), BF16)
    return pl.pallas_call(
        prepare_kernel,
        out_shape=(jax.ShapeDtypeStruct((2 * share, local), BF16), some, some),
        in_specs=[pl.BlockSpec(memory_space=pltpu.SMEM)] + [pl.BlockSpec(memory_space=pltpu.HBM)] * 4,
        out_specs=(in_vmem,) * 3,
        scratch_shapes=[
            pltpu.VMEM((steps, local // steps, wide), F32),
            pltpu.VMEM((local, width), BF16),
            pltpu.VMEM((1, width), jnp.int32),
            pltpu.VMEM((2, share, local), F32),
            pltpu.SemaphoreType.DMA((steps + 3,)),
        ],
        compiler_params=pltpu.CompilerParams(vmem_limit_bytes=16 << 20),
        cost_estimate=pl.CostEstimate(
            flops=2 * local * wide * width, bytes_accessed=4 * local * wide, transcendentals=0
        ),
    )(here, select[None, :], eigvecs, two, one)


def moved(order, x):
    width = x.shape[1]
    high = x.astype(BF16)
    parts = jnp.concatenate([high, (x - high.astype(F32)).astype(BF16)], axis=1)
    both = jnp.dot(order, parts, preferred_element_type=F32)
    return both[:, :width] + both[:, width:]


def factor_kernel(count, place_ref, *refs):
    mine, sib, out_ref = refs[:count], refs[count : 2 * count], refs[2 * count]
    size = out_ref.shape[0]
    half = size // 2
    turned = (((1,), (1,)), ((), ()))
    gram = jnp.zeros((size, size), F32)
    for one, other, _ in pairs_of(mine, sib):
        both = jnp.concatenate([one[...], other[...]], axis=0)
        gram = gram + lax.dot_general(both, both, turned, preferred_element_type=F32)
    reflectors = lax.broadcasted_iota(jnp.int32, (size, size), 0)
    order = jnp.where(reflectors == place_ref[...], 1.0, 0.0)
    back = order.T.astype(BF16)
    order = order.astype(BF16)
    gram = moved(order, moved(order, gram).T)
    two, one = inverses([gram[:half, :half], gram[half:, half:]])
    mixed = -precise(one, precise(gram[half:, :half], two))
    factor = jnp.concatenate(
        [
            jnp.concatenate([two, jnp.zeros_like(two)], axis=1),
            jnp.concatenate([mixed, one], axis=1),
        ],
        axis=0,
    )
    out_ref[...] = moved(back, moved(back, factor).T).T


def factor_of(place, mine, sib):
    _, half, local = mine[0].shape
    size = 2 * half
    rows = sum(part.shape[0] for part in mine)
    return pl.pallas_call(
        functools.partial(factor_kernel, len(mine)),
        out_shape=jax.ShapeDtypeStruct((size, size), F32),
        compiler_params=pltpu.CompilerParams(vmem_limit_bytes=16 << 20),
        cost_estimate=pl.CostEstimate(
            flops=2 * size * size * rows * local + 2 * 6 * 16 * size**3,
            bytes_accessed=8 * size * size + 2 * size * rows * local,
            transcendentals=0,
        ),
    )(place, *mine, *sib)


def spread_kernel(count, here_ref, map_ref, ritz_ref, *refs):
    mine, sib = refs[:count], refs[count : 2 * count]
    vec, out_ref = refs[2 * count :]
    _, half, local = mine[0].shape
    for one, other, numbers in pairs_of(mine, sib):
        start = (here_ref[0] ^ jnp.where(here_ref[2] == 0, *numbers)) * local
        for at in range(0, local, TILE):
            goal = pl.multiple_of(map_ref[(start + at) // TILE] * TILE, TILE)
            vec[:half, pl.ds(goal, TILE)] = one[:, at : at + TILE]
            vec[half:, pl.ds(goal, TILE)] = other[:, at : at + TILE]
    out_ref[...] = lax.dot_general(
        ritz_ref[...], vec[...], (((1,), (1,)), ((), ())), preferred_element_type=F32
    ).astype(BF16)


def spread(here, tile_map, ritz_basis, mine, sib):
    dofs, order = ritz_basis.shape
    size = 2 * mine[0].shape[1]
    in_vmem = pl.BlockSpec(memory_space=pltpu.VMEM)
    in_smem = pl.BlockSpec(memory_space=pltpu.SMEM)
    return pl.pallas_call(
        functools.partial(spread_kernel, len(mine)),
        out_shape=(jax.ShapeDtypeStruct((size, order), BF16), jax.ShapeDtypeStruct((dofs, size), BF16)),
        in_specs=[in_smem, in_smem] + [in_vmem] * (1 + 2 * len(mine)),
        out_specs=(in_vmem, in_vmem),
        compiler_params=pltpu.CompilerParams(vmem_limit_bytes=16 << 20),
        cost_estimate=pl.CostEstimate(
            flops=2 * order * size * dofs, bytes_accessed=2 * dofs * order, transcendentals=0
        ),
    )(here, tile_map, ritz_basis, *mine, *sib)


def modes_kernel(count, here_ref, map_ref, ritz_ref, vec_ref, spread_ref, factor_ref, *refs):
    mine, sib = refs[:count], refs[count : 2 * count]
    out_ref, sel = refs[2 * count :]
    _, deep, piece, _ = mine[0].shape
    local = 2 * deep * piece
    for one, other, numbers in pairs_of(mine, sib):
        start = (here_ref[0] ^ jnp.where(here_ref[2] == 0, *numbers)) * local
        for core, source in ((here_ref[2], one), (1 - here_ref[2], other)):
            for level in range(deep):
                row = start + ((here_ref[1] ^ level) * 2 + core) * piece
                goal = pl.multiple_of(map_ref[row // TILE] * TILE + row % TILE, piece)
                sel[pl.ds(goal, piece), :] = source[level]
    projected = jnp.dot(vec_ref[...], sel[...], preferred_element_type=F32)
    weights = precise(factor_ref[...], projected).astype(BF16)
    modes = jnp.dot(ritz_ref[...], sel[...], preferred_element_type=F32)
    modes = modes - jnp.dot(spread_ref[...], weights, preferred_element_type=F32)
    out_ref[...] = modes.astype(BF16)


def modes_of(here, tile_map, ritz_basis, vec, spreads, factor, mine, sib):
    dofs, order = ritz_basis.shape
    width = mine[0].shape[-1]
    size = factor.shape[0]
    in_vmem = pl.BlockSpec(memory_space=pltpu.VMEM)
    in_smem = pl.BlockSpec(memory_space=pltpu.SMEM)
    return pl.pallas_call(
        functools.partial(modes_kernel, len(mine)),
        out_shape=jax.ShapeDtypeStruct((dofs, width), BF16),
        in_specs=[in_smem, in_smem] + [in_vmem] * (4 + 2 * len(mine)),
        out_specs=in_vmem,
        scratch_shapes=[pltpu.VMEM((order, width), BF16)],
        compiler_params=pltpu.CompilerParams(vmem_limit_bytes=16 << 20),
        cost_estimate=pl.CostEstimate(
            flops=2 * order * width * (dofs + size), bytes_accessed=2 * dofs * order, transcendentals=0
        ),
    )(here, tile_map, ritz_basis, vec, spreads, factor, *mine, *sib)


def per_device(rows, cols, eigvecs, house_one, house_two, tile_map, select, ritz_basis):
    deep = cols // 2
    row_at, col_at = lax.axis_index("row"), lax.axis_index("col")
    deep_at, core_at = col_at // 2, col_at % 2
    here = jnp.stack([row_at, deep_at, core_at]).astype(jnp.int32)
    local, wide = eigvecs.shape
    share = house_one.shape[1]
    size = 2 * share * cols

    def to_core(x):
        return lax.ppermute(x, "col", [(i, i ^ 1) for i in range(cols)])

    def to_deep(x, level):
        return lax.ppermute(x, "col", [(i, i ^ (2 * level)) for i in range(cols)])

    def to_row(x, peer):
        return lax.ppermute(x, "row", [(i, i ^ peer) for i in range(rows)])

    steps = rows.bit_length() - 1

    def over_step(x, step):
        pairs = []
        for row in range(rows):
            for col in range(cols):
                bit = steps - 1 - step if col % 2 else step
                pairs.append((row * cols + col, (row ^ (1 << bit)) * cols + col))
        return lax.ppermute(x, ("row", "col"), pairs)

    def over_rows(x, after=None):
        parts = [x[None]]
        for step in range(steps):
            held = jnp.concatenate(parts) if step else parts[0]
            if after is not None:
                held = lax.optimization_barrier((held, after(step)))[0]
            parts.append(over_step(held, step))
        return parts

    own, keep, give = prepare(here, select, eigvecs, house_two.T, house_one.T, cols)

    got, own = lax.optimization_barrier((to_core(give), own))
    keep = keep + got

    mine_here = jnp.concatenate([own] + [to_deep(own, level) for level in range(1, deep)], axis=0)
    mine_here, keep = lax.optimization_barrier((mine_here, keep))
    mine_v = over_rows(mine_here)
    sib_v = [to_core(x) for x in mine_v]

    part = wide // rows
    here_v = jnp.concatenate([mine_here, sib_v[0][0]], axis=0)
    partial = jnp.dot(here_v, eigvecs.astype(BF16), preferred_element_type=F32)

    def chunk_of(number):
        away = jnp.where(core_at == 0, number, mirrored(number, rows))
        return lax.dynamic_slice_in_dim(partial, (row_at ^ away) * part, part, axis=1)

    chunks = jnp.stack([chunk_of(number) for number in range(rows)])
    block, chunks = lax.optimization_barrier((keep[0], chunks))
    sums = []
    for step in reversed(range(steps)):
        kept = 1 << step
        chunks = chunks[:kept] + over_step(chunks[kept:].astype(BF16), step).astype(F32)
        sums.append(chunks)
    projected = chunks[0]

    arrival = jnp.arange(size, dtype=jnp.int32)
    at_share = arrival % share
    at_block = arrival // share % 2
    at_level = arrival // (2 * share) % deep
    at_core = arrival // (2 * share * deep)
    place = at_block * (size // 2) + ((at_level ^ deep_at) * 2 + (at_core ^ core_at)) * share + at_share
    factor = factor_of(place[None, :], mine_v, sib_v)

    for level in range(1, deep):
        block = block + to_deep(keep[level], level)
    mine_sel = jnp.stack([block] + [to_deep(block, level) for level in range(1, deep)])
    mine_e = over_rows(mine_sel, lambda step: sums[step] if step else (sums[step], sib_v))
    sib_e = [to_core(x) for x in mine_e]

    weights = precise(factor, projected).astype(BF16)
    all_weights = jnp.zeros((size, wide), BF16)
    for peer in range(rows):
        arrived = to_row(weights, peer) if peer else weights
        all_weights = lax.dynamic_update_slice_in_dim(all_weights, arrived, (row_at ^ peer) * part, axis=1)
    change = lax.dot_general(here_v, all_weights, (((0,), (0,)), ((), ())), preferred_element_type=F32)
    back_vectors = eigvecs - change

    vec, spreads = spread(here, tile_map, ritz_basis, mine_v, sib_v)
    modes = modes_of(here, tile_map, ritz_basis, vec, spreads, factor, mine_e, sib_e)
    return back_vectors, modes


def solution(mesh):
    return jax.shard_map(
        functools.partial(per_device, mesh.shape["row"], mesh.shape["col"]),
        mesh=mesh,
        in_specs=(P("row", "col"), P("row", "col"), P("row", "col"), P(), P(), P(("row", "col"), None)),
        out_specs=(P("row", "col"), P(("row", "col"), None)),
        check_vma=False,
    )
```

time: 84.5 us -> 69.5 us (0.82)
  other arithmetic: 6.42 us -> 0.42 us
  matrix products: 7.24 us -> 2.67 us
  waiting for transfers between devices: 19.9 us -> 16.3 us
  Pallas kernels: 14.6 us -> 17.1 us
  starting transfers between devices: 29.8 us -> 27.7 us
  local copies, waits for them, and re-layouts: 5.06 us -> 4.19 us
    ppermute x12 -> x3, starting transfers between devices: 15.1 us -> 3.55 us  [to_row(): return lax.ppermute(x, 'row', [(i, i ^ peer) for i in range(rows)])]
    ppermute x12 -> x3, waiting for transfers between devices: 10.9 us -> 0.7 us  [to_row(): return lax.ppermute(x, 'row', [(i, i ^ peer) for i in range(rows)])]
    ppermute x0 -> x6, starting transfers between devices: none -> 8.42 us  [over_step(): return lax.ppermute(x, ('row', 'col'), pairs)]
    ppermute x0 -> x6, waiting for transfers between devices: none -> 5.3 us  [over_step(): return lax.ppermute(x, ('row', 'col'), pairs)]
    dot_general x6 -> x1, matrix products: 5.03 us -> 0.45 us  [per_device(): partial = jnp.dot(here_v, eigvecs.astype(BF16), preferred_element_type=F32)]
    unnamed x2 -> x1, other arithmetic: 2.92 us -> 0.01 us
    pallas_call x2 -> x4, Pallas kernels: 14.6 us -> 17.1 us  [the longest x1 6.07 us: modes_of(): pl.pallas_call(functools.partial(modes_kernel, len(mine)), out_shape=jax....]
    another operation x4 -> x1, other arithmetic: 2.38 us -> 0.04 us  [per_device(): chunks = jnp.stack([chunk_of(number) for number in range(rows)])]
  transfers between devices with their start and end apart: 25 -> 25, of which waited for: 9 -> 10; matrix products, arithmetic and copies ran while one was open for 19% -> 5% of each run, Pallas kernels for 5% -> 13%
where the time goes in v2:
time: 69.5 us; the launch traced here: 69.2 us
  starting transfers between devices  27.7 us (40%)
  Pallas kernels  17.1 us (25%)
  waiting for transfers between devices  16.3 us (23%)
  local copies, waits for them, and re-layouts  4.19 us (6%)
  matrix products  2.67 us (4%)
  between operations  0.94 us (1%)
    ppermute x9, starting transfers between devices, to_deep(): return lax.ppermute(x, 'col', [(i, i ^ 2 * level) for i in range(cols)])  14.4 us
    ppermute x9, waiting for transfers between devices, to_deep(): return lax.ppermute(x, 'col', [(i, i ^ 2 * level) for i in range(cols)])  9.07 us
    ppermute x6, starting transfers between devices, over_step(): return lax.ppermute(x, ('row', 'col'), pairs)  8.42 us
    pallas_call x1, Pallas kernels, modes_of(): pl.pallas_call(functools.partial(modes_kernel, len(mine)), out_shape=jax....  6.07 us
    pallas_call x1, Pallas kernels, factor_of(): pl.pallas_call(functools.partial(factor_kernel, len(mine)), out_shape=jax...  5.31 us
    ppermute x6, waiting for transfers between devices, over_step(): return lax.ppermute(x, ('row', 'col'), pairs)  5.3 us
    unnamed x16, local copies, waits for them, and re-layouts  3.97 us
    ppermute x3, starting transfers between devices, to_row(): return lax.ppermute(x, 'row', [(i, i ^ peer) for i in range(rows)])  3.55 us
  transfers between devices with their start and end apart: 25, of which 10 were waited for; matrix products, arithmetic and copies ran while one was open for 5% of the time, Pallas kernels for 13%

profile of v2, /device:TPU:0, one launch (start us, length us, event | category | flops | bytes accessed | tf_op | source)
XLA Modules:
  0.0 69.2 jit_solution(12706880460866297440)
XLA Ops:
  0.7 1.6 %copy-done = f32[1024,512]{1,0:T(8,128)S(1)} copy-done((f32[1024,512]{1,0:T(8,128)S(1)}, f32[1024,512]{1,0:T(8,128)}, u32[]{:S(2)}) %copy-start) | copy-done | bytes 2097176
  4.7 2.2 %shard_map.77 = (bf16[32,1024]{1,0:T(8,128)(2,1)S(1)}, bf16[4,128,256]{2,1,0:T(8,128)(2,1)S(1)}, bf16[4,128,256]{2,1,0:T(8,128)(2,1)S(1)}) custom-call(s32[3]{0:T(128)S(1)} %pad_add_fusion.here_ref, s32[1,256]{1,0:T(1,128)S(1)} %bitcast.48, f32[1024,512]{1,0:T(8,128)S(1)} %copy-done, f32[16,1024]{1,0:T(8,128)S(1)} %bitcast.46, f32[16,1024]{1,0:T(8,128)S(1)} %bitcast.47), custom_call_target="tpu_custom_call" | custom-call | flops 268435456 | bytes 2097152 | tf_op jit(solution)/shard_map/pallas_call | solution.py:96
  8.5 2.9 %collective-permute-start.1 = (bf16[32,1024]{1,0:T(8,128)(2,1)S(1)}, bf16[32,1024]{1,0:T(8,128)(2,1)S(1)}, u32[]{:S(2)}, u32[]{:S(2)}) collective-permute-start(bf16[32,1024]{1,0:T(8,128)(2,1)S(1)} %get-tuple-element.17), channel_id=1, source_target_pairs={{0,2},{1,3},{2,0},{3,1},{4,6},{5,7},{6,4},{7,5},{8,10},{9,11},{10,... | collective-permute-start | bytes 196616 | tf_op jit(solution)/shard_map/ppermute | solution.py:248
  11.5 2.6 %collective-permute-start.2 = (bf16[32,1024]{1,0:T(8,128)(2,1)S(1)}, bf16[32,1024]{1,0:T(8,128)(2,1)S(1)}, u32[]{:S(2)}, u32[]{:S(2)}) collective-permute-start(bf16[32,1024]{1,0:T(8,128)(2,1)S(1)} %get-tuple-element.17), channel_id=1, source_target_pairs={{0,4},{1,5},{2,6},{3,7},{4,0},{5,1},{6,2},{7,3},{8,12},{9,13},{10,... | collective-permute-start | bytes 196616 | tf_op jit(solution)/shard_map/ppermute | solution.py:248
  14.2 4.9 %collective-permute-done.2 = bf16[32,1024]{1,0:T(8,128)(2,1)S(1)} collective-permute-done((bf16[32,1024]{1,0:T(8,128)(2,1)S(1)}, bf16[32,1024]{1,0:T(8,128)(2,1)S(1)}, u32[]{:S(2)}, u32[]{:S(2)}) %collective-permute-start.2) | collective-permute-done | bytes 65568 | tf_op jit(solution)/shard_map/ppermute | solution.py:248
  20.3 1.6 %collective-permute-start.5 = (bf16[1,128,1024]{2,1,0:T(8,128)(2,1)S(1)}, bf16[1,128,1024]{2,1,0:T(8,128)(2,1)S(1)}, u32[]{:S(2)}, u32[]{:S(2)}) collective-permute-start(bf16[1,128,1024]{2,1,0:T(8,128)(2,1)S(1)} %bitcast.39), channel_id=1, source_target_pairs={{0,8},{1,17},{2,10},{3,19},{4,12},{5,21},{6,14},{7,23},{8,0},{9,25... | collective-permute-start | bytes 786440 | tf_op jit(solution)/shard_map/ppermute | solution.py:261
  22.9 1.7 %collective-permute-start.15 = (bf16[128,256]{1,0:T(8,128)(2,1)S(1)}, bf16[128,256]{1,0:T(8,128)(2,1)S(1)}, u32[]{:S(2)}, u32[]{:S(2)}) collective-permute-start(bf16[128,256]{1,0:T(8,128)(2,1)S(1)} %get-tuple-element.34), channel_id=1, source_target_pairs={{0,4},{1,5},{2,6},{3,7},{4,0},{5,1},{6,2},{7,3},{8,12},{9,13},{10,... | collective-permute-start | bytes 196616 | tf_op jit(solution)/shard_map/ppermute | solution.py:248
  24.6 1.8 %collective-permute-start.16 = (bf16[128,256]{1,0:T(8,128)(2,1)S(1)}, bf16[128,256]{1,0:T(8,128)(2,1)S(1)}, u32[]{:S(2)}, u32[]{:S(2)}) collective-permute-start(bf16[128,256]{1,0:T(8,128)(2,1)S(1)} %get-tuple-element.33), channel_id=1, source_target_pairs={{0,6},{1,7},{2,4},{3,5},{4,2},{5,3},{6,0},{7,1},{8,14},{9,15},{10,... | collective-permute-start | bytes 196616 | tf_op jit(solution)/shard_map/ppermute | solution.py:248
  26.8 1.6 %collective-permute-start.6 = (bf16[2,128,1024]{2,1,0:T(8,128)(2,1)S(1)}, bf16[2,128,1024]{2,1,0:T(8,128)(2,1)S(1)}, u32[]{:S(2)}, u32[]{:S(2)}) collective-permute-start(bf16[2,128,1024]{2,1,0:T(8,128)(2,1)S(1)} %pad_maximum_fusion.1), channel_id=1, source_target_pairs={{0,16},{1,9},{2,18},{3,11},{4,20},{5,13},{6,22},{7,15},{8,24},{9,1... | collective-permute-start | bytes 1572872 | tf_op jit(solution)/shard_map/ppermute | solution.py:261
  29.6 1.8 %collective-permute-done.15 = bf16[128,256]{1,0:T(8,128)(2,1)S(1)} collective-permute-done((bf16[128,256]{1,0:T(8,128)(2,1)S(1)}, bf16[128,256]{1,0:T(8,128)(2,1)S(1)}, u32[]{:S(2)}, u32[]{:S(2)}) %collective-permute-start.15) | collective-permute-done | bytes 65568 | tf_op jit(solution)/shard_map/ppermute | solution.py:248
  31.4 1.6 %collective-permute-start.17 = (bf16[128,256]{1,0:T(8,128)(2,1)S(1)}, bf16[128,256]{1,0:T(8,128)(2,1)S(1)}, u32[]{:S(2)}, u32[]{:S(2)}) collective-permute-start(bf16[128,256]{1,0:T(8,128)(2,1)S(1)} %add_add_fusion), channel_id=1, source_target_pairs={{0,2},{1,3},{2,0},{3,1},{4,6},{5,7},{6,4},{7,5},{8,10},{9,11},{10,... | collective-permute-start | bytes 196616 | tf_op jit(solution)/shard_map/ppermute | solution.py:248
  32.9 1.2 %collective-permute-start.18 = (bf16[128,256]{1,0:T(8,128)(2,1)S(1)}, bf16[128,256]{1,0:T(8,128)(2,1)S(1)}, u32[]{:S(2)}, u32[]{:S(2)}) collective-permute-start(bf16[128,256]{1,0:T(8,128)(2,1)S(1)} %add_add_fusion), channel_id=1, source_target_pairs={{0,4},{1,5},{2,6},{3,7},{4,0},{5,1},{6,2},{7,3},{8,12},{9,13},{10,... | collective-permute-start | bytes 196616 | tf_op jit(solution)/shard_map/ppermute | solution.py:248
  34.2 1.6 %collective-permute-start.19 = (bf16[128,256]{1,0:T(8,128)(2,1)S(1)}, bf16[128,256]{1,0:T(8,128)(2,1)S(1)}, u32[]{:S(2)}, u32[]{:S(2)}) collective-permute-start(bf16[128,256]{1,0:T(8,128)(2,1)S(1)} %add_add_fusion), channel_id=1, source_target_pairs={{0,6},{1,7},{2,4},{3,5},{4,2},{5,3},{6,0},{7,1},{8,14},{9,15},{10,... | collective-permute-start | bytes 196616 | tf_op jit(solution)/shard_map/ppermute | solution.py:248
  35.8 1.6 %collective-permute-done.9 = bf16[2,256,128]{2,1,0:T(8,128)(2,1)S(1)} collective-permute-done((bf16[2,256,128]{2,1,0:T(8,128)(2,1)S(1)}, bf16[2,256,128]{2,1,0:T(8,128)(2,1)S(1)}, u32[]{:S(2)}, u32[]{:S(2)}) %collective-permute-start.9) | collective-permute-done | bytes 131104 | tf_op jit(solution)/shard_map/ppermute | solution.py:261
  38.0 1.6 %collective-permute-start.10 = (bf16[1,256,128]{2,1,0:T(8,128)(2,1)S(1)}, bf16[1,256,128]{2,1,0:T(8,128)(2,1)S(1)}, u32[]{:S(2)}, u32[]{:S(2)}) collective-permute-start(bf16[1,256,128]{2,1,0:T(8,128)(2,1)S(1)} %slice.46), channel_id=1, source_target_pairs={{0,8},{1,17},{2,10},{3,19},{4,12},{5,21},{6,14},{7,23},{8,0},{9,25... | collective-permute-start | bytes 196616 | tf_op jit(solution)/shard_map/ppermute | solution.py:261
  40.8 1.5 %collective-permute-done.10 = bf16[1,256,128]{2,1,0:T(8,128)(2,1)S(1)} collective-permute-done((bf16[1,256,128]{2,1,0:T(8,128)(2,1)S(1)}, bf16[1,256,128]{2,1,0:T(8,128)(2,1)S(1)}, u32[]{:S(2)}, u32[]{:S(2)}) %collective-permute-start.10) | collective-permute-done | bytes 65568 | tf_op jit(solution)/shard_map/ppermute | solution.py:261
  42.4 1.6 %collective-permute-start.20 = (bf16[1,4,128,256]{3,2,1,0:T(8,128)(2,1)S(1)}, bf16[1,4,128,256]{3,2,1,0:T(8,128)(2,1)S(1)}, u32[]{:S(2)}, u32[]{:S(2)}) collective-permute-start(bf16[1,4,128,256]{3,2,1,0:T(8,128)(2,1)S(1)} %maximum_bitcast_fusion.refs_0_), channel_id=1, source_target_pairs={{0,8},{1,17},{2,10},{3,19},{4,12},{5,21},{6,14},{7,23},{8,0},{9,25... | collective-permute-start | bytes 786440 | tf_op jit(solution)/shard_map/ppermute | solution.py:261
  43.9 5.3 %shard_map.78.factor_ref = f32[256,256]{1,0:T(8,128)S(1)} custom-call(s32[1,256]{1,0:T(1,128)S(1)} %fusion.3.place_ref, bf16[1,128,1024]{2,1,0:T(8,128)(2,1)S(1)} %bitcast.42, bf16[1,128,1024]{2,1,0:T(8,128)(2,1)S(1)} %collective-permute-done.5.refs_1_, bf16[2,128,1024]{2,1,0:T(8,128)(2,1)S(1)} %collective-permute-done.6.refs_2_, ...), custom_call_target="tpu_custom_call" | custom-call | flops 3758096384 | bytes 2621440 | tf_op jit(solution)/shard_map/pallas_call | solution.py:153
  49.3 1.6 %collective-permute-start.21 = (bf16[2,4,128,256]{3,2,1,0:T(8,128)(2,1)S(1)}, bf16[2,4,128,256]{3,2,1,0:T(8,128)(2,1)S(1)}, u32[]{:S(2)}, u32[]{:S(2)}) collective-permute-start(bf16[2,4,128,256]{3,2,1,0:T(8,128)(2,1)S(1)} %pad_maximum_fusion.3), channel_id=1, source_target_pairs={{0,16},{1,9},{2,18},{3,11},{4,20},{5,13},{6,22},{7,15},{8,24},{9,1... | collective-permute-start | bytes 1572872 | tf_op jit(solution)/shard_map/ppermute | solution.py:261
  53.0 1.9 %collective-permute-start.13 = (bf16[256,128]{1,0:T(8,128)(2,1)S(1)}, bf16[256,128]{1,0:T(8,128)(2,1)S(1)}, u32[]{:S(2)}, u32[]{:S(2)}) collective-permute-start(bf16[256,128]{1,0:T(8,128)(2,1)S(1)} %get-tuple-element.37), channel_id=1, source_target_pairs={{0,24},{8,16},{16,8},{24,0},{1,25},{9,17},{17,9},{25,1},{2,26},{10... | collective-permute-start | bytes 196616 | tf_op jit(solution)/shard_map/ppermute | solution.py:251
  54.9 3.5 %shard_map.79 = (bf16[256,4096]{1,0:T(8,128)(2,1)S(1)}, bf16[1024,256]{1,0:T(8,128)(2,1)S(1)}) custom-call(s32[3]{0:T(128)S(1)} %pad_add_fusion.here_ref, s32[32]{0:T(128)S(1)} %copy-done.4, bf16[1024,4096]{1,0:T(8,128)(2,1)S(1)} %bitcast.38, bf16[1,128,1024]{2,1,0:T(8,128)(2,1)S(1)} %bitcast.43, bf16[1,128,1024]{2,1,0:T(8,128)(2,1)S(1)} %collective-permute-done.5.refs_1_, ...), custom_call_target="tpu_custom_call" | custom-call | flops 2147483648 | bytes 8388608 | tf_op jit(solution)/shard_map/pallas_call | solution.py:185
  58.5 2.0 %collective-permute-done.21.refs_2_ = bf16[2,4,128,256]{3,2,1,0:T(8,128)(2,1)S(1)} collective-permute-done((bf16[2,4,128,256]{3,2,1,0:T(8,128)(2,1)S(1)}, bf16[2,4,128,256]{3,2,1,0:T(8,128)(2,1)S(1)}, u32[]{:S(2)}, u32[]{:S(2)}) %collective-permute-start.21) | collective-permute-done | bytes 524320 | tf_op jit(solution)/shard_map/ppermute | solution.py:261
  61.3 1.8 %convolution_subtract_fusion = f32[1024,512]{1,0:T(8,128)} fusion(f32[1024,512]{1,0:T(8,128)S(1)} %copy-done.1, bf16[256,512]{1,0:T(8,128)(2,1)S(1)} %constant_dynamic-update-slice_fusion, bf16[128,1024]{1,0:T(8,128)(2,1)S(1)} %bitcast.45, bf16[128,1024]{1,0:T(8,128)(2,1)S(1)} %pad_maximum_fusion.6), kind=kOutput, calls=%fused_computation | convolution fusion | flops 270008320 | bytes 4980736 | tf_op jit(solution)/shard_map/dot_general | solution.py:318
  63.1 6.1 %shard_map.80 = bf16[1024,256]{1,0:T(8,128)(2,1)} custom-call(s32[3]{0:T(128)S(1)} %pad_add_fusion.here_ref, s32[32]{0:T(128)S(1)} %copy-done.4, bf16[1024,4096]{1,0:T(8,128)(2,1)S(1)} %bitcast.38, bf16[256,4096]{1,0:T(8,128)(2,1)S(1)} %get-tuple-element.23.vec_ref, bf16[1024,256]{1,0:T(8,128)(2,1)S(1)} %get-tuple-element.24.spread_ref, ...), custom_call_target="tpu_custom_call" | custom-call | flops 2684354560 | bytes 8388608 | tf_op jit(solution)/shard_map/pallas_call | solution.py:222
  (69 shorter events, 12.8 us)
Async XLA Ops:
  8.5 5.6 %collective-permute-start.1 = (bf16[32,1024]{1,0:T(8,128)(2,1)S(1)}, bf16[32,1024]{1,0:T(8,128)(2,1)S(1)}, u32[]{:S(2)}, u32[]{:S(2)}) collective-permute-start(bf16[32,1024]{1,0:T(8,128)(2,1)S(1)} %get-tuple-element.17), channel_id=1, source_target_pairs={{0,2},{1,3},{2,0},{3,1},{4,6},{5,7},{6,4},{7,5},{8,10},{9,11},{10,... | collective-permute-start | bytes 196616 | tf_op jit(solution)/shard_map/ppermute | solution.py:248
  11.5 7.5 %collective-permute-start.2 = (bf16[32,1024]{1,0:T(8,128)(2,1)S(1)}, bf16[32,1024]{1,0:T(8,128)(2,1)S(1)}, u32[]{:S(2)}, u32[]{:S(2)}) collective-permute-start(bf16[32,1024]{1,0:T(8,128)(2,1)S(1)} %get-tuple-element.17), channel_id=1, source_target_pairs={{0,4},{1,5},{2,6},{3,7},{4,0},{5,1},{6,2},{7,3},{8,12},{9,13},{10,... | collective-permute-start | bytes 196616 | tf_op jit(solution)/shard_map/ppermute | solution.py:248
  14.1 6.2 %collective-permute-start.3 = (bf16[32,1024]{1,0:T(8,128)(2,1)S(1)}, bf16[32,1024]{1,0:T(8,128)(2,1)S(1)}, u32[]{:S(2)}, u32[]{:S(2)}) collective-permute-start(bf16[32,1024]{1,0:T(8,128)(2,1)S(1)} %get-tuple-element.17), channel_id=1, source_target_pairs={{0,6},{1,7},{2,4},{3,5},{4,2},{5,3},{6,0},{7,1},{8,14},{9,15},{10,... | collective-permute-start | bytes 196616 | tf_op jit(solution)/shard_map/ppermute | solution.py:248
  20.3 6.4 %collective-permute-start.5 = (bf16[1,128,1024]{2,1,0:T(8,128)(2,1)S(1)}, bf16[1,128,1024]{2,1,0:T(8,128)(2,1)S(1)}, u32[]{:S(2)}, u32[]{:S(2)}) collective-permute-start(bf16[1,128,1024]{2,1,0:T(8,128)(2,1)S(1)} %bitcast.39), channel_id=1, source_target_pairs={{0,8},{1,17},{2,10},{3,19},{4,12},{5,21},{6,14},{7,23},{8,0},{9,25... | collective-permute-start | bytes 786440 | tf_op jit(solution)/shard_map/ppermute | solution.py:261
  21.9 6.5 %collective-permute-start.4 = (bf16[1,128,1024]{2,1,0:T(8,128)(2,1)S(1)}, bf16[1,128,1024]{2,1,0:T(8,128)(2,1)S(1)}, u32[]{:S(2)}, u32[]{:S(2)}) collective-permute-start(bf16[1,128,1024]{2,1,0:T(8,128)(2,1)S(1)} %bitcast.40), channel_id=1, source_target_pairs={{0,1},{1,0},{2,3},{3,2},{4,5},{5,4},{6,7},{7,6},{8,9},{9,8},{10,11... | collective-permute-start | bytes 786440 | tf_op jit(solution)/shard_map/ppermute | solution.py:245
  22.0 7.6 %collective-permute-start.14 = (bf16[128,256]{1,0:T(8,128)(2,1)S(1)}, bf16[128,256]{1,0:T(8,128)(2,1)S(1)}, u32[]{:S(2)}, u32[]{:S(2)}) collective-permute-start(bf16[128,256]{1,0:T(8,128)(2,1)S(1)} %get-tuple-element.32), channel_id=1, source_target_pairs={{0,2},{1,3},{2,0},{3,1},{4,6},{5,7},{6,4},{7,5},{8,10},{9,11},{10,... | collective-permute-start | bytes 196616 | tf_op jit(solution)/shard_map/ppermute | solution.py:248
  22.9 8.4 %collective-permute-start.15 = (bf16[128,256]{1,0:T(8,128)(2,1)S(1)}, bf16[128,256]{1,0:T(8,128)(2,1)S(1)}, u32[]{:S(2)}, u32[]{:S(2)}) collective-permute-start(bf16[128,256]{1,0:T(8,128)(2,1)S(1)} %get-tuple-element.34), channel_id=1, source_target_pairs={{0,4},{1,5},{2,6},{3,7},{4,0},{5,1},{6,2},{7,3},{8,12},{9,13},{10,... | collective-permute-start | bytes 196616 | tf_op jit(solution)/shard_map/ppermute | solution.py:248
  24.6 6.7 %collective-permute-start.16 = (bf16[128,256]{1,0:T(8,128)(2,1)S(1)}, bf16[128,256]{1,0:T(8,128)(2,1)S(1)}, u32[]{:S(2)}, u32[]{:S(2)}) collective-permute-start(bf16[128,256]{1,0:T(8,128)(2,1)S(1)} %get-tuple-element.33), channel_id=1, source_target_pairs={{0,6},{1,7},{2,4},{3,5},{4,2},{5,3},{6,0},{7,1},{8,14},{9,15},{10,... | collective-permute-start | bytes 196616 | tf_op jit(solution)/shard_map/ppermute | solution.py:248
  26.8 10.7 %collective-permute-start.6 = (bf16[2,128,1024]{2,1,0:T(8,128)(2,1)S(1)}, bf16[2,128,1024]{2,1,0:T(8,128)(2,1)S(1)}, u32[]{:S(2)}, u32[]{:S(2)}) collective-permute-start(bf16[2,128,1024]{2,1,0:T(8,128)(2,1)S(1)} %pad_maximum_fusion.1), channel_id=1, source_target_pairs={{0,16},{1,9},{2,18},{3,11},{4,20},{5,13},{6,22},{7,15},{8,24},{9,1... | collective-permute-start | bytes 1572872 | tf_op jit(solution)/shard_map/ppermute | solution.py:261
  29.0 8.4 %collective-permute-start.9 = (bf16[2,256,128]{2,1,0:T(8,128)(2,1)S(1)}, bf16[2,256,128]{2,1,0:T(8,128)(2,1)S(1)}, u32[]{:S(2)}, u32[]{:S(2)}) collective-permute-start(bf16[2,256,128]{2,1,0:T(8,128)(2,1)S(1)} %slice.45), channel_id=1, source_target_pairs={{0,16},{1,9},{2,18},{3,11},{4,20},{5,13},{6,22},{7,15},{8,24},{9,1... | collective-permute-start | bytes 393224 | tf_op jit(solution)/shard_map/ppermute | solution.py:261
  31.4 6.6 %collective-permute-start.17 = (bf16[128,256]{1,0:T(8,128)(2,1)S(1)}, bf16[128,256]{1,0:T(8,128)(2,1)S(1)}, u32[]{:S(2)}, u32[]{:S(2)}) collective-permute-start(bf16[128,256]{1,0:T(8,128)(2,1)S(1)} %add_add_fusion), channel_id=1, source_target_pairs={{0,2},{1,3},{2,0},{3,1},{4,6},{5,7},{6,4},{7,5},{8,10},{9,11},{10,... | collective-permute-start | bytes 196616 | tf_op jit(solution)/shard_map/ppermute | solution.py:248
  32.9 7.8 %collective-permute-start.18 = (bf16[128,256]{1,0:T(8,128)(2,1)S(1)}, bf16[128,256]{1,0:T(8,128)(2,1)S(1)}, u32[]{:S(2)}, u32[]{:S(2)}) collective-permute-start(bf16[128,256]{1,0:T(8,128)(2,1)S(1)} %add_add_fusion), channel_id=1, source_target_pairs={{0,4},{1,5},{2,6},{3,7},{4,0},{5,1},{6,2},{7,3},{8,12},{9,13},{10,... | collective-permute-start | bytes 196616 | tf_op jit(solution)/shard_map/ppermute | solution.py:248
  34.2 6.5 %collective-permute-start.19 = (bf16[128,256]{1,0:T(8,128)(2,1)S(1)}, bf16[128,256]{1,0:T(8,128)(2,1)S(1)}, u32[]{:S(2)}, u32[]{:S(2)}) collective-permute-start(bf16[128,256]{1,0:T(8,128)(2,1)S(1)} %add_add_fusion), channel_id=1, source_target_pairs={{0,6},{1,7},{2,4},{3,5},{4,2},{5,3},{6,0},{7,1},{8,14},{9,15},{10,... | collective-permute-start | bytes 196616 | tf_op jit(solution)/shard_map/ppermute | solution.py:248
  37.4 5.0 %collective-permute-start.7 = (bf16[1,128,1024]{2,1,0:T(8,128)(2,1)S(1)}, bf16[1,128,1024]{2,1,0:T(8,128)(2,1)S(1)}, u32[]{:S(2)}, u32[]{:S(2)}) collective-permute-start(bf16[1,128,1024]{2,1,0:T(8,128)(2,1)S(1)} %collective-permute-done.5.refs_1_), channel_id=1, source_target_pairs={{0,1},{1,0},{2,3},{3,2},{4,5},{5,4},{6,7},{7,6},{8,9},{9,8},{10,11... | collective-permute-start | bytes 786440 | tf_op jit(solution)/shard_map/ppermute | solution.py:245
  37.4 5.0 %collective-permute-start.8 = (bf16[2,128,1024]{2,1,0:T(8,128)(2,1)S(1)}, bf16[2,128,1024]{2,1,0:T(8,128)(2,1)S(1)}, u32[]{:S(2)}, u32[]{:S(2)}) collective-permute-start(bf16[2,128,1024]{2,1,0:T(8,128)(2,1)S(1)} %collective-permute-done.6.refs_2_), channel_id=1, source_target_pairs={{0,1},{1,0},{2,3},{3,2},{4,5},{5,4},{6,7},{7,6},{8,9},{9,8},{10,11... | collective-permute-start | bytes 1572872 | tf_op jit(solution)/shard_map/ppermute | solution.py:245
  38.0 4.3 %collective-permute-start.10 = (bf16[1,256,128]{2,1,0:T(8,128)(2,1)S(1)}, bf16[1,256,128]{2,1,0:T(8,128)(2,1)S(1)}, u32[]{:S(2)}, u32[]{:S(2)}) collective-permute-start(bf16[1,256,128]{2,1,0:T(8,128)(2,1)S(1)} %slice.46), channel_id=1, source_target_pairs={{0,8},{1,17},{2,10},{3,19},{4,12},{5,21},{6,14},{7,23},{8,0},{9,25... | collective-permute-start | bytes 196616 | tf_op jit(solution)/shard_map/ppermute | solution.py:261
  40.8 22.3 %collective-permute-start.22 = (bf16[1,4,128,256]{3,2,1,0:T(8,128)(2,1)S(1)}, bf16[1,4,128,256]{3,2,1,0:T(8,128)(2,1)S(1)}, u32[]{:S(2)}, u32[]{:S(2)}) collective-permute-start(bf16[1,4,128,256]{3,2,1,0:T(8,128)(2,1)S(1)} %maximum_bitcast_fusion.refs_0_), channel_id=1, source_target_pairs={{0,1},{1,0},{2,3},{3,2},{4,5},{5,4},{6,7},{7,6},{8,9},{9,8},{10,11... | collective-permute-start | bytes 786440 | tf_op jit(solution)/shard_map/ppermute | solution.py:245
  42.4 6.9 %collective-permute-start.20 = (bf16[1,4,128,256]{3,2,1,0:T(8,128)(2,1)S(1)}, bf16[1,4,128,256]{3,2,1,0:T(8,128)(2,1)S(1)}, u32[]{:S(2)}, u32[]{:S(2)}) collective-permute-start(bf16[1,4,128,256]{3,2,1,0:T(8,128)(2,1)S(1)} %maximum_bitcast_fusion.refs_0_), channel_id=1, source_target_pairs={{0,8},{1,17},{2,10},{3,19},{4,12},{5,21},{6,14},{7,23},{8,0},{9,25... | collective-permute-start | bytes 786440 | tf_op jit(solution)/shard_map/ppermute | solution.py:261
  49.3 11.1 %collective-permute-start.21 = (bf16[2,4,128,256]{3,2,1,0:T(8,128)(2,1)S(1)}, bf16[2,4,128,256]{3,2,1,0:T(8,128)(2,1)S(1)}, u32[]{:S(2)}, u32[]{:S(2)}) collective-permute-start(bf16[2,4,128,256]{3,2,1,0:T(8,128)(2,1)S(1)} %pad_maximum_fusion.3), channel_id=1, source_target_pairs={{0,16},{1,9},{2,18},{3,11},{4,20},{5,13},{6,22},{7,15},{8,24},{9,1... | collective-permute-start | bytes 1572872 | tf_op jit(solution)/shard_map/ppermute | solution.py:261
  51.4 7.1 %collective-permute-start.11 = (bf16[256,128]{1,0:T(8,128)(2,1)S(1)}, bf16[256,128]{1,0:T(8,128)(2,1)S(1)}, u32[]{:S(2)}, u32[]{:S(2)}) collective-permute-start(bf16[256,128]{1,0:T(8,128)(2,1)S(1)} %get-tuple-element.37), channel_id=1, source_target_pairs={{0,8},{8,0},{16,24},{24,16},{1,9},{9,1},{17,25},{25,17},{2,10},{10... | collective-permute-start | bytes 196616 | tf_op jit(solution)/shard_map/ppermute | solution.py:251
  52.5 8.7 %collective-permute-start.12 = (bf16[256,128]{1,0:T(8,128)(2,1)S(1)}, bf16[256,128]{1,0:T(8,128)(2,1)S(1)}, u32[]{:S(2)}, u32[]{:S(2)}) collective-permute-start(bf16[256,128]{1,0:T(8,128)(2,1)S(1)} %get-tuple-element.37), channel_id=1, source_target_pairs={{0,16},{8,24},{16,0},{24,8},{1,17},{9,25},{17,1},{25,9},{2,18},{10... | collective-permute-start | bytes 196616 | tf_op jit(solution)/shard_map/ppermute | solution.py:251
  53.0 8.2 %collective-permute-start.13 = (bf16[256,128]{1,0:T(8,128)(2,1)S(1)}, bf16[256,128]{1,0:T(8,128)(2,1)S(1)}, u32[]{:S(2)}, u32[]{:S(2)}) collective-permute-start(bf16[256,128]{1,0:T(8,128)(2,1)S(1)} %get-tuple-element.37), channel_id=1, source_target_pairs={{0,24},{8,16},{16,8},{24,0},{1,25},{9,17},{17,9},{25,1},{2,26},{10... | collective-permute-start | bytes 196616 | tf_op jit(solution)/shard_map/ppermute | solution.py:251
  60.5 2.7 %collective-permute-start.24 = (bf16[2,4,128,256]{3,2,1,0:T(8,128)(2,1)S(1)}, bf16[2,4,128,256]{3,2,1,0:T(8,128)(2,1)S(1)}, u32[]{:S(2)}, u32[]{:S(2)}) collective-permute-start(bf16[2,4,128,256]{3,2,1,0:T(8,128)(2,1)S(1)} %collective-permute-done.21.refs_2_), channel_id=1, source_target_pairs={{0,1},{1,0},{2,3},{3,2},{4,5},{5,4},{6,7},{7,6},{8,9},{9,8},{10,11... | collective-permute-start | bytes 1572872 | tf_op jit(solution)/shard_map/ppermute | solution.py:245
  61.2 1.9 %collective-permute-start.23 = (bf16[1,4,128,256]{3,2,1,0:T(8,128)(2,1)S(1)}, bf16[1,4,128,256]{3,2,1,0:T(8,128)(2,1)S(1)}, u32[]{:S(2)}, u32[]{:S(2)}) collective-permute-start(bf16[1,4,128,256]{3,2,1,0:T(8,128)(2,1)S(1)} %collective-permute-done.20.refs_1_), channel_id=1, source_target_pairs={{0,1},{1,0},{2,3},{3,2},{4,5},{5,4},{6,7},{7,6},{8,9},{9,8},{10,11... | collective-permute-start | bytes 786440 | tf_op jit(solution)/shard_map/ppermute | solution.py:245
  (9 other events, 67.0 us)

commit v3 on v2

--- a/solution.py
+++ b/solution.py
@@ -49,67 +49,36 @@
         yield mine[number], sib[other], (number, other)
 
 
-def prepare_kernel(
-    here_ref, select_ref, eig_ref, two_ref, one_ref, vec_ref, keep_ref, give_ref, buffer, picked, chosen, house, sems
-):
+def prepare_kernel(here_ref, select_ref, eig_ref, keep_ref, give_ref, picked):
     deep_at, core_at = here_ref[1], here_ref[2]
-    steps, chunk, wide = buffer.shape
+    local, wide = eig_ref.shape
     deep, piece, width = keep_ref.shape
-    share = two_ref.shape[0]
-    small = [
-        pltpu.make_async_copy(select_ref, chosen, sems.at[steps]),
-        pltpu.make_async_copy(two_ref, house.at[0], sems.at[steps + 1]),
-        pltpu.make_async_copy(one_ref, house.at[1], sems.at[steps + 2]),
-    ]
-    for copy in small:
-        copy.start()
-
-    def fetch(step):
-        return pltpu.make_async_copy(eig_ref.at[pl.ds(step * chunk, chunk)], buffer.at[step], sems.at[step])
-
-    for step in range(steps):
-        fetch(step).start()
-    for copy in small:
-        copy.wait()
-    vec_ref[:share, :] = house[0].astype(BF16)
-    vec_ref[share:, :] = house[1].astype(BF16)
     ids = lax.broadcasted_iota(jnp.int32, (wide, width), 0) + (deep_at * 2 + core_at) * wide
-    chooser = jnp.where(ids == chosen[...], 1.0, 0.0).astype(BF16)
-    for step in range(steps):
-        fetch(step).wait()
-        picked[step * chunk : (step + 1) * chunk, :] = jnp.dot(
-            buffer[step].astype(BF16), chooser, preferred_element_type=F32
-        ).astype(BF16)
+    chooser = jnp.where(ids == select_ref[...], 1.0, 0.0).astype(BF16)
+    picked[...] = jnp.dot(eig_ref[...].astype(BF16), chooser, preferred_element_type=F32).astype(BF16)
     for level in range(deep):
         for out, core in ((keep_ref, core_at), (give_ref, 1 - core_at)):
             row = ((deep_at ^ level) * 2 + core) * piece
             out[level] = picked[pl.ds(pl.multiple_of(row, piece), piece), :]
 
 
-def prepare(here, select, eigvecs, two, one, cols):
+def prepare(here, select, eigvecs, cols):
     local, wide = eigvecs.shape
     width = select.shape[0]
-    share = two.shape[0]
-    deep, piece, steps = cols // 2, local // cols, 4
+    deep, piece = cols // 2, local // cols
     in_vmem = pl.BlockSpec(memory_space=pltpu.VMEM)
     some = jax.ShapeDtypeStruct((deep, piece, width), BF16)
     return pl.pallas_call(
         prepare_kernel,
-        out_shape=(jax.ShapeDtypeStruct((2 * share, local), BF16), some, some),
-        in_specs=[pl.BlockSpec(memory_space=pltpu.SMEM)] + [pl.BlockSpec(memory_space=pltpu.HBM)] * 4,
-        out_specs=(in_vmem,) * 3,
-        scratch_shapes=[
-            pltpu.VMEM((steps, local // steps, wide), F32),
-            pltpu.VMEM((local, width), BF16),
-            pltpu.VMEM((1, width), jnp.int32),
-            pltpu.VMEM((2, share, local), F32),
-            pltpu.SemaphoreType.DMA((steps + 3,)),
-        ],
+        out_shape=(some, some),
+        in_specs=[pl.BlockSpec(memory_space=pltpu.SMEM), in_vmem, in_vmem],
+        out_specs=(in_vmem,) * 2,
+        scratch_shapes=[pltpu.VMEM((local, width), BF16)],
         compiler_params=pltpu.CompilerParams(vmem_limit_bytes=16 << 20),
         cost_estimate=pl.CostEstimate(
             flops=2 * local * wide * width, bytes_accessed=4 * local * wide, transcendentals=0
         ),
-    )(here, select[None, :], eigvecs, two, one)
+    )(here, select[None, :], eigvecs)
 
 
 def moved(order, x):
@@ -232,6 +201,102 @@
     )(here, tile_map, ritz_basis, vec, spreads, factor, *mine, *sib)
 
 
+def sort_kernel(count, here_ref, map_ref, ritz_ref, *refs):
+    mine, sib = refs[:count], refs[count : 2 * count]
+    ritz_out, vec, out_ref = refs[2 * count :]
+    _, half, local = mine[0].shape
+    deep = local // TILE // 2
+    blocks = list(pairs_of(mine, sib))
+    rows = len(blocks)
+    for one, other, numbers in blocks:
+        row = here_ref[0] ^ jnp.where(here_ref[2] == 0, *numbers)
+        for level in range(deep):
+            for side in (0, 1):
+                core = here_ref[2] ^ side
+                tile = (here_ref[1] ^ level) * 2 + core
+                place = ((side * rows + numbers[side]) * deep + level) * TILE
+                to = slice(place, place + TILE)
+                goal = pl.multiple_of(map_ref[row * 2 * deep + tile] * TILE, TILE)
+                at = pl.multiple_of(tile * TILE, TILE)
+                ritz_out[:, to] = ritz_ref[:, pl.ds(goal, TILE)]
+                vec[:half, to] = one[:, pl.ds(at, TILE)]
+                vec[half:, to] = other[:, pl.ds(at, TILE)]
+    out_ref[...] = lax.dot_general(
+        ritz_out[...], vec[...], (((1,), (1,)), ((), ())), preferred_element_type=F32
+    ).astype(BF16)
+
+
+def sort(here, tile_map, ritz_basis, mine, sib):
+    dofs, order = ritz_basis.shape
+    size = 2 * mine[0].shape[1]
+    in_vmem = pl.BlockSpec(memory_space=pltpu.VMEM)
+    in_smem = pl.BlockSpec(memory_space=pltpu.SMEM)
+    return pl.pallas_call(
+        functools.partial(sort_kernel, len(mine)),
+        out_shape=(
+            jax.ShapeDtypeStruct((dofs, order), BF16),
+            jax.ShapeDtypeStruct((size, order), BF16),
+            jax.ShapeDtypeStruct((dofs, size), BF16),
+        ),
+        in_specs=[in_smem, in_smem] + [in_vmem] * (1 + 2 * len(mine)),
+        out_specs=(in_vmem,) * 3,
+        compiler_params=pltpu.CompilerParams(vmem_limit_bytes=24 << 20),
+        cost_estimate=pl.CostEstimate(
+            flops=2 * order * size * dofs, bytes_accessed=4 * dofs * order, transcendentals=0
+        ),
+    )(here, tile_map, ritz_basis, *mine, *sib)
+
+
+def blocks_in(parts):
+    return jnp.concatenate([part[...].reshape(-1, part.shape[-1]) for part in parts], axis=0)
+
+
+def first_kernel(ritz_ref, vec_ref, *refs):
+    mine, (modes_ref, projected_ref) = refs[:-2], refs[-2:]
+    sel = blocks_in(mine)
+    depth = sel.shape[0]
+    projected_ref[...] = jnp.dot(vec_ref[:, :depth], sel, preferred_element_type=F32)
+    modes_ref[...] = jnp.dot(ritz_ref[:, :depth], sel, preferred_element_type=F32)
+
+
+def second_kernel(ritz_ref, vec_ref, spread_ref, factor_ref, modes_ref, projected_ref, *refs):
+    sib, out_ref = refs[:-1], refs[-1]
+    sel = blocks_in(sib)
+    depth = sel.shape[0]
+    projected = projected_ref[...] + jnp.dot(vec_ref[:, depth:], sel, preferred_element_type=F32)
+    weights = precise(factor_ref[...], projected).astype(BF16)
+    modes = modes_ref[...] + jnp.dot(ritz_ref[:, depth:], sel, preferred_element_type=F32)
+    modes = modes - jnp.dot(spread_ref[...], weights, preferred_element_type=F32)
+    out_ref[...] = modes.astype(BF16)
+
+
+def modes_in_two(ritz_sorted, vec, spreads, factor, mine, sib):
+    dofs, order = ritz_sorted.shape
+    width = mine[0].shape[-1]
+    size = factor.shape[0]
+    in_vmem = pl.BlockSpec(memory_space=pltpu.VMEM)
+    params = pltpu.CompilerParams(vmem_limit_bytes=16 << 20)
+    cost = pl.CostEstimate(
+        flops=order * width * (dofs + size), bytes_accessed=dofs * order, transcendentals=0
+    )
+    modes, projected = pl.pallas_call(
+        first_kernel,
+        out_shape=(jax.ShapeDtypeStruct((dofs, width), F32), jax.ShapeDtypeStruct((size, width), F32)),
+        in_specs=[in_vmem] * (2 + len(mine)),
+        out_specs=(in_vmem, in_vmem),
+        compiler_params=params,
+        cost_estimate=cost,
+    )(ritz_sorted, vec, *mine)
+    return pl.pallas_call(
+        second_kernel,
+        out_shape=jax.ShapeDtypeStruct((dofs, width), BF16),
+        in_specs=[in_vmem] * (6 + len(sib)),
+        out_specs=in_vmem,
+        compiler_params=params,
+        cost_estimate=cost,
+    )(ritz_sorted, vec, spreads, factor, modes, projected, *sib)
+
+
 def per_device(rows, cols, eigvecs, house_one, house_two, tile_map, select, ritz_basis):
     deep = cols // 2
     row_at, col_at = lax.axis_index("row"), lax.axis_index("col")
@@ -269,7 +334,9 @@
             parts.append(over_step(held, step))
         return parts
 
-    own, keep, give = prepare(here, select, eigvecs, house_two.T, house_one.T, cols)
+    keep, give = prepare(here, select, eigvecs, cols)
+    own = jnp.pad(house_two.T, ((0, share), (0, 0))) + jnp.pad(house_one.T, ((share, 0), (0, 0)))
+    own = own.astype(BF16)
 
     got, own = lax.optimization_barrier((to_core(give), own))
     keep = keep + got
@@ -318,8 +385,12 @@
     change = lax.dot_general(here_v, all_weights, (((0,), (0,)), ((), ())), preferred_element_type=F32)
     back_vectors = eigvecs - change
 
-    vec, spreads = spread(here, tile_map, ritz_basis, mine_v, sib_v)
-    modes = modes_of(here, tile_map, ritz_basis, vec, spreads, factor, mine_e, sib_e)
+    if local // cols == TILE:
+        ritz_sorted, vec, spreads = sort(here, tile_map, ritz_basis, mine_v, sib_v)
+        modes = modes_in_two(ritz_sorted, vec, spreads, factor, mine_e, sib_e)
+    else:
+        vec, spreads = spread(here, tile_map, ritz_basis, mine_v, sib_v)
+        modes = modes_of(here, tile_map, ritz_basis, vec, spreads, factor, mine_e, sib_e)
     return back_vectors, modes
 
 

time: 69.5 us -> 65.9 us (0.948)
  local copies, waits for them, and re-layouts: 4.19 us -> 2.52 us
  Pallas kernels: 17.1 us -> 15.5 us
  waiting for transfers between devices: 16.3 us -> 15.5 us
    ppermute x6, waiting for transfers between devices: 5.3 us -> 3.34 us  [over_step(): return lax.ppermute(x, ('row', 'col'), pairs)]
    unnamed x16, local copies, waits for them, and re-layouts: 3.97 us -> 2.3 us
    pallas_call x3 -> x4, Pallas kernels: 11.8 us -> 10.2 us  [the longest x1 4.26 us: sort(): pl.pallas_call(functools.partial(sort_kernel, len(mine)), out_shape=(jax....]
    ppermute x3, waiting for transfers between devices: 0.7 us -> 1.93 us  [to_row(): return lax.ppermute(x, 'row', [(i, i ^ peer) for i in range(rows)])]
  transfers between devices with their start and end apart: 25 -> 25, of which waited for: 10 -> 9; matrix products, arithmetic and copies ran while one was open for 5% -> 5% of each run, Pallas kernels for 13% -> 17%
where the time goes in v3:
time: 65.9 us; the launch traced here: 65.8 us
  starting transfers between devices  28.2 us (43%)
  Pallas kernels  15.5 us (24%)
  waiting for transfers between devices  15.5 us (24%)
  matrix products  2.63 us (4%)
  local copies, waits for them, and re-layouts  2.52 us (4%)
  between operations  0.98 us (1%)
    ppermute x9, starting transfers between devices, to_deep(): return lax.ppermute(x, 'col', [(i, i ^ 2 * level) for i in range(cols)])  14.4 us
    ppermute x9, waiting for transfers between devices, to_deep(): return lax.ppermute(x, 'col', [(i, i ^ 2 * level) for i in range(cols)])  9.08 us
    ppermute x6, starting transfers between devices, over_step(): return lax.ppermute(x, ('row', 'col'), pairs)  8.41 us
    pallas_call x1, Pallas kernels, factor_of(): pl.pallas_call(functools.partial(factor_kernel, len(mine)), out_shape=jax...  5.31 us
    pallas_call x1, Pallas kernels, sort(): pl.pallas_call(functools.partial(sort_kernel, len(mine)), out_shape=(jax....  4.26 us
    ppermute x3, starting transfers between devices, to_row(): return lax.ppermute(x, 'row', [(i, i ^ peer) for i in range(rows)])  3.55 us
    pallas_call x1, Pallas kernels, modes_in_two(): pl.pallas_call(second_kernel, out_shape=jax.ShapeDtypeStruct((dofs, width...  3.38 us
    ppermute x6, waiting for transfers between devices, over_step(): return lax.ppermute(x, ('row', 'col'), pairs)  3.34 us
  transfers between devices with their start and end apart: 25, of which 9 were waited for; matrix products, arithmetic and copies ran while one was open for 5% of the time, Pallas kernels for 17%

profile of v3, /device:TPU:0, one launch (start us, length us, event | category | flops | bytes accessed | tf_op | source)
XLA Modules:
  0.0 65.8 jit_solution(14518152588462766928)
XLA Ops:
  0.7 1.6 %copy-done = f32[1024,512]{1,0:T(8,128)S(1)} copy-done((f32[1024,512]{1,0:T(8,128)S(1)}, f32[1024,512]{1,0:T(8,128)}, u32[]{:S(2)}) %copy-start) | copy-done | bytes 2097176
  5.7 2.9 %collective-permute-start.1 = (bf16[32,1024]{1,0:T(8,128)(2,1)S(1)}, bf16[32,1024]{1,0:T(8,128)(2,1)S(1)}, u32[]{:S(2)}, u32[]{:S(2)}) collective-permute-start(bf16[32,1024]{1,0:T(8,128)(2,1)S(1)} %add_convert_fusion), channel_id=1, source_target_pairs={{0,2},{1,3},{2,0},{3,1},{4,6},{5,7},{6,4},{7,5},{8,10},{9,11},{10,... | collective-permute-start | bytes 196616 | tf_op jit(solution)/shard_map/ppermute | solution.py:313
  8.7 2.6 %collective-permute-start.2 = (bf16[32,1024]{1,0:T(8,128)(2,1)S(1)}, bf16[32,1024]{1,0:T(8,128)(2,1)S(1)}, u32[]{:S(2)}, u32[]{:S(2)}) collective-permute-start(bf16[32,1024]{1,0:T(8,128)(2,1)S(1)} %add_convert_fusion), channel_id=1, source_target_pairs={{0,4},{1,5},{2,6},{3,7},{4,0},{5,1},{6,2},{7,3},{8,12},{9,13},{10,... | collective-permute-start | bytes 196616 | tf_op jit(solution)/shard_map/ppermute | solution.py:313
  11.3 4.9 %collective-permute-done.2 = bf16[32,1024]{1,0:T(8,128)(2,1)S(1)} collective-permute-done((bf16[32,1024]{1,0:T(8,128)(2,1)S(1)}, bf16[32,1024]{1,0:T(8,128)(2,1)S(1)}, u32[]{:S(2)}, u32[]{:S(2)}) %collective-permute-start.2) | collective-permute-done | bytes 65568 | tf_op jit(solution)/shard_map/ppermute | solution.py:313
  17.4 1.6 %collective-permute-start.5 = (bf16[1,128,1024]{2,1,0:T(8,128)(2,1)S(1)}, bf16[1,128,1024]{2,1,0:T(8,128)(2,1)S(1)}, u32[]{:S(2)}, u32[]{:S(2)}) collective-permute-start(bf16[1,128,1024]{2,1,0:T(8,128)(2,1)S(1)} %bitcast.39), channel_id=1, source_target_pairs={{0,8},{1,17},{2,10},{3,19},{4,12},{5,21},{6,14},{7,23},{8,0},{9,25... | collective-permute-start | bytes 786440 | tf_op jit(solution)/shard_map/ppermute | solution.py:326
  20.1 1.7 %collective-permute-start.15 = (bf16[128,256]{1,0:T(8,128)(2,1)S(1)}, bf16[128,256]{1,0:T(8,128)(2,1)S(1)}, u32[]{:S(2)}, u32[]{:S(2)}) collective-permute-start(bf16[128,256]{1,0:T(8,128)(2,1)S(1)} %get-tuple-element.38), channel_id=1, source_target_pairs={{0,4},{1,5},{2,6},{3,7},{4,0},{5,1},{6,2},{7,3},{8,12},{9,13},{10,... | collective-permute-start | bytes 196616 | tf_op jit(solution)/shard_map/ppermute | solution.py:313
  21.8 1.8 %collective-permute-start.16 = (bf16[128,256]{1,0:T(8,128)(2,1)S(1)}, bf16[128,256]{1,0:T(8,128)(2,1)S(1)}, u32[]{:S(2)}, u32[]{:S(2)}) collective-permute-start(bf16[128,256]{1,0:T(8,128)(2,1)S(1)} %get-tuple-element.37), channel_id=1, source_target_pairs={{0,6},{1,7},{2,4},{3,5},{4,2},{5,3},{6,0},{7,1},{8,14},{9,15},{10,... | collective-permute-start | bytes 196616 | tf_op jit(solution)/shard_map/ppermute | solution.py:313
  23.9 1.6 %collective-permute-start.6 = (bf16[2,128,1024]{2,1,0:T(8,128)(2,1)S(1)}, bf16[2,128,1024]{2,1,0:T(8,128)(2,1)S(1)}, u32[]{:S(2)}, u32[]{:S(2)}) collective-permute-start(bf16[2,128,1024]{2,1,0:T(8,128)(2,1)S(1)} %pad_maximum_fusion.1), channel_id=1, source_target_pairs={{0,16},{1,9},{2,18},{3,11},{4,20},{5,13},{6,22},{7,15},{8,24},{9,1... | collective-permute-start | bytes 1572872 | tf_op jit(solution)/shard_map/ppermute | solution.py:326
  26.7 1.8 %collective-permute-done.15 = bf16[128,256]{1,0:T(8,128)(2,1)S(1)} collective-permute-done((bf16[128,256]{1,0:T(8,128)(2,1)S(1)}, bf16[128,256]{1,0:T(8,128)(2,1)S(1)}, u32[]{:S(2)}, u32[]{:S(2)}) %collective-permute-start.15) | collective-permute-done | bytes 65568 | tf_op jit(solution)/shard_map/ppermute | solution.py:313
  28.5 1.6 %collective-permute-start.17 = (bf16[128,256]{1,0:T(8,128)(2,1)S(1)}, bf16[128,256]{1,0:T(8,128)(2,1)S(1)}, u32[]{:S(2)}, u32[]{:S(2)}) collective-permute-start(bf16[128,256]{1,0:T(8,128)(2,1)S(1)} %add_add_fusion), channel_id=1, source_target_pairs={{0,2},{1,3},{2,0},{3,1},{4,6},{5,7},{6,4},{7,5},{8,10},{9,11},{10,... | collective-permute-start | bytes 196616 | tf_op jit(solution)/shard_map/ppermute | solution.py:313
  30.1 1.2 %collective-permute-start.18 = (bf16[128,256]{1,0:T(8,128)(2,1)S(1)}, bf16[128,256]{1,0:T(8,128)(2,1)S(1)}, u32[]{:S(2)}, u32[]{:S(2)}) collective-permute-start(bf16[128,256]{1,0:T(8,128)(2,1)S(1)} %add_add_fusion), channel_id=1, source_target_pairs={{0,4},{1,5},{2,6},{3,7},{4,0},{5,1},{6,2},{7,3},{8,12},{9,13},{10,... | collective-permute-start | bytes 196616 | tf_op jit(solution)/shard_map/ppermute | solution.py:313
  31.4 1.6 %collective-permute-start.19 = (bf16[128,256]{1,0:T(8,128)(2,1)S(1)}, bf16[128,256]{1,0:T(8,128)(2,1)S(1)}, u32[]{:S(2)}, u32[]{:S(2)}) collective-permute-start(bf16[128,256]{1,0:T(8,128)(2,1)S(1)} %add_add_fusion), channel_id=1, source_target_pairs={{0,6},{1,7},{2,4},{3,5},{4,2},{5,3},{6,0},{7,1},{8,14},{9,15},{10,... | collective-permute-start | bytes 196616 | tf_op jit(solution)/shard_map/ppermute | solution.py:313
  33.0 1.6 %collective-permute-done.9 = bf16[2,256,128]{2,1,0:T(8,128)(2,1)S(1)} collective-permute-done((bf16[2,256,128]{2,1,0:T(8,128)(2,1)S(1)}, bf16[2,256,128]{2,1,0:T(8,128)(2,1)S(1)}, u32[]{:S(2)}, u32[]{:S(2)}) %collective-permute-start.9) | collective-permute-done | bytes 131104 | tf_op jit(solution)/shard_map/ppermute | solution.py:326
  35.2 1.6 %collective-permute-start.10 = (bf16[1,256,128]{2,1,0:T(8,128)(2,1)S(1)}, bf16[1,256,128]{2,1,0:T(8,128)(2,1)S(1)}, u32[]{:S(2)}, u32[]{:S(2)}) collective-permute-start(bf16[1,256,128]{2,1,0:T(8,128)(2,1)S(1)} %slice.46), channel_id=1, source_target_pairs={{0,8},{1,17},{2,10},{3,19},{4,12},{5,21},{6,14},{7,23},{8,0},{9,25... | collective-permute-start | bytes 196616 | tf_op jit(solution)/shard_map/ppermute | solution.py:326
  38.0 1.5 %collective-permute-done.10 = bf16[1,256,128]{2,1,0:T(8,128)(2,1)S(1)} collective-permute-done((bf16[1,256,128]{2,1,0:T(8,128)(2,1)S(1)}, bf16[1,256,128]{2,1,0:T(8,128)(2,1)S(1)}, u32[]{:S(2)}, u32[]{:S(2)}) %collective-permute-start.10) | collective-permute-done | bytes 65568 | tf_op jit(solution)/shard_map/ppermute | solution.py:326
  39.6 1.6 %collective-permute-start.20 = (bf16[1,4,128,256]{3,2,1,0:T(8,128)(2,1)S(1)}, bf16[1,4,128,256]{3,2,1,0:T(8,128)(2,1)S(1)}, u32[]{:S(2)}, u32[]{:S(2)}) collective-permute-start(bf16[1,4,128,256]{3,2,1,0:T(8,128)(2,1)S(1)} %maximum_bitcast_fusion.refs_0_), channel_id=1, source_target_pairs={{0,8},{1,17},{2,10},{3,19},{4,12},{5,21},{6,14},{7,23},{8,0},{9,25... | collective-permute-start | bytes 786440 | tf_op jit(solution)/shard_map/ppermute | solution.py:326
  41.1 5.3 %shard_map.78.factor_ref = f32[256,256]{1,0:T(8,128)S(1)} custom-call(s32[1,256]{1,0:T(1,128)S(1)} %fusion.3.place_ref, bf16[1,128,1024]{2,1,0:T(8,128)(2,1)S(1)} %bitcast.42, bf16[1,128,1024]{2,1,0:T(8,128)(2,1)S(1)} %collective-permute-done.5.refs_1_, bf16[2,128,1024]{2,1,0:T(8,128)(2,1)S(1)} %collective-permute-done.6.refs_2_, ...), custom_call_target="tpu_custom_call" | custom-call | flops 3758096384 | bytes 2621440 | tf_op jit(solution)/shard_map/pallas_call | solution.py:122
  46.5 1.6 %collective-permute-start.21 = (bf16[2,4,128,256]{3,2,1,0:T(8,128)(2,1)S(1)}, bf16[2,4,128,256]{3,2,1,0:T(8,128)(2,1)S(1)}, u32[]{:S(2)}, u32[]{:S(2)}) collective-permute-start(bf16[2,4,128,256]{3,2,1,0:T(8,128)(2,1)S(1)} %pad_maximum_fusion.3), channel_id=1, source_target_pairs={{0,16},{1,9},{2,18},{3,11},{4,20},{5,13},{6,22},{7,15},{8,24},{9,1... | collective-permute-start | bytes 1572872 | tf_op jit(solution)/shard_map/ppermute | solution.py:326
  50.1 1.9 %collective-permute-start.13 = (bf16[256,128]{1,0:T(8,128)(2,1)S(1)}, bf16[256,128]{1,0:T(8,128)(2,1)S(1)}, u32[]{:S(2)}, u32[]{:S(2)}) collective-permute-start(bf16[256,128]{1,0:T(8,128)(2,1)S(1)} %get-tuple-element.41), channel_id=1, source_target_pairs={{0,24},{8,16},{16,8},{24,0},{1,25},{9,17},{17,9},{25,1},{2,26},{10... | collective-permute-start | bytes 196616 | tf_op jit(solution)/shard_map/ppermute | solution.py:316
  52.1 4.3 %shard_map.79 = (bf16[1024,4096]{1,0:T(8,128)(2,1)S(1)}, bf16[256,4096]{1,0:T(8,128)(2,1)S(1)}, bf16[1024,256]{1,0:T(8,128)(2,1)S(1)}) custom-call(s32[3]{0:T(128)S(1)} %pad_add_fusion.here_ref, s32[32]{0:T(128)S(1)} %copy-done.3, bf16[1024,4096]{1,0:T(8,128)(2,1)S(1)} %bitcast.38, bf16[1,128,1024]{2,1,0:T(8,128)(2,1)S(1)} %bitcast.43, ...), custom_call_target="tpu_custom_call" | custom-call | flops 2147483648 | bytes 16777216 | tf_op jit(solution)/shard_map/pallas_call | solution.py:234
  56.4 1.9 %collective-permute-done.12 = bf16[256,128]{1,0:T(8,128)(2,1)S(1)} collective-permute-done((bf16[256,128]{1,0:T(8,128)(2,1)S(1)}, bf16[256,128]{1,0:T(8,128)(2,1)S(1)}, u32[]{:S(2)}, u32[]{:S(2)}) %collective-permute-start.12) | collective-permute-done | bytes 65568 | tf_op jit(solution)/shard_map/ppermute | solution.py:316
  59.0 1.8 %convolution_subtract_fusion = f32[1024,512]{1,0:T(8,128)} fusion(f32[1024,512]{1,0:T(8,128)S(1)} %copy-done.1, bf16[256,512]{1,0:T(8,128)(2,1)S(1)} %constant_dynamic-update-slice_fusion, bf16[128,1024]{1,0:T(8,128)(2,1)S(1)} %bitcast.45, bf16[128,1024]{1,0:T(8,128)(2,1)S(1)} %pad_maximum_fusion.6), kind=kOutput, calls=%fused_computation | convolution fusion | flops 270008320 | bytes 4980736 | tf_op jit(solution)/shard_map/dot_general | solution.py:385
  60.8 1.5 %shard_map.80 = (f32[1024,256]{1,0:T(8,128)S(1)}, f32[256,256]{1,0:T(8,128)S(1)}) custom-call(bf16[1024,4096]{1,0:T(8,128)(2,1)S(1)} %get-tuple-element.24.ritz_ref, bf16[256,4096]{1,0:T(8,128)(2,1)S(1)} %get-tuple-element.25.vec_ref, bf16[1,4,128,256]{3,2,1,0:T(8,128)(2,1)S(1)} %maximum_bitcast_fusion.refs_0_, ...), custom_call_target="tpu_custom_call" | custom-call | flops 1342177280 | bytes 4194304 | tf_op jit(solution)/shard_map/pallas_call | solution.py:282
  62.4 3.4 %shard_map.81 = bf16[1024,256]{1,0:T(8,128)(2,1)} custom-call(bf16[1024,4096]{1,0:T(8,128)(2,1)S(1)} %get-tuple-element.24.ritz_ref, bf16[256,4096]{1,0:T(8,128)(2,1)S(1)} %get-tuple-element.25.vec_ref, bf16[1024,256]{1,0:T(8,128)(2,1)S(1)} %get-tuple-element.26.spread_ref, f32[256,256]{1,0:T(8,128)S(1)} %shard_map.78.factor_ref, ...), custom_call_target="tpu_custom_call" | custom-call | flops 1342177280 | bytes 4194304 | tf_op jit(solution)/shard_map/pallas_call | solution.py:290
  (71 shorter events, 12.0 us)
Async XLA Ops:
  5.7 5.6 %collective-permute-start.1 = (bf16[32,1024]{1,0:T(8,128)(2,1)S(1)}, bf16[32,1024]{1,0:T(8,128)(2,1)S(1)}, u32[]{:S(2)}, u32[]{:S(2)}) collective-permute-start(bf16[32,1024]{1,0:T(8,128)(2,1)S(1)} %add_convert_fusion), channel_id=1, source_target_pairs={{0,2},{1,3},{2,0},{3,1},{4,6},{5,7},{6,4},{7,5},{8,10},{9,11},{10,... | collective-permute-start | bytes 196616 | tf_op jit(solution)/shard_map/ppermute | solution.py:313
  8.7 7.5 %collective-permute-start.2 = (bf16[32,1024]{1,0:T(8,128)(2,1)S(1)}, bf16[32,1024]{1,0:T(8,128)(2,1)S(1)}, u32[]{:S(2)}, u32[]{:S(2)}) collective-permute-start(bf16[32,1024]{1,0:T(8,128)(2,1)S(1)} %add_convert_fusion), channel_id=1, source_target_pairs={{0,4},{1,5},{2,6},{3,7},{4,0},{5,1},{6,2},{7,3},{8,12},{9,13},{10,... | collective-permute-start | bytes 196616 | tf_op jit(solution)/shard_map/ppermute | solution.py:313
  11.3 6.2 %collective-permute-start.3 = (bf16[32,1024]{1,0:T(8,128)(2,1)S(1)}, bf16[32,1024]{1,0:T(8,128)(2,1)S(1)}, u32[]{:S(2)}, u32[]{:S(2)}) collective-permute-start(bf16[32,1024]{1,0:T(8,128)(2,1)S(1)} %add_convert_fusion), channel_id=1, source_target_pairs={{0,6},{1,7},{2,4},{3,5},{4,2},{5,3},{6,0},{7,1},{8,14},{9,15},{10,... | collective-permute-start | bytes 196616 | tf_op jit(solution)/shard_map/ppermute | solution.py:313
  17.4 6.4 %collective-permute-start.5 = (bf16[1,128,1024]{2,1,0:T(8,128)(2,1)S(1)}, bf16[1,128,1024]{2,1,0:T(8,128)(2,1)S(1)}, u32[]{:S(2)}, u32[]{:S(2)}) collective-permute-start(bf16[1,128,1024]{2,1,0:T(8,128)(2,1)S(1)} %bitcast.39), channel_id=1, source_target_pairs={{0,8},{1,17},{2,10},{3,19},{4,12},{5,21},{6,14},{7,23},{8,0},{9,25... | collective-permute-start | bytes 786440 | tf_op jit(solution)/shard_map/ppermute | solution.py:326
  19.1 6.5 %collective-permute-start.4 = (bf16[1,128,1024]{2,1,0:T(8,128)(2,1)S(1)}, bf16[1,128,1024]{2,1,0:T(8,128)(2,1)S(1)}, u32[]{:S(2)}, u32[]{:S(2)}) collective-permute-start(bf16[1,128,1024]{2,1,0:T(8,128)(2,1)S(1)} %bitcast.40), channel_id=1, source_target_pairs={{0,1},{1,0},{2,3},{3,2},{4,5},{5,4},{6,7},{7,6},{8,9},{9,8},{10,11... | collective-permute-start | bytes 786440 | tf_op jit(solution)/shard_map/ppermute | solution.py:310
  19.2 7.5 %collective-permute-start.14 = (bf16[128,256]{1,0:T(8,128)(2,1)S(1)}, bf16[128,256]{1,0:T(8,128)(2,1)S(1)}, u32[]{:S(2)}, u32[]{:S(2)}) collective-permute-start(bf16[128,256]{1,0:T(8,128)(2,1)S(1)} %get-tuple-element.36), channel_id=1, source_target_pairs={{0,2},{1,3},{2,0},{3,1},{4,6},{5,7},{6,4},{7,5},{8,10},{9,11},{10,... | collective-permute-start | bytes 196616 | tf_op jit(solution)/shard_map/ppermute | solution.py:313
  20.1 8.4 %collective-permute-start.15 = (bf16[128,256]{1,0:T(8,128)(2,1)S(1)}, bf16[128,256]{1,0:T(8,128)(2,1)S(1)}, u32[]{:S(2)}, u32[]{:S(2)}) collective-permute-start(bf16[128,256]{1,0:T(8,128)(2,1)S(1)} %get-tuple-element.38), channel_id=1, source_target_pairs={{0,4},{1,5},{2,6},{3,7},{4,0},{5,1},{6,2},{7,3},{8,12},{9,13},{10,... | collective-permute-start | bytes 196616 | tf_op jit(solution)/shard_map/ppermute | solution.py:313
  21.8 6.7 %collective-permute-start.16 = (bf16[128,256]{1,0:T(8,128)(2,1)S(1)}, bf16[128,256]{1,0:T(8,128)(2,1)S(1)}, u32[]{:S(2)}, u32[]{:S(2)}) collective-permute-start(bf16[128,256]{1,0:T(8,128)(2,1)S(1)} %get-tuple-element.37), channel_id=1, source_target_pairs={{0,6},{1,7},{2,4},{3,5},{4,2},{5,3},{6,0},{7,1},{8,14},{9,15},{10,... | collective-permute-start | bytes 196616 | tf_op jit(solution)/shard_map/ppermute | solution.py:313
  23.9 10.7 %collective-permute-start.6 = (bf16[2,128,1024]{2,1,0:T(8,128)(2,1)S(1)}, bf16[2,128,1024]{2,1,0:T(8,128)(2,1)S(1)}, u32[]{:S(2)}, u32[]{:S(2)}) collective-permute-start(bf16[2,128,1024]{2,1,0:T(8,128)(2,1)S(1)} %pad_maximum_fusion.1), channel_id=1, source_target_pairs={{0,16},{1,9},{2,18},{3,11},{4,20},{5,13},{6,22},{7,15},{8,24},{9,1... | collective-permute-start | bytes 1572872 | tf_op jit(solution)/shard_map/ppermute | solution.py:326
  26.1 8.5 %collective-permute-start.9 = (bf16[2,256,128]{2,1,0:T(8,128)(2,1)S(1)}, bf16[2,256,128]{2,1,0:T(8,128)(2,1)S(1)}, u32[]{:S(2)}, u32[]{:S(2)}) collective-permute-start(bf16[2,256,128]{2,1,0:T(8,128)(2,1)S(1)} %slice.45), channel_id=1, source_target_pairs={{0,16},{1,9},{2,18},{3,11},{4,20},{5,13},{6,22},{7,15},{8,24},{9,1... | collective-permute-start | bytes 393224 | tf_op jit(solution)/shard_map/ppermute | solution.py:326
  28.5 6.6 %collective-permute-start.17 = (bf16[128,256]{1,0:T(8,128)(2,1)S(1)}, bf16[128,256]{1,0:T(8,128)(2,1)S(1)}, u32[]{:S(2)}, u32[]{:S(2)}) collective-permute-start(bf16[128,256]{1,0:T(8,128)(2,1)S(1)} %add_add_fusion), channel_id=1, source_target_pairs={{0,2},{1,3},{2,0},{3,1},{4,6},{5,7},{6,4},{7,5},{8,10},{9,11},{10,... | collective-permute-start | bytes 196616 | tf_op jit(solution)/shard_map/ppermute | solution.py:313
  30.1 7.8 %collective-permute-start.18 = (bf16[128,256]{1,0:T(8,128)(2,1)S(1)}, bf16[128,256]{1,0:T(8,128)(2,1)S(1)}, u32[]{:S(2)}, u32[]{:S(2)}) collective-permute-start(bf16[128,256]{1,0:T(8,128)(2,1)S(1)} %add_add_fusion), channel_id=1, source_target_pairs={{0,4},{1,5},{2,6},{3,7},{4,0},{5,1},{6,2},{7,3},{8,12},{9,13},{10,... | collective-permute-start | bytes 196616 | tf_op jit(solution)/shard_map/ppermute | solution.py:313
  31.4 6.5 %collective-permute-start.19 = (bf16[128,256]{1,0:T(8,128)(2,1)S(1)}, bf16[128,256]{1,0:T(8,128)(2,1)S(1)}, u32[]{:S(2)}, u32[]{:S(2)}) collective-permute-start(bf16[128,256]{1,0:T(8,128)(2,1)S(1)} %add_add_fusion), channel_id=1, source_target_pairs={{0,6},{1,7},{2,4},{3,5},{4,2},{5,3},{6,0},{7,1},{8,14},{9,15},{10,... | collective-permute-start | bytes 196616 | tf_op jit(solution)/shard_map/ppermute | solution.py:313
  34.6 5.0 %collective-permute-start.7 = (bf16[1,128,1024]{2,1,0:T(8,128)(2,1)S(1)}, bf16[1,128,1024]{2,1,0:T(8,128)(2,1)S(1)}, u32[]{:S(2)}, u32[]{:S(2)}) collective-permute-start(bf16[1,128,1024]{2,1,0:T(8,128)(2,1)S(1)} %collective-permute-done.5.refs_1_), channel_id=1, source_target_pairs={{0,1},{1,0},{2,3},{3,2},{4,5},{5,4},{6,7},{7,6},{8,9},{9,8},{10,11... | collective-permute-start | bytes 786440 | tf_op jit(solution)/shard_map/ppermute | solution.py:310
  34.6 5.0 %collective-permute-start.8 = (bf16[2,128,1024]{2,1,0:T(8,128)(2,1)S(1)}, bf16[2,128,1024]{2,1,0:T(8,128)(2,1)S(1)}, u32[]{:S(2)}, u32[]{:S(2)}) collective-permute-start(bf16[2,128,1024]{2,1,0:T(8,128)(2,1)S(1)} %collective-permute-done.6.refs_2_), channel_id=1, source_target_pairs={{0,1},{1,0},{2,3},{3,2},{4,5},{5,4},{6,7},{7,6},{8,9},{9,8},{10,11... | collective-permute-start | bytes 1572872 | tf_op jit(solution)/shard_map/ppermute | solution.py:310
  35.2 4.3 %collective-permute-start.10 = (bf16[1,256,128]{2,1,0:T(8,128)(2,1)S(1)}, bf16[1,256,128]{2,1,0:T(8,128)(2,1)S(1)}, u32[]{:S(2)}, u32[]{:S(2)}) collective-permute-start(bf16[1,256,128]{2,1,0:T(8,128)(2,1)S(1)} %slice.46), channel_id=1, source_target_pairs={{0,8},{1,17},{2,10},{3,19},{4,12},{5,21},{6,14},{7,23},{8,0},{9,25... | collective-permute-start | bytes 196616 | tf_op jit(solution)/shard_map/ppermute | solution.py:326
  37.9 24.4 %collective-permute-start.22 = (bf16[1,4,128,256]{3,2,1,0:T(8,128)(2,1)S(1)}, bf16[1,4,128,256]{3,2,1,0:T(8,128)(2,1)S(1)}, u32[]{:S(2)}, u32[]{:S(2)}) collective-permute-start(bf16[1,4,128,256]{3,2,1,0:T(8,128)(2,1)S(1)} %maximum_bitcast_fusion.refs_0_), channel_id=1, source_target_pairs={{0,1},{1,0},{2,3},{3,2},{4,5},{5,4},{6,7},{7,6},{8,9},{9,8},{10,11... | collective-permute-start | bytes 786440 | tf_op jit(solution)/shard_map/ppermute | solution.py:310
  39.6 6.9 %collective-permute-start.20 = (bf16[1,4,128,256]{3,2,1,0:T(8,128)(2,1)S(1)}, bf16[1,4,128,256]{3,2,1,0:T(8,128)(2,1)S(1)}, u32[]{:S(2)}, u32[]{:S(2)}) collective-permute-start(bf16[1,4,128,256]{3,2,1,0:T(8,128)(2,1)S(1)} %maximum_bitcast_fusion.refs_0_), channel_id=1, source_target_pairs={{0,8},{1,17},{2,10},{3,19},{4,12},{5,21},{6,14},{7,23},{8,0},{9,25... | collective-permute-start | bytes 786440 | tf_op jit(solution)/shard_map/ppermute | solution.py:326
  46.5 11.8 %collective-permute-start.21 = (bf16[2,4,128,256]{3,2,1,0:T(8,128)(2,1)S(1)}, bf16[2,4,128,256]{3,2,1,0:T(8,128)(2,1)S(1)}, u32[]{:S(2)}, u32[]{:S(2)}) collective-permute-start(bf16[2,4,128,256]{3,2,1,0:T(8,128)(2,1)S(1)} %pad_maximum_fusion.3), channel_id=1, source_target_pairs={{0,16},{1,9},{2,18},{3,11},{4,20},{5,13},{6,22},{7,15},{8,24},{9,1... | collective-permute-start | bytes 1572872 | tf_op jit(solution)/shard_map/ppermute | solution.py:326
  48.5 7.8 %collective-permute-start.11 = (bf16[256,128]{1,0:T(8,128)(2,1)S(1)}, bf16[256,128]{1,0:T(8,128)(2,1)S(1)}, u32[]{:S(2)}, u32[]{:S(2)}) collective-permute-start(bf16[256,128]{1,0:T(8,128)(2,1)S(1)} %get-tuple-element.41), channel_id=1, source_target_pairs={{0,8},{8,0},{16,24},{24,16},{1,9},{9,1},{17,25},{25,17},{2,10},{10... | collective-permute-start | bytes 196616 | tf_op jit(solution)/shard_map/ppermute | solution.py:316
  49.6 8.7 %collective-permute-start.12 = (bf16[256,128]{1,0:T(8,128)(2,1)S(1)}, bf16[256,128]{1,0:T(8,128)(2,1)S(1)}, u32[]{:S(2)}, u32[]{:S(2)}) collective-permute-start(bf16[256,128]{1,0:T(8,128)(2,1)S(1)} %get-tuple-element.41), channel_id=1, source_target_pairs={{0,16},{8,24},{16,0},{24,8},{1,17},{9,25},{17,1},{25,9},{2,18},{10... | collective-permute-start | bytes 196616 | tf_op jit(solution)/shard_map/ppermute | solution.py:316
  50.1 8.3 %collective-permute-start.13 = (bf16[256,128]{1,0:T(8,128)(2,1)S(1)}, bf16[256,128]{1,0:T(8,128)(2,1)S(1)}, u32[]{:S(2)}, u32[]{:S(2)}) collective-permute-start(bf16[256,128]{1,0:T(8,128)(2,1)S(1)} %get-tuple-element.41), channel_id=1, source_target_pairs={{0,24},{8,16},{16,8},{24,0},{1,25},{9,17},{17,9},{25,1},{2,26},{10... | collective-permute-start | bytes 196616 | tf_op jit(solution)/shard_map/ppermute | solution.py:316
  58.4 4.0 %collective-permute-start.24 = (bf16[2,4,128,256]{3,2,1,0:T(8,128)(2,1)S(1)}, bf16[2,4,128,256]{3,2,1,0:T(8,128)(2,1)S(1)}, u32[]{:S(2)}, u32[]{:S(2)}) collective-permute-start(bf16[2,4,128,256]{3,2,1,0:T(8,128)(2,1)S(1)} %collective-permute-done.21.refs_2_), channel_id=1, source_target_pairs={{0,1},{1,0},{2,3},{3,2},{4,5},{5,4},{6,7},{7,6},{8,9},{9,8},{10,11... | collective-permute-start | bytes 1572872 | tf_op jit(solution)/shard_map/ppermute | solution.py:310
  58.5 3.9 %collective-permute-start.23 = (bf16[1,4,128,256]{3,2,1,0:T(8,128)(2,1)S(1)}, bf16[1,4,128,256]{3,2,1,0:T(8,128)(2,1)S(1)}, u32[]{:S(2)}, u32[]{:S(2)}) collective-permute-start(bf16[1,4,128,256]{3,2,1,0:T(8,128)(2,1)S(1)} %collective-permute-done.20.refs_1_), channel_id=1, source_target_pairs={{0,1},{1,0},{2,3},{3,2},{4,5},{5,4},{6,7},{7,6},{8,9},{9,8},{10,11... | collective-permute-start | bytes 786440 | tf_op jit(solution)/shard_map/ppermute | solution.py:310
  (9 other events, 66.3 us)

commit v4 on v3

--- a/solution.py
+++ b/solution.py
@@ -81,12 +81,31 @@
     )(here, select[None, :], eigvecs)
 
 
-def moved(order, x):
+def halves(x):
+    high = x.astype(BF16)
+    return high, (x - high.astype(F32)).astype(BF16)
+
+
+def moved(order, x, dims):
     width = x.shape[1]
-    high = x.astype(BF16)
-    parts = jnp.concatenate([high, (x - high.astype(F32)).astype(BF16)], axis=1)
-    both = jnp.dot(order, parts, preferred_element_type=F32)
+    both = lax.dot_general(order, jnp.concatenate(halves(x), axis=1), (dims, ((), ())), preferred_element_type=F32)
     return both[:, :width] + both[:, width:]
+
+
+def moved_sides(x, order, dims):
+    depth = x.shape[0]
+    both = lax.dot_general(jnp.concatenate(halves(x), axis=0), order, (dims, ((), ())), preferred_element_type=F32)
+    return both[:depth] + both[depth:]
+
+
+def close(left, right):
+    left_high, left_low = halves(left)
+    right_high, right_low = halves(right)
+    return jnp.dot(
+        jnp.concatenate([left_high, left_low, left_high], axis=1),
+        jnp.concatenate([right_high, right_high, right_low], axis=0),
+        preferred_element_type=F32,
+    )
 
 
 def factor_kernel(count, place_ref, *refs):
@@ -99,10 +118,8 @@
         both = jnp.concatenate([one[...], other[...]], axis=0)
         gram = gram + lax.dot_general(both, both, turned, preferred_element_type=F32)
     reflectors = lax.broadcasted_iota(jnp.int32, (size, size), 0)
-    order = jnp.where(reflectors == place_ref[...], 1.0, 0.0)
-    back = order.T.astype(BF16)
-    order = order.astype(BF16)
-    gram = moved(order, moved(order, gram).T)
+    order = jnp.where(reflectors == place_ref[...], 1.0, 0.0).astype(BF16)
+    gram = moved_sides(moved(order, gram, ((1,), (0,))), order, ((1,), (1,)))
     two, one = inverses([gram[:half, :half], gram[half:, half:]])
     mixed = -precise(one, precise(gram[half:, :half], two))
     factor = jnp.concatenate(
@@ -112,7 +129,7 @@
         ],
         axis=0,
     )
-    out_ref[...] = moved(back, moved(back, factor).T).T
+    out_ref[...] = moved_sides(moved(order, factor, ((0,), (0,))), order, ((1,), (0,)))
 
 
 def factor_of(place, mine, sib):
@@ -176,7 +193,7 @@
                 goal = pl.multiple_of(map_ref[row // TILE] * TILE + row % TILE, piece)
                 sel[pl.ds(goal, piece), :] = source[level]
     projected = jnp.dot(vec_ref[...], sel[...], preferred_element_type=F32)
-    weights = precise(factor_ref[...], projected).astype(BF16)
+    weights = close(factor_ref[...], projected).astype(BF16)
     modes = jnp.dot(ritz_ref[...], sel[...], preferred_element_type=F32)
     modes = modes - jnp.dot(spread_ref[...], weights, preferred_element_type=F32)
     out_ref[...] = modes.astype(BF16)
@@ -264,7 +281,7 @@
     sel = blocks_in(sib)
     depth = sel.shape[0]
     projected = projected_ref[...] + jnp.dot(vec_ref[:, depth:], sel, preferred_element_type=F32)
-    weights = precise(factor_ref[...], projected).astype(BF16)
+    weights = close(factor_ref[...], projected).astype(BF16)
     modes = modes_ref[...] + jnp.dot(ritz_ref[:, depth:], sel, preferred_element_type=F32)
     modes = modes - jnp.dot(spread_ref[...], weights, preferred_element_type=F32)
     out_ref[...] = modes.astype(BF16)

time: 65.9 us -> 65.4 us (level)
  transfers between devices with their start and end apart: 25 -> 25, of which waited for: 9 -> 9; matrix products, arithmetic and copies ran while one was open for 5% -> 5% of each run, Pallas kernels for 17% -> 16%
where the time goes in v4:
time: 65.4 us; the launch traced here: 65.2 us
  starting transfers between devices  28.2 us (43%)
  waiting for transfers between devices  15.5 us (24%)
  Pallas kernels  14.9 us (23%)
  matrix products  2.63 us (4%)
  local copies, waits for them, and re-layouts  2.52 us (4%)
  between operations  0.98 us (1%)
    ppermute x9, starting transfers between devices, to_deep(): return lax.ppermute(x, 'col', [(i, i ^ 2 * level) for i in range(cols)])  14.4 us
    ppermute x9, waiting for transfers between devices, to_deep(): return lax.ppermute(x, 'col', [(i, i ^ 2 * level) for i in range(cols)])  9.08 us
    ppermute x6, starting transfers between devices, over_step(): return lax.ppermute(x, ('row', 'col'), pairs)  8.4 us
    pallas_call x1, Pallas kernels, factor_of(): pl.pallas_call(functools.partial(factor_kernel, len(mine)), out_shape=jax...  4.9 us
    pallas_call x1, Pallas kernels, sort(): pl.pallas_call(functools.partial(sort_kernel, len(mine)), out_shape=(jax....  4.23 us
    ppermute x3, starting transfers between devices, to_row(): return lax.ppermute(x, 'row', [(i, i ^ peer) for i in range(rows)])  3.55 us
    ppermute x6, waiting for transfers between devices, over_step(): return lax.ppermute(x, ('row', 'col'), pairs)  3.34 us
    pallas_call x1, Pallas kernels, modes_in_two(): pl.pallas_call(second_kernel, out_shape=jax.ShapeDtypeStruct((dofs, width...  3.23 us
  transfers between devices with their start and end apart: 25, of which 9 were waited for; matrix products, arithmetic and copies ran while one was open for 5% of the time, Pallas kernels for 16%

profile of v4, /device:TPU:0, one launch (start us, length us, event | category | flops | bytes accessed | tf_op | source)
XLA Modules:
  0.0 65.2 jit_solution(4984286735014366945)
XLA Ops:
  0.7 1.6 %copy-done = f32[1024,512]{1,0:T(8,128)S(1)} copy-done((f32[1024,512]{1,0:T(8,128)S(1)}, f32[1024,512]{1,0:T(8,128)}, u32[]{:S(2)}) %copy-start) | copy-done | bytes 2097176
  5.7 2.9 %collective-permute-start.1 = (bf16[32,1024]{1,0:T(8,128)(2,1)S(1)}, bf16[32,1024]{1,0:T(8,128)(2,1)S(1)}, u32[]{:S(2)}, u32[]{:S(2)}) collective-permute-start(bf16[32,1024]{1,0:T(8,128)(2,1)S(1)} %add_convert_fusion), channel_id=1, source_target_pairs={{0,2},{1,3},{2,0},{3,1},{4,6},{5,7},{6,4},{7,5},{8,10},{9,11},{10,... | collective-permute-start | bytes 196616 | tf_op jit(solution)/shard_map/ppermute | solution.py:330
  8.7 2.6 %collective-permute-start.2 = (bf16[32,1024]{1,0:T(8,128)(2,1)S(1)}, bf16[32,1024]{1,0:T(8,128)(2,1)S(1)}, u32[]{:S(2)}, u32[]{:S(2)}) collective-permute-start(bf16[32,1024]{1,0:T(8,128)(2,1)S(1)} %add_convert_fusion), channel_id=1, source_target_pairs={{0,4},{1,5},{2,6},{3,7},{4,0},{5,1},{6,2},{7,3},{8,12},{9,13},{10,... | collective-permute-start | bytes 196616 | tf_op jit(solution)/shard_map/ppermute | solution.py:330
  11.3 4.9 %collective-permute-done.2 = bf16[32,1024]{1,0:T(8,128)(2,1)S(1)} collective-permute-done((bf16[32,1024]{1,0:T(8,128)(2,1)S(1)}, bf16[32,1024]{1,0:T(8,128)(2,1)S(1)}, u32[]{:S(2)}, u32[]{:S(2)}) %collective-permute-start.2) | collective-permute-done | bytes 65568 | tf_op jit(solution)/shard_map/ppermute | solution.py:330
  17.4 1.6 %collective-permute-start.5 = (bf16[1,128,1024]{2,1,0:T(8,128)(2,1)S(1)}, bf16[1,128,1024]{2,1,0:T(8,128)(2,1)S(1)}, u32[]{:S(2)}, u32[]{:S(2)}) collective-permute-start(bf16[1,128,1024]{2,1,0:T(8,128)(2,1)S(1)} %bitcast.39), channel_id=1, source_target_pairs={{0,8},{1,17},{2,10},{3,19},{4,12},{5,21},{6,14},{7,23},{8,0},{9,25... | collective-permute-start | bytes 786440 | tf_op jit(solution)/shard_map/ppermute | solution.py:343
  20.1 1.7 %collective-permute-start.15 = (bf16[128,256]{1,0:T(8,128)(2,1)S(1)}, bf16[128,256]{1,0:T(8,128)(2,1)S(1)}, u32[]{:S(2)}, u32[]{:S(2)}) collective-permute-start(bf16[128,256]{1,0:T(8,128)(2,1)S(1)} %get-tuple-element.38), channel_id=1, source_target_pairs={{0,4},{1,5},{2,6},{3,7},{4,0},{5,1},{6,2},{7,3},{8,12},{9,13},{10,... | collective-permute-start | bytes 196616 | tf_op jit(solution)/shard_map/ppermute | solution.py:330
  21.8 1.8 %collective-permute-start.16 = (bf16[128,256]{1,0:T(8,128)(2,1)S(1)}, bf16[128,256]{1,0:T(8,128)(2,1)S(1)}, u32[]{:S(2)}, u32[]{:S(2)}) collective-permute-start(bf16[128,256]{1,0:T(8,128)(2,1)S(1)} %get-tuple-element.37), channel_id=1, source_target_pairs={{0,6},{1,7},{2,4},{3,5},{4,2},{5,3},{6,0},{7,1},{8,14},{9,15},{10,... | collective-permute-start | bytes 196616 | tf_op jit(solution)/shard_map/ppermute | solution.py:330
  23.9 1.6 %collective-permute-start.6 = (bf16[2,128,1024]{2,1,0:T(8,128)(2,1)S(1)}, bf16[2,128,1024]{2,1,0:T(8,128)(2,1)S(1)}, u32[]{:S(2)}, u32[]{:S(2)}) collective-permute-start(bf16[2,128,1024]{2,1,0:T(8,128)(2,1)S(1)} %pad_maximum_fusion.1), channel_id=1, source_target_pairs={{0,16},{1,9},{2,18},{3,11},{4,20},{5,13},{6,22},{7,15},{8,24},{9,1... | collective-permute-start | bytes 1572872 | tf_op jit(solution)/shard_map/ppermute | solution.py:343
  26.7 1.8 %collective-permute-done.15 = bf16[128,256]{1,0:T(8,128)(2,1)S(1)} collective-permute-done((bf16[128,256]{1,0:T(8,128)(2,1)S(1)}, bf16[128,256]{1,0:T(8,128)(2,1)S(1)}, u32[]{:S(2)}, u32[]{:S(2)}) %collective-permute-start.15) | collective-permute-done | bytes 65568 | tf_op jit(solution)/shard_map/ppermute | solution.py:330
  28.5 1.6 %collective-permute-start.17 = (bf16[128,256]{1,0:T(8,128)(2,1)S(1)}, bf16[128,256]{1,0:T(8,128)(2,1)S(1)}, u32[]{:S(2)}, u32[]{:S(2)}) collective-permute-start(bf16[128,256]{1,0:T(8,128)(2,1)S(1)} %add_add_fusion), channel_id=1, source_target_pairs={{0,2},{1,3},{2,0},{3,1},{4,6},{5,7},{6,4},{7,5},{8,10},{9,11},{10,... | collective-permute-start | bytes 196616 | tf_op jit(solution)/shard_map/ppermute | solution.py:330
  31.4 1.6 %collective-permute-start.19 = (bf16[128,256]{1,0:T(8,128)(2,1)S(1)}, bf16[128,256]{1,0:T(8,128)(2,1)S(1)}, u32[]{:S(2)}, u32[]{:S(2)}) collective-permute-start(bf16[128,256]{1,0:T(8,128)(2,1)S(1)} %add_add_fusion), channel_id=1, source_target_pairs={{0,6},{1,7},{2,4},{3,5},{4,2},{5,3},{6,0},{7,1},{8,14},{9,15},{10,... | collective-permute-start | bytes 196616 | tf_op jit(solution)/shard_map/ppermute | solution.py:330
  33.0 1.6 %collective-permute-done.9 = bf16[2,256,128]{2,1,0:T(8,128)(2,1)S(1)} collective-permute-done((bf16[2,256,128]{2,1,0:T(8,128)(2,1)S(1)}, bf16[2,256,128]{2,1,0:T(8,128)(2,1)S(1)}, u32[]{:S(2)}, u32[]{:S(2)}) %collective-permute-start.9) | collective-permute-done | bytes 131104 | tf_op jit(solution)/shard_map/ppermute | solution.py:343
  35.2 1.6 %collective-permute-start.10 = (bf16[1,256,128]{2,1,0:T(8,128)(2,1)S(1)}, bf16[1,256,128]{2,1,0:T(8,128)(2,1)S(1)}, u32[]{:S(2)}, u32[]{:S(2)}) collective-permute-start(bf16[1,256,128]{2,1,0:T(8,128)(2,1)S(1)} %slice.46), channel_id=1, source_target_pairs={{0,8},{1,17},{2,10},{3,19},{4,12},{5,21},{6,14},{7,23},{8,0},{9,25... | collective-permute-start | bytes 196616 | tf_op jit(solution)/shard_map/ppermute | solution.py:343
  38.0 1.5 %collective-permute-done.10 = bf16[1,256,128]{2,1,0:T(8,128)(2,1)S(1)} collective-permute-done((bf16[1,256,128]{2,1,0:T(8,128)(2,1)S(1)}, bf16[1,256,128]{2,1,0:T(8,128)(2,1)S(1)}, u32[]{:S(2)}, u32[]{:S(2)}) %collective-permute-start.10) | collective-permute-done | bytes 65568 | tf_op jit(solution)/shard_map/ppermute | solution.py:343
  39.6 1.6 %collective-permute-start.20 = (bf16[1,4,128,256]{3,2,1,0:T(8,128)(2,1)S(1)}, bf16[1,4,128,256]{3,2,1,0:T(8,128)(2,1)S(1)}, u32[]{:S(2)}, u32[]{:S(2)}) collective-permute-start(bf16[1,4,128,256]{3,2,1,0:T(8,128)(2,1)S(1)} %maximum_bitcast_fusion.refs_0_), channel_id=1, source_target_pairs={{0,8},{1,17},{2,10},{3,19},{4,12},{5,21},{6,14},{7,23},{8,0},{9,25... | collective-permute-start | bytes 786440 | tf_op jit(solution)/shard_map/ppermute | solution.py:343
  41.1 4.9 %shard_map.78.factor_ref = f32[256,256]{1,0:T(8,128)S(1)} custom-call(s32[1,256]{1,0:T(1,128)S(1)} %fusion.3.place_ref, bf16[1,128,1024]{2,1,0:T(8,128)(2,1)S(1)} %bitcast.42, bf16[1,128,1024]{2,1,0:T(8,128)(2,1)S(1)} %collective-permute-done.5.refs_1_, bf16[2,128,1024]{2,1,0:T(8,128)(2,1)S(1)} %collective-permute-done.6.refs_2_, ...), custom_call_target="tpu_custom_call" | custom-call | flops 3758096384 | bytes 2621440 | tf_op jit(solution)/shard_map/pallas_call | solution.py:139
  46.1 1.6 %collective-permute-start.21 = (bf16[2,4,128,256]{3,2,1,0:T(8,128)(2,1)S(1)}, bf16[2,4,128,256]{3,2,1,0:T(8,128)(2,1)S(1)}, u32[]{:S(2)}, u32[]{:S(2)}) collective-permute-start(bf16[2,4,128,256]{3,2,1,0:T(8,128)(2,1)S(1)} %pad_maximum_fusion.3), channel_id=1, source_target_pairs={{0,16},{1,9},{2,18},{3,11},{4,20},{5,13},{6,22},{7,15},{8,24},{9,1... | collective-permute-start | bytes 1572872 | tf_op jit(solution)/shard_map/ppermute | solution.py:343
  48.1 1.5 %collective-permute-start.11 = (bf16[256,128]{1,0:T(8,128)(2,1)S(1)}, bf16[256,128]{1,0:T(8,128)(2,1)S(1)}, u32[]{:S(2)}, u32[]{:S(2)}) collective-permute-start(bf16[256,128]{1,0:T(8,128)(2,1)S(1)} %get-tuple-element.41), channel_id=1, source_target_pairs={{0,8},{8,0},{16,24},{24,16},{1,9},{9,1},{17,25},{25,17},{2,10},{10... | collective-permute-start | bytes 196616 | tf_op jit(solution)/shard_map/ppermute | solution.py:333
  50.1 1.5 %collective-permute-start.13 = (bf16[256,128]{1,0:T(8,128)(2,1)S(1)}, bf16[256,128]{1,0:T(8,128)(2,1)S(1)}, u32[]{:S(2)}, u32[]{:S(2)}) collective-permute-start(bf16[256,128]{1,0:T(8,128)(2,1)S(1)} %get-tuple-element.41), channel_id=1, source_target_pairs={{0,24},{8,16},{16,8},{24,0},{1,25},{9,17},{17,9},{25,1},{2,26},{10... | collective-permute-start | bytes 196616 | tf_op jit(solution)/shard_map/ppermute | solution.py:333
  51.7 4.2 %shard_map.79 = (bf16[1024,4096]{1,0:T(8,128)(2,1)S(1)}, bf16[256,4096]{1,0:T(8,128)(2,1)S(1)}, bf16[1024,256]{1,0:T(8,128)(2,1)S(1)}) custom-call(s32[3]{0:T(128)S(1)} %pad_add_fusion.here_ref, s32[32]{0:T(128)S(1)} %copy-done.3, bf16[1024,4096]{1,0:T(8,128)(2,1)S(1)} %bitcast.38, bf16[1,128,1024]{2,1,0:T(8,128)(2,1)S(1)} %bitcast.43, ...), custom_call_target="tpu_custom_call" | custom-call | flops 2147483648 | bytes 16777216 | tf_op jit(solution)/shard_map/pallas_call | solution.py:251
  56.0 2.0 %collective-permute-done.12 = bf16[256,128]{1,0:T(8,128)(2,1)S(1)} collective-permute-done((bf16[256,128]{1,0:T(8,128)(2,1)S(1)}, bf16[256,128]{1,0:T(8,128)(2,1)S(1)}, u32[]{:S(2)}, u32[]{:S(2)}) %collective-permute-start.12) | collective-permute-done | bytes 65568 | tf_op jit(solution)/shard_map/ppermute | solution.py:333
  58.6 1.8 %convolution_subtract_fusion = f32[1024,512]{1,0:T(8,128)} fusion(f32[1024,512]{1,0:T(8,128)S(1)} %copy-done.1, bf16[256,512]{1,0:T(8,128)(2,1)S(1)} %constant_dynamic-update-slice_fusion, bf16[128,1024]{1,0:T(8,128)(2,1)S(1)} %bitcast.45, bf16[128,1024]{1,0:T(8,128)(2,1)S(1)} %pad_maximum_fusion.6), kind=kOutput, calls=%fused_computation | convolution fusion | flops 270008320 | bytes 4980736 | tf_op jit(solution)/shard_map/dot_general | solution.py:402
  60.4 1.5 %shard_map.80 = (f32[1024,256]{1,0:T(8,128)S(1)}, f32[256,256]{1,0:T(8,128)S(1)}) custom-call(bf16[1024,4096]{1,0:T(8,128)(2,1)S(1)} %get-tuple-element.24.ritz_ref, bf16[256,4096]{1,0:T(8,128)(2,1)S(1)} %get-tuple-element.25.vec_ref, bf16[1,4,128,256]{3,2,1,0:T(8,128)(2,1)S(1)} %maximum_bitcast_fusion.refs_0_, ...), custom_call_target="tpu_custom_call" | custom-call | flops 1342177280 | bytes 4194304 | tf_op jit(solution)/shard_map/pallas_call | solution.py:299
  62.0 3.2 %shard_map.81 = bf16[1024,256]{1,0:T(8,128)(2,1)} custom-call(bf16[1024,4096]{1,0:T(8,128)(2,1)S(1)} %get-tuple-element.24.ritz_ref, bf16[256,4096]{1,0:T(8,128)(2,1)S(1)} %get-tuple-element.25.vec_ref, bf16[1024,256]{1,0:T(8,128)(2,1)S(1)} %get-tuple-element.26.spread_ref, f32[256,256]{1,0:T(8,128)S(1)} %shard_map.78.factor_ref, ...), custom_call_target="tpu_custom_call" | custom-call | flops 1342177280 | bytes 4194304 | tf_op jit(solution)/shard_map/pallas_call | solution.py:307
  (71 shorter events, 12.1 us)
Async XLA Ops:
  5.7 5.6 %collective-permute-start.1 = (bf16[32,1024]{1,0:T(8,128)(2,1)S(1)}, bf16[32,1024]{1,0:T(8,128)(2,1)S(1)}, u32[]{:S(2)}, u32[]{:S(2)}) collective-permute-start(bf16[32,1024]{1,0:T(8,128)(2,1)S(1)} %add_convert_fusion), channel_id=1, source_target_pairs={{0,2},{1,3},{2,0},{3,1},{4,6},{5,7},{6,4},{7,5},{8,10},{9,11},{10,... | collective-permute-start | bytes 196616 | tf_op jit(solution)/shard_map/ppermute | solution.py:330
  8.7 7.5 %collective-permute-start.2 = (bf16[32,1024]{1,0:T(8,128)(2,1)S(1)}, bf16[32,1024]{1,0:T(8,128)(2,1)S(1)}, u32[]{:S(2)}, u32[]{:S(2)}) collective-permute-start(bf16[32,1024]{1,0:T(8,128)(2,1)S(1)} %add_convert_fusion), channel_id=1, source_target_pairs={{0,4},{1,5},{2,6},{3,7},{4,0},{5,1},{6,2},{7,3},{8,12},{9,13},{10,... | collective-permute-start | bytes 196616 | tf_op jit(solution)/shard_map/ppermute | solution.py:330
  11.3 6.2 %collective-permute-start.3 = (bf16[32,1024]{1,0:T(8,128)(2,1)S(1)}, bf16[32,1024]{1,0:T(8,128)(2,1)S(1)}, u32[]{:S(2)}, u32[]{:S(2)}) collective-permute-start(bf16[32,1024]{1,0:T(8,128)(2,1)S(1)} %add_convert_fusion), channel_id=1, source_target_pairs={{0,6},{1,7},{2,4},{3,5},{4,2},{5,3},{6,0},{7,1},{8,14},{9,15},{10,... | collective-permute-start | bytes 196616 | tf_op jit(solution)/shard_map/ppermute | solution.py:330
  17.4 6.4 %collective-permute-start.5 = (bf16[1,128,1024]{2,1,0:T(8,128)(2,1)S(1)}, bf16[1,128,1024]{2,1,0:T(8,128)(2,1)S(1)}, u32[]{:S(2)}, u32[]{:S(2)}) collective-permute-start(bf16[1,128,1024]{2,1,0:T(8,128)(2,1)S(1)} %bitcast.39), channel_id=1, source_target_pairs={{0,8},{1,17},{2,10},{3,19},{4,12},{5,21},{6,14},{7,23},{8,0},{9,25... | collective-permute-start | bytes 786440 | tf_op jit(solution)/shard_map/ppermute | solution.py:343
  19.1 6.5 %collective-permute-start.4 = (bf16[1,128,1024]{2,1,0:T(8,128)(2,1)S(1)}, bf16[1,128,1024]{2,1,0:T(8,128)(2,1)S(1)}, u32[]{:S(2)}, u32[]{:S(2)}) collective-permute-start(bf16[1,128,1024]{2,1,0:T(8,128)(2,1)S(1)} %bitcast.40), channel_id=1, source_target_pairs={{0,1},{1,0},{2,3},{3,2},{4,5},{5,4},{6,7},{7,6},{8,9},{9,8},{10,11... | collective-permute-start | bytes 786440 | tf_op jit(solution)/shard_map/ppermute | solution.py:327
  19.2 7.5 %collective-permute-start.14 = (bf16[128,256]{1,0:T(8,128)(2,1)S(1)}, bf16[128,256]{1,0:T(8,128)(2,1)S(1)}, u32[]{:S(2)}, u32[]{:S(2)}) collective-permute-start(bf16[128,256]{1,0:T(8,128)(2,1)S(1)} %get-tuple-element.36), channel_id=1, source_target_pairs={{0,2},{1,3},{2,0},{3,1},{4,6},{5,7},{6,4},{7,5},{8,10},{9,11},{10,... | collective-permute-start | bytes 196616 | tf_op jit(solution)/shard_map/ppermute | solution.py:330
  20.1 8.4 %collective-permute-start.15 = (bf16[128,256]{1,0:T(8,128)(2,1)S(1)}, bf16[128,256]{1,0:T(8,128)(2,1)S(1)}, u32[]{:S(2)}, u32[]{:S(2)}) collective-permute-start(bf16[128,256]{1,0:T(8,128)(2,1)S(1)} %get-tuple-element.38), channel_id=1, source_target_pairs={{0,4},{1,5},{2,6},{3,7},{4,0},{5,1},{6,2},{7,3},{8,12},{9,13},{10,... | collective-permute-start | bytes 196616 | tf_op jit(solution)/shard_map/ppermute | solution.py:330
  21.8 6.7 %collective-permute-start.16 = (bf16[128,256]{1,0:T(8,128)(2,1)S(1)}, bf16[128,256]{1,0:T(8,128)(2,1)S(1)}, u32[]{:S(2)}, u32[]{:S(2)}) collective-permute-start(bf16[128,256]{1,0:T(8,128)(2,1)S(1)} %get-tuple-element.37), channel_id=1, source_target_pairs={{0,6},{1,7},{2,4},{3,5},{4,2},{5,3},{6,0},{7,1},{8,14},{9,15},{10,... | collective-permute-start | bytes 196616 | tf_op jit(solution)/shard_map/ppermute | solution.py:330
  23.9 10.7 %collective-permute-start.6 = (bf16[2,128,1024]{2,1,0:T(8,128)(2,1)S(1)}, bf16[2,128,1024]{2,1,0:T(8,128)(2,1)S(1)}, u32[]{:S(2)}, u32[]{:S(2)}) collective-permute-start(bf16[2,128,1024]{2,1,0:T(8,128)(2,1)S(1)} %pad_maximum_fusion.1), channel_id=1, source_target_pairs={{0,16},{1,9},{2,18},{3,11},{4,20},{5,13},{6,22},{7,15},{8,24},{9,1... | collective-permute-start | bytes 1572872 | tf_op jit(solution)/shard_map/ppermute | solution.py:343
  26.1 8.5 %collective-permute-start.9 = (bf16[2,256,128]{2,1,0:T(8,128)(2,1)S(1)}, bf16[2,256,128]{2,1,0:T(8,128)(2,1)S(1)}, u32[]{:S(2)}, u32[]{:S(2)}) collective-permute-start(bf16[2,256,128]{2,1,0:T(8,128)(2,1)S(1)} %slice.45), channel_id=1, source_target_pairs={{0,16},{1,9},{2,18},{3,11},{4,20},{5,13},{6,22},{7,15},{8,24},{9,1... | collective-permute-start | bytes 393224 | tf_op jit(solution)/shard_map/ppermute | solution.py:343
  28.5 6.6 %collective-permute-start.17 = (bf16[128,256]{1,0:T(8,128)(2,1)S(1)}, bf16[128,256]{1,0:T(8,128)(2,1)S(1)}, u32[]{:S(2)}, u32[]{:S(2)}) collective-permute-start(bf16[128,256]{1,0:T(8,128)(2,1)S(1)} %add_add_fusion), channel_id=1, source_target_pairs={{0,2},{1,3},{2,0},{3,1},{4,6},{5,7},{6,4},{7,5},{8,10},{9,11},{10,... | collective-permute-start | bytes 196616 | tf_op jit(solution)/shard_map/ppermute | solution.py:330
  30.1 7.8 %collective-permute-start.18 = (bf16[128,256]{1,0:T(8,128)(2,1)S(1)}, bf16[128,256]{1,0:T(8,128)(2,1)S(1)}, u32[]{:S(2)}, u32[]{:S(2)}) collective-permute-start(bf16[128,256]{1,0:T(8,128)(2,1)S(1)} %add_add_fusion), channel_id=1, source_target_pairs={{0,4},{1,5},{2,6},{3,7},{4,0},{5,1},{6,2},{7,3},{8,12},{9,13},{10,... | collective-permute-start | bytes 196616 | tf_op jit(solution)/shard_map/ppermute | solution.py:330
  31.4 6.5 %collective-permute-start.19 = (bf16[128,256]{1,0:T(8,128)(2,1)S(1)}, bf16[128,256]{1,0:T(8,128)(2,1)S(1)}, u32[]{:S(2)}, u32[]{:S(2)}) collective-permute-start(bf16[128,256]{1,0:T(8,128)(2,1)S(1)} %add_add_fusion), channel_id=1, source_target_pairs={{0,6},{1,7},{2,4},{3,5},{4,2},{5,3},{6,0},{7,1},{8,14},{9,15},{10,... | collective-permute-start | bytes 196616 | tf_op jit(solution)/shard_map/ppermute | solution.py:330
  34.6 5.0 %collective-permute-start.7 = (bf16[1,128,1024]{2,1,0:T(8,128)(2,1)S(1)}, bf16[1,128,1024]{2,1,0:T(8,128)(2,1)S(1)}, u32[]{:S(2)}, u32[]{:S(2)}) collective-permute-start(bf16[1,128,1024]{2,1,0:T(8,128)(2,1)S(1)} %collective-permute-done.5.refs_1_), channel_id=1, source_target_pairs={{0,1},{1,0},{2,3},{3,2},{4,5},{5,4},{6,7},{7,6},{8,9},{9,8},{10,11... | collective-permute-start | bytes 786440 | tf_op jit(solution)/shard_map/ppermute | solution.py:327
  34.6 5.0 %collective-permute-start.8 = (bf16[2,128,1024]{2,1,0:T(8,128)(2,1)S(1)}, bf16[2,128,1024]{2,1,0:T(8,128)(2,1)S(1)}, u32[]{:S(2)}, u32[]{:S(2)}) collective-permute-start(bf16[2,128,1024]{2,1,0:T(8,128)(2,1)S(1)} %collective-permute-done.6.refs_2_), channel_id=1, source_target_pairs={{0,1},{1,0},{2,3},{3,2},{4,5},{5,4},{6,7},{7,6},{8,9},{9,8},{10,11... | collective-permute-start | bytes 1572872 | tf_op jit(solution)/shard_map/ppermute | solution.py:327
  35.2 4.3 %collective-permute-start.10 = (bf16[1,256,128]{2,1,0:T(8,128)(2,1)S(1)}, bf16[1,256,128]{2,1,0:T(8,128)(2,1)S(1)}, u32[]{:S(2)}, u32[]{:S(2)}) collective-permute-start(bf16[1,256,128]{2,1,0:T(8,128)(2,1)S(1)} %slice.46), channel_id=1, source_target_pairs={{0,8},{1,17},{2,10},{3,19},{4,12},{5,21},{6,14},{7,23},{8,0},{9,25... | collective-permute-start | bytes 196616 | tf_op jit(solution)/shard_map/ppermute | solution.py:343
  37.9 24.0 %collective-permute-start.22 = (bf16[1,4,128,256]{3,2,1,0:T(8,128)(2,1)S(1)}, bf16[1,4,128,256]{3,2,1,0:T(8,128)(2,1)S(1)}, u32[]{:S(2)}, u32[]{:S(2)}) collective-permute-start(bf16[1,4,128,256]{3,2,1,0:T(8,128)(2,1)S(1)} %maximum_bitcast_fusion.refs_0_), channel_id=1, source_target_pairs={{0,1},{1,0},{2,3},{3,2},{4,5},{5,4},{6,7},{7,6},{8,9},{9,8},{10,11... | collective-permute-start | bytes 786440 | tf_op jit(solution)/shard_map/ppermute | solution.py:327
  39.6 6.5 %collective-permute-start.20 = (bf16[1,4,128,256]{3,2,1,0:T(8,128)(2,1)S(1)}, bf16[1,4,128,256]{3,2,1,0:T(8,128)(2,1)S(1)}, u32[]{:S(2)}, u32[]{:S(2)}) collective-permute-start(bf16[1,4,128,256]{3,2,1,0:T(8,128)(2,1)S(1)} %maximum_bitcast_fusion.refs_0_), channel_id=1, source_target_pairs={{0,8},{1,17},{2,10},{3,19},{4,12},{5,21},{6,14},{7,23},{8,0},{9,25... | collective-permute-start | bytes 786440 | tf_op jit(solution)/shard_map/ppermute | solution.py:343
  46.1 11.8 %collective-permute-start.21 = (bf16[2,4,128,256]{3,2,1,0:T(8,128)(2,1)S(1)}, bf16[2,4,128,256]{3,2,1,0:T(8,128)(2,1)S(1)}, u32[]{:S(2)}, u32[]{:S(2)}) collective-permute-start(bf16[2,4,128,256]{3,2,1,0:T(8,128)(2,1)S(1)} %pad_maximum_fusion.3), channel_id=1, source_target_pairs={{0,16},{1,9},{2,18},{3,11},{4,20},{5,13},{6,22},{7,15},{8,24},{9,1... | collective-permute-start | bytes 1572872 | tf_op jit(solution)/shard_map/ppermute | solution.py:343
  48.1 7.8 %collective-permute-start.11 = (bf16[256,128]{1,0:T(8,128)(2,1)S(1)}, bf16[256,128]{1,0:T(8,128)(2,1)S(1)}, u32[]{:S(2)}, u32[]{:S(2)}) collective-permute-start(bf16[256,128]{1,0:T(8,128)(2,1)S(1)} %get-tuple-element.41), channel_id=1, source_target_pairs={{0,8},{8,0},{16,24},{24,16},{1,9},{9,1},{17,25},{25,17},{2,10},{10... | collective-permute-start | bytes 196616 | tf_op jit(solution)/shard_map/ppermute | solution.py:333
  49.6 8.3 %collective-permute-start.12 = (bf16[256,128]{1,0:T(8,128)(2,1)S(1)}, bf16[256,128]{1,0:T(8,128)(2,1)S(1)}, u32[]{:S(2)}, u32[]{:S(2)}) collective-permute-start(bf16[256,128]{1,0:T(8,128)(2,1)S(1)} %get-tuple-element.41), channel_id=1, source_target_pairs={{0,16},{8,24},{16,0},{24,8},{1,17},{9,25},{17,1},{25,9},{2,18},{10... | collective-permute-start | bytes 196616 | tf_op jit(solution)/shard_map/ppermute | solution.py:333
  50.1 7.9 %collective-permute-start.13 = (bf16[256,128]{1,0:T(8,128)(2,1)S(1)}, bf16[256,128]{1,0:T(8,128)(2,1)S(1)}, u32[]{:S(2)}, u32[]{:S(2)}) collective-permute-start(bf16[256,128]{1,0:T(8,128)(2,1)S(1)} %get-tuple-element.41), channel_id=1, source_target_pairs={{0,24},{8,16},{16,8},{24,0},{1,25},{9,17},{17,9},{25,1},{2,26},{10... | collective-permute-start | bytes 196616 | tf_op jit(solution)/shard_map/ppermute | solution.py:333
  58.0 4.0 %collective-permute-start.24 = (bf16[2,4,128,256]{3,2,1,0:T(8,128)(2,1)S(1)}, bf16[2,4,128,256]{3,2,1,0:T(8,128)(2,1)S(1)}, u32[]{:S(2)}, u32[]{:S(2)}) collective-permute-start(bf16[2,4,128,256]{3,2,1,0:T(8,128)(2,1)S(1)} %collective-permute-done.21.refs_2_), channel_id=1, source_target_pairs={{0,1},{1,0},{2,3},{3,2},{4,5},{5,4},{6,7},{7,6},{8,9},{9,8},{10,11... | collective-permute-start | bytes 1572872 | tf_op jit(solution)/shard_map/ppermute | solution.py:327
  58.1 3.9 %collective-permute-start.23 = (bf16[1,4,128,256]{3,2,1,0:T(8,128)(2,1)S(1)}, bf16[1,4,128,256]{3,2,1,0:T(8,128)(2,1)S(1)}, u32[]{:S(2)}, u32[]{:S(2)}) collective-permute-start(bf16[1,4,128,256]{3,2,1,0:T(8,128)(2,1)S(1)} %collective-permute-done.20.refs_1_), channel_id=1, source_target_pairs={{0,1},{1,0},{2,3},{3,2},{4,5},{5,4},{6,7},{7,6},{8,9},{9,8},{10,11... | collective-permute-start | bytes 786440 | tf_op jit(solution)/shard_map/ppermute | solution.py:327
  (9 other events, 65.0 us)

commit v5 on v4

--- a/solution.py
+++ b/solution.py
@@ -372,7 +372,7 @@
         return lax.dynamic_slice_in_dim(partial, (row_at ^ away) * part, part, axis=1)
 
     chunks = jnp.stack([chunk_of(number) for number in range(rows)])
-    block, chunks = lax.optimization_barrier((keep[0], chunks))
+    block = keep[0]
     sums = []
     for step in reversed(range(steps)):
         kept = 1 << step
@@ -391,10 +391,10 @@
     for level in range(1, deep):
         block = block + to_deep(keep[level], level)
     mine_sel = jnp.stack([block] + [to_deep(block, level) for level in range(1, deep)])
-    mine_e = over_rows(mine_sel, lambda step: sums[step] if step else (sums[step], sib_v))
+    mine_e = over_rows(mine_sel, lambda step: (sums[-1], sib_v))
     sib_e = [to_core(x) for x in mine_e]
 
-    weights = precise(factor, projected).astype(BF16)
+    weights = jnp.dot(factor, projected, precision=lax.Precision.HIGH, preferred_element_type=F32).astype(BF16)
     all_weights = jnp.zeros((size, wide), BF16)
     for peer in range(rows):
         arrived = to_row(weights, peer) if peer else weights

time: 65.4 us -> 65.3 us (level)
  other arithmetic: 0.44 us -> 1.28 us
    convert_element_type x1, other arithmetic: 0.01 us -> 0.88 us  [per_device(): own = own.astype(BF16)]
    ppermute x7, waiting for transfers between devices: 1.16 us -> 0.29 us  [to_core(): return lax.ppermute(x, 'col', [(i, i ^ 1) for i in range(cols)])]
    unnamed x16 -> x12, local copies, waits for them, and re-layouts: 2.3 us -> 2.29 us
  transfers between devices with their start and end apart: 25 -> 25, of which waited for: 9 -> 8; matrix products, arithmetic and copies ran while one was open for 5% -> 6% of each run, Pallas kernels for 16% -> 16%
where the time goes in v5:
time: 65.3 us; the launch traced here: 65.1 us
  starting transfers between devices  28.1 us (43%)
  Pallas kernels  14.9 us (23%)
  waiting for transfers between devices  14.9 us (23%)
  matrix products  2.53 us (4%)
  local copies, waits for them, and re-layouts  2.47 us (4%)
  other arithmetic  1.28 us (2%)
  between operations  0.97 us (1%)
    ppermute x9, starting transfers between devices, to_deep(): return lax.ppermute(x, 'col', [(i, i ^ 2 * level) for i in range(cols)])  14.4 us
    ppermute x9, waiting for transfers between devices, to_deep(): return lax.ppermute(x, 'col', [(i, i ^ 2 * level) for i in range(cols)])  8.95 us
    ppermute x6, starting transfers between devices, over_step(): return lax.ppermute(x, ('row', 'col'), pairs)  8.29 us
    pallas_call x1, Pallas kernels, factor_of(): pl.pallas_call(functools.partial(factor_kernel, len(mine)), out_shape=jax...  4.9 us
    pallas_call x1, Pallas kernels, sort(): pl.pallas_call(functools.partial(sort_kernel, len(mine)), out_shape=(jax....  4.26 us
    ppermute x6, waiting for transfers between devices, over_step(): return lax.ppermute(x, ('row', 'col'), pairs)  3.81 us
    ppermute x3, starting transfers between devices, to_row(): return lax.ppermute(x, 'row', [(i, i ^ peer) for i in range(rows)])  3.55 us
    pallas_call x1, Pallas kernels, modes_in_two(): pl.pallas_call(second_kernel, out_shape=jax.ShapeDtypeStruct((dofs, width...  3.23 us
  transfers between devices with their start and end apart: 25, of which 8 were waited for; matrix products, arithmetic and copies ran while one was open for 6% of the time, Pallas kernels for 16%

profile of v5, /device:TPU:0, one launch (start us, length us, event | category | flops | bytes accessed | tf_op | source)
XLA Modules:
  0.0 65.1 jit_solution(1285240687303570814)
XLA Ops:
  0.7 1.6 %copy-done = f32[1024,512]{1,0:T(8,128)S(1)} copy-done((f32[1024,512]{1,0:T(8,128)S(1)}, f32[1024,512]{1,0:T(8,128)}, u32[]{:S(2)}) %copy-start) | copy-done | bytes 2097176
  5.7 2.9 %collective-permute-start.1 = (bf16[32,1024]{1,0:T(8,128)(2,1)S(1)}, bf16[32,1024]{1,0:T(8,128)(2,1)S(1)}, u32[]{:S(2)}, u32[]{:S(2)}) collective-permute-start(bf16[32,1024]{1,0:T(8,128)(2,1)S(1)} %add_convert_fusion), channel_id=1, source_target_pairs={{0,2},{1,3},{2,0},{3,1},{4,6},{5,7},{6,4},{7,5},{8,10},{9,11},{10,... | collective-permute-start | bytes 196616 | tf_op jit(solution)/shard_map/ppermute | solution.py:330
  8.7 2.6 %collective-permute-start.2 = (bf16[32,1024]{1,0:T(8,128)(2,1)S(1)}, bf16[32,1024]{1,0:T(8,128)(2,1)S(1)}, u32[]{:S(2)}, u32[]{:S(2)}) collective-permute-start(bf16[32,1024]{1,0:T(8,128)(2,1)S(1)} %add_convert_fusion), channel_id=1, source_target_pairs={{0,4},{1,5},{2,6},{3,7},{4,0},{5,1},{6,2},{7,3},{8,12},{9,13},{10,... | collective-permute-start | bytes 196616 | tf_op jit(solution)/shard_map/ppermute | solution.py:330
  11.3 4.9 %collective-permute-done.2 = bf16[32,1024]{1,0:T(8,128)(2,1)S(1)} collective-permute-done((bf16[32,1024]{1,0:T(8,128)(2,1)S(1)}, bf16[32,1024]{1,0:T(8,128)(2,1)S(1)}, u32[]{:S(2)}, u32[]{:S(2)}) %collective-permute-start.2) | collective-permute-done | bytes 65568 | tf_op jit(solution)/shard_map/ppermute | solution.py:330
  17.6 1.6 %collective-permute-start.5 = (bf16[1,128,1024]{2,1,0:T(8,128)(2,1)S(1)}, bf16[1,128,1024]{2,1,0:T(8,128)(2,1)S(1)}, u32[]{:S(2)}, u32[]{:S(2)}) collective-permute-start(bf16[1,128,1024]{2,1,0:T(8,128)(2,1)S(1)} %bitcast.44), channel_id=1, source_target_pairs={{0,8},{1,17},{2,10},{3,19},{4,12},{5,21},{6,14},{7,23},{8,0},{9,25... | collective-permute-start | bytes 786440 | tf_op jit(solution)/shard_map/ppermute | solution.py:343
  20.1 1.7 %collective-permute-start.15 = (bf16[128,256]{1,0:T(8,128)(2,1)S(1)}, bf16[128,256]{1,0:T(8,128)(2,1)S(1)}, u32[]{:S(2)}, u32[]{:S(2)}) collective-permute-start(bf16[128,256]{1,0:T(8,128)(2,1)S(1)} %get-tuple-element.34), channel_id=1, source_target_pairs={{0,4},{1,5},{2,6},{3,7},{4,0},{5,1},{6,2},{7,3},{8,12},{9,13},{10,... | collective-permute-start | bytes 196616 | tf_op jit(solution)/shard_map/ppermute | solution.py:330
  21.8 1.8 %collective-permute-start.16 = (bf16[128,256]{1,0:T(8,128)(2,1)S(1)}, bf16[128,256]{1,0:T(8,128)(2,1)S(1)}, u32[]{:S(2)}, u32[]{:S(2)}) collective-permute-start(bf16[128,256]{1,0:T(8,128)(2,1)S(1)} %get-tuple-element.33), channel_id=1, source_target_pairs={{0,6},{1,7},{2,4},{3,5},{4,2},{5,3},{6,0},{7,1},{8,14},{9,15},{10,... | collective-permute-start | bytes 196616 | tf_op jit(solution)/shard_map/ppermute | solution.py:330
  24.1 1.6 %collective-permute-start.6 = (bf16[2,128,1024]{2,1,0:T(8,128)(2,1)S(1)}, bf16[2,128,1024]{2,1,0:T(8,128)(2,1)S(1)}, u32[]{:S(2)}, u32[]{:S(2)}) collective-permute-start(bf16[2,128,1024]{2,1,0:T(8,128)(2,1)S(1)} %pad_maximum_fusion.1), channel_id=1, source_target_pairs={{0,16},{1,9},{2,18},{3,11},{4,20},{5,13},{6,22},{7,15},{8,24},{9,1... | collective-permute-start | bytes 1572872 | tf_op jit(solution)/shard_map/ppermute | solution.py:343
  26.4 2.1 %collective-permute-done.15 = bf16[128,256]{1,0:T(8,128)(2,1)S(1)} collective-permute-done((bf16[128,256]{1,0:T(8,128)(2,1)S(1)}, bf16[128,256]{1,0:T(8,128)(2,1)S(1)}, u32[]{:S(2)}, u32[]{:S(2)}) %collective-permute-start.15) | collective-permute-done | bytes 65568 | tf_op jit(solution)/shard_map/ppermute | solution.py:330
  28.5 1.4 %collective-permute-start.17 = (bf16[128,256]{1,0:T(8,128)(2,1)S(1)}, bf16[128,256]{1,0:T(8,128)(2,1)S(1)}, u32[]{:S(2)}, u32[]{:S(2)}) collective-permute-start(bf16[128,256]{1,0:T(8,128)(2,1)S(1)} %fusion.6), channel_id=1, source_target_pairs={{0,2},{1,3},{2,0},{3,1},{4,6},{5,7},{6,4},{7,5},{8,10},{9,11},{10,... | collective-permute-start | bytes 196616 | tf_op jit(solution)/shard_map/ppermute | solution.py:330
  31.1 1.8 %collective-permute-start.19 = (bf16[128,256]{1,0:T(8,128)(2,1)S(1)}, bf16[128,256]{1,0:T(8,128)(2,1)S(1)}, u32[]{:S(2)}, u32[]{:S(2)}) collective-permute-start(bf16[128,256]{1,0:T(8,128)(2,1)S(1)} %fusion.6), channel_id=1, source_target_pairs={{0,6},{1,7},{2,4},{3,5},{4,2},{5,3},{6,0},{7,1},{8,14},{9,15},{10,... | collective-permute-start | bytes 196616 | tf_op jit(solution)/shard_map/ppermute | solution.py:330
  33.0 1.8 %collective-permute-done.9 = bf16[2,256,128]{2,1,0:T(8,128)(2,1)S(1)} collective-permute-done((bf16[2,256,128]{2,1,0:T(8,128)(2,1)S(1)}, bf16[2,256,128]{2,1,0:T(8,128)(2,1)S(1)}, u32[]{:S(2)}, u32[]{:S(2)}) %collective-permute-start.9) | collective-permute-done | bytes 131104 | tf_op jit(solution)/shard_map/ppermute | solution.py:343
  35.4 1.5 %collective-permute-start.10 = (bf16[1,256,128]{2,1,0:T(8,128)(2,1)S(1)}, bf16[1,256,128]{2,1,0:T(8,128)(2,1)S(1)}, u32[]{:S(2)}, u32[]{:S(2)}) collective-permute-start(bf16[1,256,128]{2,1,0:T(8,128)(2,1)S(1)} %slice.37), channel_id=1, source_target_pairs={{0,8},{1,17},{2,10},{3,19},{4,12},{5,21},{6,14},{7,23},{8,0},{9,25... | collective-permute-start | bytes 196616 | tf_op jit(solution)/shard_map/ppermute | solution.py:343
  37.7 1.9 %collective-permute-done.10 = bf16[1,256,128]{2,1,0:T(8,128)(2,1)S(1)} collective-permute-done((bf16[1,256,128]{2,1,0:T(8,128)(2,1)S(1)}, bf16[1,256,128]{2,1,0:T(8,128)(2,1)S(1)}, u32[]{:S(2)}, u32[]{:S(2)}) %collective-permute-start.10) | collective-permute-done | bytes 65568 | tf_op jit(solution)/shard_map/ppermute | solution.py:343
  39.8 1.5 %collective-permute-start.20 = (bf16[1,4,128,256]{3,2,1,0:T(8,128)(2,1)S(1)}, bf16[1,4,128,256]{3,2,1,0:T(8,128)(2,1)S(1)}, u32[]{:S(2)}, u32[]{:S(2)}) collective-permute-start(bf16[1,4,128,256]{3,2,1,0:T(8,128)(2,1)S(1)} %maximum_bitcast_fusion.refs_0_), channel_id=1, source_target_pairs={{0,8},{1,17},{2,10},{3,19},{4,12},{5,21},{6,14},{7,23},{8,0},{9,25... | collective-permute-start | bytes 786440 | tf_op jit(solution)/shard_map/ppermute | solution.py:343
  41.3 4.9 %shard_map.78.factor_ref = f32[256,256]{1,0:T(8,128)S(1)} custom-call(s32[1,256]{1,0:T(1,128)S(1)} %fusion.7.place_ref, bf16[1,128,1024]{2,1,0:T(8,128)(2,1)S(1)} %bitcast.46, bf16[1,128,1024]{2,1,0:T(8,128)(2,1)S(1)} %collective-permute-done.5.refs_1_, bf16[2,128,1024]{2,1,0:T(8,128)(2,1)S(1)} %collective-permute-done.6.refs_2_, ...), custom_call_target="tpu_custom_call" | custom-call | flops 3758096384 | bytes 2621440 | tf_op jit(solution)/shard_map/pallas_call | solution.py:139
  46.2 1.6 %collective-permute-start.21 = (bf16[2,4,128,256]{3,2,1,0:T(8,128)(2,1)S(1)}, bf16[2,4,128,256]{3,2,1,0:T(8,128)(2,1)S(1)}, u32[]{:S(2)}, u32[]{:S(2)}) collective-permute-start(bf16[2,4,128,256]{3,2,1,0:T(8,128)(2,1)S(1)} %pad_maximum_fusion.2), channel_id=1, source_target_pairs={{0,16},{1,9},{2,18},{3,11},{4,20},{5,13},{6,22},{7,15},{8,24},{9,1... | collective-permute-start | bytes 1572872 | tf_op jit(solution)/shard_map/ppermute | solution.py:343
  48.2 1.5 %collective-permute-start.11 = (bf16[256,128]{1,0:T(8,128)(2,1)S(1)}, bf16[256,128]{1,0:T(8,128)(2,1)S(1)}, u32[]{:S(2)}, u32[]{:S(2)}) collective-permute-start(bf16[256,128]{1,0:T(8,128)(2,1)S(1)} %get-tuple-element.36), channel_id=1, source_target_pairs={{0,8},{8,0},{16,24},{24,16},{1,9},{9,1},{17,25},{25,17},{2,10},{10... | collective-permute-start | bytes 196616 | tf_op jit(solution)/shard_map/ppermute | solution.py:333
  50.2 1.5 %collective-permute-start.13 = (bf16[256,128]{1,0:T(8,128)(2,1)S(1)}, bf16[256,128]{1,0:T(8,128)(2,1)S(1)}, u32[]{:S(2)}, u32[]{:S(2)}) collective-permute-start(bf16[256,128]{1,0:T(8,128)(2,1)S(1)} %get-tuple-element.36), channel_id=1, source_target_pairs={{0,24},{8,16},{16,8},{24,0},{1,25},{9,17},{17,9},{25,1},{2,26},{10... | collective-permute-start | bytes 196616 | tf_op jit(solution)/shard_map/ppermute | solution.py:333
  51.7 4.3 %shard_map.79 = (bf16[1024,4096]{1,0:T(8,128)(2,1)S(1)}, bf16[256,4096]{1,0:T(8,128)(2,1)S(1)}, bf16[1024,256]{1,0:T(8,128)(2,1)S(1)}) custom-call(s32[3]{0:T(128)S(1)} %pad_add_fusion.here_ref, s32[32]{0:T(128)S(1)} %copy-done.3, bf16[1024,4096]{1,0:T(8,128)(2,1)S(1)} %bitcast.42, bf16[1,128,1024]{2,1,0:T(8,128)(2,1)S(1)} %bitcast.47, ...), custom_call_target="tpu_custom_call" | custom-call | flops 2147483648 | bytes 16777216 | tf_op jit(solution)/shard_map/pallas_call | solution.py:251
  56.0 1.8 %collective-permute-done.12 = bf16[256,128]{1,0:T(8,128)(2,1)S(1)} collective-permute-done((bf16[256,128]{1,0:T(8,128)(2,1)S(1)}, bf16[256,128]{1,0:T(8,128)(2,1)S(1)}, u32[]{:S(2)}, u32[]{:S(2)}) %collective-permute-start.12) | collective-permute-done | bytes 65568 | tf_op jit(solution)/shard_map/ppermute | solution.py:333
  58.5 1.8 %convolution_subtract_fusion = f32[1024,512]{1,0:T(8,128)} fusion(f32[1024,512]{1,0:T(8,128)S(1)} %copy-done.1, bf16[256,512]{1,0:T(8,128)(2,1)S(1)} %constant_dynamic-update-slice_fusion, bf16[128,1024]{1,0:T(8,128)(2,1)S(1)} %bitcast.49, bf16[128,1024]{1,0:T(8,128)(2,1)S(1)} %pad_maximum_fusion.5), kind=kOutput, calls=%fused_computation | convolution fusion | flops 270008320 | bytes 4980736 | tf_op jit(solution)/shard_map/dot_general | solution.py:402
  60.3 1.5 %shard_map.80 = (f32[1024,256]{1,0:T(8,128)S(1)}, f32[256,256]{1,0:T(8,128)S(1)}) custom-call(bf16[1024,4096]{1,0:T(8,128)(2,1)S(1)} %get-tuple-element.20.ritz_ref, bf16[256,4096]{1,0:T(8,128)(2,1)S(1)} %get-tuple-element.21.vec_ref, bf16[1,4,128,256]{3,2,1,0:T(8,128)(2,1)S(1)} %maximum_bitcast_fusion.refs_0_, ...), custom_call_target="tpu_custom_call" | custom-call | flops 1342177280 | bytes 4194304 | tf_op jit(solution)/shard_map/pallas_call | solution.py:299
  61.9 3.2 %shard_map.81 = bf16[1024,256]{1,0:T(8,128)(2,1)} custom-call(bf16[1024,4096]{1,0:T(8,128)(2,1)S(1)} %get-tuple-element.20.ritz_ref, bf16[256,4096]{1,0:T(8,128)(2,1)S(1)} %get-tuple-element.21.vec_ref, bf16[1024,256]{1,0:T(8,128)(2,1)S(1)} %get-tuple-element.22.spread_ref, f32[256,256]{1,0:T(8,128)S(1)} %shard_map.78.factor_ref, ...), custom_call_target="tpu_custom_call" | custom-call | flops 1342177280 | bytes 4194304 | tf_op jit(solution)/shard_map/pallas_call | solution.py:307
  (67 shorter events, 11.2 us)
Async XLA Ops:
  5.7 5.6 %collective-permute-start.1 = (bf16[32,1024]{1,0:T(8,128)(2,1)S(1)}, bf16[32,1024]{1,0:T(8,128)(2,1)S(1)}, u32[]{:S(2)}, u32[]{:S(2)}) collective-permute-start(bf16[32,1024]{1,0:T(8,128)(2,1)S(1)} %add_convert_fusion), channel_id=1, source_target_pairs={{0,2},{1,3},{2,0},{3,1},{4,6},{5,7},{6,4},{7,5},{8,10},{9,11},{10,... | collective-permute-start | bytes 196616 | tf_op jit(solution)/shard_map/ppermute | solution.py:330
  8.7 7.5 %collective-permute-start.2 = (bf16[32,1024]{1,0:T(8,128)(2,1)S(1)}, bf16[32,1024]{1,0:T(8,128)(2,1)S(1)}, u32[]{:S(2)}, u32[]{:S(2)}) collective-permute-start(bf16[32,1024]{1,0:T(8,128)(2,1)S(1)} %add_convert_fusion), channel_id=1, source_target_pairs={{0,4},{1,5},{2,6},{3,7},{4,0},{5,1},{6,2},{7,3},{8,12},{9,13},{10,... | collective-permute-start | bytes 196616 | tf_op jit(solution)/shard_map/ppermute | solution.py:330
  11.2 6.2 %collective-permute-start.3 = (bf16[32,1024]{1,0:T(8,128)(2,1)S(1)}, bf16[32,1024]{1,0:T(8,128)(2,1)S(1)}, u32[]{:S(2)}, u32[]{:S(2)}) collective-permute-start(bf16[32,1024]{1,0:T(8,128)(2,1)S(1)} %add_convert_fusion), channel_id=1, source_target_pairs={{0,6},{1,7},{2,4},{3,5},{4,2},{5,3},{6,0},{7,1},{8,14},{9,15},{10,... | collective-permute-start | bytes 196616 | tf_op jit(solution)/shard_map/ppermute | solution.py:330
  17.4 6.2 %collective-permute-start.4 = (bf16[1,128,1024]{2,1,0:T(8,128)(2,1)S(1)}, bf16[1,128,1024]{2,1,0:T(8,128)(2,1)S(1)}, u32[]{:S(2)}, u32[]{:S(2)}) collective-permute-start(bf16[1,128,1024]{2,1,0:T(8,128)(2,1)S(1)} %bitcast.43), channel_id=1, source_target_pairs={{0,1},{1,0},{2,3},{3,2},{4,5},{5,4},{6,7},{7,6},{8,9},{9,8},{10,11... | collective-permute-start | bytes 786440 | tf_op jit(solution)/shard_map/ppermute | solution.py:327
  17.6 6.5 %collective-permute-start.5 = (bf16[1,128,1024]{2,1,0:T(8,128)(2,1)S(1)}, bf16[1,128,1024]{2,1,0:T(8,128)(2,1)S(1)}, u32[]{:S(2)}, u32[]{:S(2)}) collective-permute-start(bf16[1,128,1024]{2,1,0:T(8,128)(2,1)S(1)} %bitcast.44), channel_id=1, source_target_pairs={{0,8},{1,17},{2,10},{3,19},{4,12},{5,21},{6,14},{7,23},{8,0},{9,25... | collective-permute-start | bytes 786440 | tf_op jit(solution)/shard_map/ppermute | solution.py:343
  19.2 7.2 %collective-permute-start.14 = (bf16[128,256]{1,0:T(8,128)(2,1)S(1)}, bf16[128,256]{1,0:T(8,128)(2,1)S(1)}, u32[]{:S(2)}, u32[]{:S(2)}) collective-permute-start(bf16[128,256]{1,0:T(8,128)(2,1)S(1)} %get-tuple-element.32), channel_id=1, source_target_pairs={{0,2},{1,3},{2,0},{3,1},{4,6},{5,7},{6,4},{7,5},{8,10},{9,11},{10,... | collective-permute-start | bytes 196616 | tf_op jit(solution)/shard_map/ppermute | solution.py:330
  20.1 8.4 %collective-permute-start.15 = (bf16[128,256]{1,0:T(8,128)(2,1)S(1)}, bf16[128,256]{1,0:T(8,128)(2,1)S(1)}, u32[]{:S(2)}, u32[]{:S(2)}) collective-permute-start(bf16[128,256]{1,0:T(8,128)(2,1)S(1)} %get-tuple-element.34), channel_id=1, source_target_pairs={{0,4},{1,5},{2,6},{3,7},{4,0},{5,1},{6,2},{7,3},{8,12},{9,13},{10,... | collective-permute-start | bytes 196616 | tf_op jit(solution)/shard_map/ppermute | solution.py:330
  21.8 6.7 %collective-permute-start.16 = (bf16[128,256]{1,0:T(8,128)(2,1)S(1)}, bf16[128,256]{1,0:T(8,128)(2,1)S(1)}, u32[]{:S(2)}, u32[]{:S(2)}) collective-permute-start(bf16[128,256]{1,0:T(8,128)(2,1)S(1)} %get-tuple-element.33), channel_id=1, source_target_pairs={{0,6},{1,7},{2,4},{3,5},{4,2},{5,3},{6,0},{7,1},{8,14},{9,15},{10,... | collective-permute-start | bytes 196616 | tf_op jit(solution)/shard_map/ppermute | solution.py:330
  24.1 10.7 %collective-permute-start.6 = (bf16[2,128,1024]{2,1,0:T(8,128)(2,1)S(1)}, bf16[2,128,1024]{2,1,0:T(8,128)(2,1)S(1)}, u32[]{:S(2)}, u32[]{:S(2)}) collective-permute-start(bf16[2,128,1024]{2,1,0:T(8,128)(2,1)S(1)} %pad_maximum_fusion.1), channel_id=1, source_target_pairs={{0,16},{1,9},{2,18},{3,11},{4,20},{5,13},{6,22},{7,15},{8,24},{9,1... | collective-permute-start | bytes 1572872 | tf_op jit(solution)/shard_map/ppermute | solution.py:343
  25.8 9.0 %collective-permute-start.9 = (bf16[2,256,128]{2,1,0:T(8,128)(2,1)S(1)}, bf16[2,256,128]{2,1,0:T(8,128)(2,1)S(1)}, u32[]{:S(2)}, u32[]{:S(2)}) collective-permute-start(bf16[2,256,128]{2,1,0:T(8,128)(2,1)S(1)} %pad_maximum_fusion.6), channel_id=1, source_target_pairs={{0,16},{1,9},{2,18},{3,11},{4,20},{5,13},{6,22},{7,15},{8,24},{9,1... | collective-permute-start | bytes 393224 | tf_op jit(solution)/shard_map/ppermute | solution.py:343
  28.5 6.9 %collective-permute-start.17 = (bf16[128,256]{1,0:T(8,128)(2,1)S(1)}, bf16[128,256]{1,0:T(8,128)(2,1)S(1)}, u32[]{:S(2)}, u32[]{:S(2)}) collective-permute-start(bf16[128,256]{1,0:T(8,128)(2,1)S(1)} %fusion.6), channel_id=1, source_target_pairs={{0,2},{1,3},{2,0},{3,1},{4,6},{5,7},{6,4},{7,5},{8,10},{9,11},{10,... | collective-permute-start | bytes 196616 | tf_op jit(solution)/shard_map/ppermute | solution.py:330
  29.9 7.7 %collective-permute-start.18 = (bf16[128,256]{1,0:T(8,128)(2,1)S(1)}, bf16[128,256]{1,0:T(8,128)(2,1)S(1)}, u32[]{:S(2)}, u32[]{:S(2)}) collective-permute-start(bf16[128,256]{1,0:T(8,128)(2,1)S(1)} %fusion.6), channel_id=1, source_target_pairs={{0,4},{1,5},{2,6},{3,7},{4,0},{5,1},{6,2},{7,3},{8,12},{9,13},{10,... | collective-permute-start | bytes 196616 | tf_op jit(solution)/shard_map/ppermute | solution.py:330
  31.1 6.5 %collective-permute-start.19 = (bf16[128,256]{1,0:T(8,128)(2,1)S(1)}, bf16[128,256]{1,0:T(8,128)(2,1)S(1)}, u32[]{:S(2)}, u32[]{:S(2)}) collective-permute-start(bf16[128,256]{1,0:T(8,128)(2,1)S(1)} %fusion.6), channel_id=1, source_target_pairs={{0,6},{1,7},{2,4},{3,5},{4,2},{5,3},{6,0},{7,1},{8,14},{9,15},{10,... | collective-permute-start | bytes 196616 | tf_op jit(solution)/shard_map/ppermute | solution.py:330
  34.8 5.0 %collective-permute-start.7 = (bf16[1,128,1024]{2,1,0:T(8,128)(2,1)S(1)}, bf16[1,128,1024]{2,1,0:T(8,128)(2,1)S(1)}, u32[]{:S(2)}, u32[]{:S(2)}) collective-permute-start(bf16[1,128,1024]{2,1,0:T(8,128)(2,1)S(1)} %collective-permute-done.5.refs_1_), channel_id=1, source_target_pairs={{0,1},{1,0},{2,3},{3,2},{4,5},{5,4},{6,7},{7,6},{8,9},{9,8},{10,11... | collective-permute-start | bytes 786440 | tf_op jit(solution)/shard_map/ppermute | solution.py:327
  34.8 5.0 %collective-permute-start.8 = (bf16[2,128,1024]{2,1,0:T(8,128)(2,1)S(1)}, bf16[2,128,1024]{2,1,0:T(8,128)(2,1)S(1)}, u32[]{:S(2)}, u32[]{:S(2)}) collective-permute-start(bf16[2,128,1024]{2,1,0:T(8,128)(2,1)S(1)} %collective-permute-done.6.refs_2_), channel_id=1, source_target_pairs={{0,1},{1,0},{2,3},{3,2},{4,5},{5,4},{6,7},{7,6},{8,9},{9,8},{10,11... | collective-permute-start | bytes 1572872 | tf_op jit(solution)/shard_map/ppermute | solution.py:327
  35.4 4.3 %collective-permute-start.10 = (bf16[1,256,128]{2,1,0:T(8,128)(2,1)S(1)}, bf16[1,256,128]{2,1,0:T(8,128)(2,1)S(1)}, u32[]{:S(2)}, u32[]{:S(2)}) collective-permute-start(bf16[1,256,128]{2,1,0:T(8,128)(2,1)S(1)} %slice.37), channel_id=1, source_target_pairs={{0,8},{1,17},{2,10},{3,19},{4,12},{5,21},{6,14},{7,23},{8,0},{9,25... | collective-permute-start | bytes 196616 | tf_op jit(solution)/shard_map/ppermute | solution.py:343
  37.7 24.2 %collective-permute-start.22 = (bf16[1,4,128,256]{3,2,1,0:T(8,128)(2,1)S(1)}, bf16[1,4,128,256]{3,2,1,0:T(8,128)(2,1)S(1)}, u32[]{:S(2)}, u32[]{:S(2)}) collective-permute-start(bf16[1,4,128,256]{3,2,1,0:T(8,128)(2,1)S(1)} %maximum_bitcast_fusion.refs_0_), channel_id=1, source_target_pairs={{0,1},{1,0},{2,3},{3,2},{4,5},{5,4},{6,7},{7,6},{8,9},{9,8},{10,11... | collective-permute-start | bytes 786440 | tf_op jit(solution)/shard_map/ppermute | solution.py:327
  39.8 6.4 %collective-permute-start.20 = (bf16[1,4,128,256]{3,2,1,0:T(8,128)(2,1)S(1)}, bf16[1,4,128,256]{3,2,1,0:T(8,128)(2,1)S(1)}, u32[]{:S(2)}, u32[]{:S(2)}) collective-permute-start(bf16[1,4,128,256]{3,2,1,0:T(8,128)(2,1)S(1)} %maximum_bitcast_fusion.refs_0_), channel_id=1, source_target_pairs={{0,8},{1,17},{2,10},{3,19},{4,12},{5,21},{6,14},{7,23},{8,0},{9,25... | collective-permute-start | bytes 786440 | tf_op jit(solution)/shard_map/ppermute | solution.py:343
  46.2 11.6 %collective-permute-start.21 = (bf16[2,4,128,256]{3,2,1,0:T(8,128)(2,1)S(1)}, bf16[2,4,128,256]{3,2,1,0:T(8,128)(2,1)S(1)}, u32[]{:S(2)}, u32[]{:S(2)}) collective-permute-start(bf16[2,4,128,256]{3,2,1,0:T(8,128)(2,1)S(1)} %pad_maximum_fusion.2), channel_id=1, source_target_pairs={{0,16},{1,9},{2,18},{3,11},{4,20},{5,13},{6,22},{7,15},{8,24},{9,1... | collective-permute-start | bytes 1572872 | tf_op jit(solution)/shard_map/ppermute | solution.py:343
  48.2 7.8 %collective-permute-start.11 = (bf16[256,128]{1,0:T(8,128)(2,1)S(1)}, bf16[256,128]{1,0:T(8,128)(2,1)S(1)}, u32[]{:S(2)}, u32[]{:S(2)}) collective-permute-start(bf16[256,128]{1,0:T(8,128)(2,1)S(1)} %get-tuple-element.36), channel_id=1, source_target_pairs={{0,8},{8,0},{16,24},{24,16},{1,9},{9,1},{17,25},{25,17},{2,10},{10... | collective-permute-start | bytes 196616 | tf_op jit(solution)/shard_map/ppermute | solution.py:333
  49.7 8.2 %collective-permute-start.12 = (bf16[256,128]{1,0:T(8,128)(2,1)S(1)}, bf16[256,128]{1,0:T(8,128)(2,1)S(1)}, u32[]{:S(2)}, u32[]{:S(2)}) collective-permute-start(bf16[256,128]{1,0:T(8,128)(2,1)S(1)} %get-tuple-element.36), channel_id=1, source_target_pairs={{0,16},{8,24},{16,0},{24,8},{1,17},{9,25},{17,1},{25,9},{2,18},{10... | collective-permute-start | bytes 196616 | tf_op jit(solution)/shard_map/ppermute | solution.py:333
  50.2 7.8 %collective-permute-start.13 = (bf16[256,128]{1,0:T(8,128)(2,1)S(1)}, bf16[256,128]{1,0:T(8,128)(2,1)S(1)}, u32[]{:S(2)}, u32[]{:S(2)}) collective-permute-start(bf16[256,128]{1,0:T(8,128)(2,1)S(1)} %get-tuple-element.36), channel_id=1, source_target_pairs={{0,24},{8,16},{16,8},{24,0},{1,25},{9,17},{17,9},{25,1},{2,26},{10... | collective-permute-start | bytes 196616 | tf_op jit(solution)/shard_map/ppermute | solution.py:333
  57.9 4.0 %collective-permute-start.24 = (bf16[2,4,128,256]{3,2,1,0:T(8,128)(2,1)S(1)}, bf16[2,4,128,256]{3,2,1,0:T(8,128)(2,1)S(1)}, u32[]{:S(2)}, u32[]{:S(2)}) collective-permute-start(bf16[2,4,128,256]{3,2,1,0:T(8,128)(2,1)S(1)} %collective-permute-done.21.refs_2_), channel_id=1, source_target_pairs={{0,1},{1,0},{2,3},{3,2},{4,5},{5,4},{6,7},{7,6},{8,9},{9,8},{10,11... | collective-permute-start | bytes 1572872 | tf_op jit(solution)/shard_map/ppermute | solution.py:327
  58.0 3.9 %collective-permute-start.23 = (bf16[1,4,128,256]{3,2,1,0:T(8,128)(2,1)S(1)}, bf16[1,4,128,256]{3,2,1,0:T(8,128)(2,1)S(1)}, u32[]{:S(2)}, u32[]{:S(2)}) collective-permute-start(bf16[1,4,128,256]{3,2,1,0:T(8,128)(2,1)S(1)} %collective-permute-done.20.refs_1_), channel_id=1, source_target_pairs={{0,1},{1,0},{2,3},{3,2},{4,5},{5,4},{6,7},{7,6},{8,9},{9,8},{10,11... | collective-permute-start | bytes 786440 | tf_op jit(solution)/shard_map/ppermute | solution.py:327
  (7 other events, 60.6 us)
